TPU v7x, 32 devices: a whole 2x2x4 slice. The times are simulated.
32 devices in a mesh: dp: 8 (over z, y), seq: 2 (over x), shard: 2 (over core).
Axes of the slice: x: 2, y: 2, z: 4, core: 2. Of those that a mesh axis runs over, the one named last changes fastest.
Arguments:
- inputs: float32 [16, 256, 512], P(('dp', 'shard'), 'seq'), may hold values from -5 to 5
- cotangent: float32 [16, 256, 512], P(('dp', 'shard'), 'seq'), may hold values from -6 to 6
- w_up: float32 [512, 4096], P(('dp', 'seq', 'shard')), may hold values from -0.25 to 0.25
- w_down: float32 [512, 4096], P(('dp', 'seq', 'shard')), may hold values from -0.25 to 0.25
- w_qkv: float32 [512, 1536], P(('dp', 'seq', 'shard')), may hold values from -0.25 to 0.25
- w_out: float32 [512, 512], P(('dp', 'seq', 'shard')), may hold values from -1.5 to 1.5
- w_glu: float32 [512, 1024], P(('dp', 'seq', 'shard')), may hold values from -0.25 to 0.25
- w_point: float32 [512, 512], P(('dp', 'seq', 'shard')), may hold values from -0.375 to 0.375
- vectors: float32 [512, 7], P(('dp', 'seq', 'shard')), may hold values from -2.5 to 2.5, as said below
- depth_kernel: float32 [512, 31], P(('dp', 'seq', 'shard')), may hold values from -1 to 1
- rel_bias: float32 [128, 8], P(('dp', 'seq', 'shard')), may hold values from -2.5 to 2.5
- bucket_table: int32 [511], replicated, may hold values from 0 to 127
- m_up: float32 [512, 4096], P(('dp', 'seq', 'shard')), may hold values from -128 to 128
- m_down: float32 [512, 4096], P(('dp', 'seq', 'shard')), may hold values from -128 to 128
- m_qkv: float32 [512, 1536], P(('dp', 'seq', 'shard')), may hold values from -128 to 128
- m_out: float32 [512, 512], P(('dp', 'seq', 'shard')), may hold values from -2000 to 2000
- m_glu: float32 [512, 1024], P(('dp', 'seq', 'shard')), may hold values from -128 to 128
- m_point: float32 [512, 512], P(('dp', 'seq', 'shard')), may hold values from -2000 to 2000
- m_vectors: float32 [512, 7], P(('dp', 'seq', 'shard')), may hold values from -400 to 400
- m_depth: float32 [512, 31], P(('dp', 'seq', 'shard')), may hold values from -400 to 400
- m_rel: float32 [128, 8], P(('dp', 'seq', 'shard')), may hold values from -400 to 400
Outputs:
- outputs: float32 [16, 256, 512], P(('dp', 'shard'), 'seq')
- input_grad: float32 [16, 256, 512], P(('dp', 'shard'), 'seq')
- grad_up: float32 [512, 4096], P(('dp', 'seq', 'shard'))
- grad_down: float32 [512, 4096], P(('dp', 'seq', 'shard'))
- grad_qkv: float32 [512, 1536], P(('dp', 'seq', 'shard'))
- grad_out: float32 [512, 512], P(('dp', 'seq', 'shard'))
- grad_glu: float32 [512, 1024], P(('dp', 'seq', 'shard'))
- grad_point: float32 [512, 512], P(('dp', 'seq', 'shard'))
- grad_vectors: float32 [512, 7], P(('dp', 'seq', 'shard'))
- grad_depth: float32 [512, 31], P(('dp', 'seq', 'shard'))
- grad_rel: float32 [128, 8], P(('dp', 'seq', 'shard'))
- new_up: float32 [512, 4096], P(('dp', 'seq', 'shard'))
- new_down: float32 [512, 4096], P(('dp', 'seq', 'shard'))
- new_qkv: float32 [512, 1536], P(('dp', 'seq', 'shard'))
- new_out: float32 [512, 512], P(('dp', 'seq', 'shard'))
- new_glu: float32 [512, 1024], P(('dp', 'seq', 'shard'))
- new_point: float32 [512, 512], P(('dp', 'seq', 'shard'))
- new_vectors: float32 [512, 7], P(('dp', 'seq', 'shard'))
- new_depth: float32 [512, 31], P(('dp', 'seq', 'shard'))
- new_rel: float32 [128, 8], P(('dp', 'seq', 'shard'))
- next_m_up: float32 [512, 4096], P(('dp', 'seq', 'shard'))
- next_m_down: float32 [512, 4096], P(('dp', 'seq', 'shard'))
- next_m_qkv: float32 [512, 1536], P(('dp', 'seq', 'shard'))
- next_m_out: float32 [512, 512], P(('dp', 'seq', 'shard'))
- next_m_glu: float32 [512, 1024], P(('dp', 'seq', 'shard'))
- next_m_point: float32 [512, 512], P(('dp', 'seq', 'shard'))
- next_m_vectors: float32 [512, 7], P(('dp', 'seq', 'shard'))
- next_m_depth: float32 [512, 31], P(('dp', 'seq', 'shard'))
- next_m_rel: float32 [128, 8], P(('dp', 'seq', 'shard'))
Inputs may be any that keep to these rules, and one draw needn't show every extreme that they name: `bucket_table`: entry r is the bucket of the relative offset r - 255. `vectors`: LayerNorm and BatchNorm gains near one in columns 0 to 5, the BatchNorm bias in column 6.
All inputs are finite; a program needn't handle non-finite values.
Results may differ from a plain program's by a relative error of at most 0.019.
Values may be sent and summed in bfloat16 or wider, within the bound.
A program may use at most 192 MiB of HBM per device.

v0:
```python
import jax
import jax.numpy as jnp
from jax import lax
from jax.sharding import PartitionSpec as P

D = 512
FF = 2048
H = 8
DH = 64
K = 31
NB = 128


EPS_NORM = 1e-05
EPS_BATCH = 1e-05
EPS_SCALE = 1e-06
MOMENTUM = 0.9
RATE_MATRIX = 1.0
RATE_VECTOR = 0.25
COEF_A = 3.4445
COEF_B = -4.775
COEF_C = 2.0315
HIGHEST = lax.Precision.HIGHEST


def with_halo(value, sides, width):
    for axis, dim in sides:
        devices, length = (lax.axis_size(axis), value.shape[dim])
        up = [(i, (i + 1) % devices) for i in range(devices - 1)]
        down = [(j, i) for i, j in up]
        last = lax.slice_in_dim(value, length - width, length, axis=dim)
        first = lax.slice_in_dim(value, 0, width, axis=dim)
        before = lax.ppermute(last, axis, up)
        after = lax.ppermute(first, axis, down)
        value = jnp.concatenate([before, value, after], axis=dim)
    return value


def matmul(left, right):
    return jnp.dot(left, right, preferred_element_type=jnp.float32)


def matmul_right_t(left, right):
    return lax.dot_general(
        left, right, (((1,), (1,)), ((), ())), preferred_element_type=jnp.float32
    )


def matmul_left_t(left, right):
    return lax.dot_general(
        left, right, (((0,), (0,)), ((), ())), preferred_element_type=jnp.float32
    )


def layer_norm(field, gain):
    centre = jnp.mean(field, axis=-1, keepdims=True)
    shifted = field - centre
    inverse = lax.rsqrt(jnp.mean(shifted * shifted, axis=-1, keepdims=True) + EPS_NORM)
    normed = shifted * inverse
    return (normed * gain, normed, inverse)


def norm_back(grad_out, normed, inverse, gain):
    scaled = grad_out * gain
    grad_in = inverse * (
        scaled
        - jnp.mean(scaled, axis=-1, keepdims=True)
        - normed * jnp.mean(scaled * normed, axis=-1, keepdims=True)
    )
    return (grad_in, jnp.sum(grad_out * normed, axis=0))


def silu_slope(values):
    sigma = jax.nn.sigmoid(values)
    return sigma * (1.0 + values * (1.0 - sigma))


def ffn_forward(field, gain, w_in, w_back):
    normed_out, normed, inverse = layer_norm(field, gain)
    lifted = normed_out.astype(jnp.bfloat16)
    hidden_pre = matmul(lifted, w_in)
    hidden_act = jax.nn.silu(hidden_pre).astype(jnp.bfloat16)
    return (
        field + 0.5 * matmul_right_t(hidden_act, w_back),
        (lifted, hidden_pre, hidden_act, normed, inverse),
    )


def ffn_backward(grad, saved, gain, w_in, w_back):
    lifted, hidden_pre, hidden_act, normed, inverse = saved
    grad_branch = (0.5 * grad).astype(jnp.bfloat16)
    grad_back = matmul_left_t(grad_branch, hidden_act)
    grad_act = matmul(grad_branch, w_back)
    grad_pre = (grad_act * silu_slope(hidden_pre)).astype(jnp.bfloat16)
    grad_in = matmul_left_t(lifted, grad_pre)
    grad_field, grad_gain = norm_back(matmul_right_t(grad_pre, w_in), normed, inverse, gain)
    return (grad + grad_field, grad_in, grad_back, grad_gain)


def depthwise(wide, kernel, count):
    total = wide[0:count] * kernel[:, 0]
    for tap_idx in range(1, K):
        total = total + wide[tap_idx : tap_idx + count] * kernel[:, tap_idx]
    return total


def spread_rows(window, count, keys_len):
    padded = jnp.concatenate([window, jnp.zeros((1,), window.dtype)])
    tiled = jnp.broadcast_to(padded[None, :], (count, keys_len + count)).reshape(-1)
    shaped = tiled[: count * (keys_len + count - 1)].reshape(count, keys_len + count - 1)
    return shaped[:, count - 1 : count - 1 + keys_len]


def collect_rows(grid, count, keys_len):
    placed = jnp.concatenate([jnp.zeros((count, count - 1), grid.dtype), grid], axis=1).reshape(-1)
    placed = jnp.concatenate([placed, jnp.zeros((count,), grid.dtype)])
    return jnp.sum(placed.reshape(count, keys_len + count), axis=0)[: keys_len + count - 1]


def attention_scores(query, keys, offsets, first_row, row_start, block, head_idx):
    length = keys.shape[0]
    columns = slice(head_idx * DH, (head_idx + 1) * DH)
    anchor = length - block - first_row - row_start
    window = lax.dynamic_slice_in_dim(offsets[head_idx], anchor, length + block - 1)
    product = matmul_right_t(query[row_start : row_start + block, columns], keys[:, columns])
    return product * DH ** (-0.5) + spread_rows(window, block, length)


def attention_forward(query, keys, values, offsets, first_row):
    total_rows = query.shape[0]
    block = min(512, total_rows)
    head_outs = []
    head_lse = []
    for head_idx in range(H):
        scores = attention_scores(query, keys, offsets, first_row, 0, block, head_idx)
        row_max = jnp.max(scores, axis=1, keepdims=True)
        shifted_exp = jnp.exp(scores - row_max)
        row_total = jnp.sum(shifted_exp, axis=1, keepdims=True)
        prob_low = (shifted_exp / row_total).astype(jnp.bfloat16)
        head_outs.append(matmul(prob_low, values[:, head_idx * DH : (head_idx + 1) * DH]))
        head_lse.append((row_max + jnp.log(row_total))[:, 0])
    out_blocks = jnp.concatenate(head_outs, axis=1)
    lse_blocks = jnp.stack(head_lse, axis=0)
    return (out_blocks, lse_blocks)


def attention_backward(query, keys, values, offsets, first_row, log_total, grad_attended, delta):
    total_rows = query.shape[0]
    length = keys.shape[0]
    block = min(512, total_rows)
    scale = DH ** (-0.5)
    key_parts = [jnp.zeros((length, DH), jnp.float32) for head_idx in range(H)]
    value_parts = [jnp.zeros((length, DH), jnp.float32) for head_idx in range(H)]
    offset_rows = [jnp.zeros((2 * length - 1,), jnp.float32) for head_idx in range(H)]
    head_grads = []
    for head_idx in range(H):
        columns = slice(head_idx * DH, (head_idx + 1) * DH)
        scores = attention_scores(query, keys, offsets, first_row, 0, block, head_idx)
        prob = jnp.exp(scores - log_total[head_idx, 0:block][:, None])
        prob_low = prob.astype(jnp.bfloat16)
        grad_piece = grad_attended[0:block, columns]
        value_parts[head_idx] = matmul_left_t(prob_low, grad_piece)
        grad_prob = matmul_right_t(grad_piece, values[:, columns])
        grad_score = prob * (grad_prob - delta[0:block, head_idx][:, None])
        score_low = grad_score.astype(jnp.bfloat16)
        head_grads.append(matmul(score_low, keys[:, columns]) * scale)
        key_parts[head_idx] = matmul_left_t(score_low, query[0:block, columns]) * scale
        anchor = length - block - first_row - 0
        offset_rows[head_idx] = lax.dynamic_update_slice_in_dim(
            offset_rows[head_idx], collect_rows(grad_score, block, length), anchor, 0
        )
    query_blocks = jnp.concatenate(head_grads, axis=1)
    return (
        query_blocks,
        jnp.concatenate(key_parts, axis=1),
        jnp.concatenate(value_parts, axis=1),
        jnp.stack(offset_rows, axis=0),
    )


def orthogonalize_columns(matrix, start, part_width):
    iterate = matrix / (jnp.sqrt(jnp.sum(matrix * matrix)) + 1e-07)
    for iter_step in range(4):
        gram = jnp.dot(iterate, iterate.T, precision=HIGHEST)
        mixed = COEF_B * gram + COEF_C * jnp.dot(gram, gram, precision=HIGHEST)
        iterate = COEF_A * iterate + jnp.dot(mixed, iterate, precision=HIGHEST)
    gram = jnp.dot(iterate, iterate.T, precision=HIGHEST)
    mixed = COEF_B * gram + COEF_C * jnp.dot(gram, gram, precision=HIGHEST)
    columns = lax.dynamic_slice_in_dim(iterate, start, part_width, 1)
    return COEF_A * columns + jnp.dot(mixed, columns, precision=HIGHEST)


def pad_columns(matrix, width):
    return jnp.pad(matrix, ((0, 0), (0, width - matrix.shape[1])))


def local(
    inputs,
    cotangent,
    w_up,
    w_down,
    w_qkv,
    w_out,
    w_glu,
    w_point,
    vectors,
    depth_kernel,
    rel_bias,
    bucket_table,
    m_up,
    m_down,
    m_qkv,
    m_out,
    m_glu,
    m_point,
    m_vectors,
    m_depth,
    m_rel,
):
    bf16 = jnp.bfloat16
    gathered = (
        lax.all_gather(w_up.astype(bf16), ("dp", "seq", "shard"), axis=0, tiled=True),
        lax.all_gather(w_down.astype(bf16), ("dp", "seq", "shard"), axis=0, tiled=True),
        lax.all_gather(w_qkv.astype(bf16), ("dp", "seq", "shard"), axis=0, tiled=True),
        lax.all_gather(w_out.astype(bf16), ("dp", "seq", "shard"), axis=0, tiled=True),
        lax.all_gather(w_glu.astype(bf16), ("dp", "seq", "shard"), axis=0, tiled=True),
        lax.all_gather(w_point.astype(bf16), ("dp", "seq", "shard"), axis=0, tiled=True),
        lax.all_gather(vectors.astype(bf16), ("dp", "seq", "shard"), axis=0, tiled=True),
        lax.all_gather(depth_kernel.astype(bf16), ("dp", "seq", "shard"), axis=0, tiled=True),
        lax.all_gather(rel_bias.astype(bf16), ("dp", "seq", "shard"), axis=0, tiled=True),
    )
    up_all, down_all, qkv_w, out_w, glu_w, point_w, vec_low, kern_low, rel_low = gathered
    gains = vec_low.astype(jnp.float32)
    kernel = kern_low.astype(jnp.float32)
    bucket_hit = (bucket_table[:, None] == jnp.arange(NB, dtype=jnp.int32)[None, :]).astype(
        jnp.float32
    )
    offsets = jnp.dot(bucket_hit, rel_low.astype(jnp.float32), precision=HIGHEST).T
    seq_rows = inputs[0]
    row_count = seq_rows.shape[0]
    first_row = lax.axis_index("seq") * row_count
    token_total = row_count * lax.axis_size(("dp", "seq", "shard"))
    section_one, ffn_saved = ffn_forward(seq_rows, gains[:, 0], up_all[:, :FF], down_all[:, :FF])
    normed_out2, normed2, inverse2 = layer_norm(section_one, gains[:, 1])
    lifted2 = normed_out2.astype(bf16)
    projected = matmul(lifted2, qkv_w).astype(bf16)
    query = projected[:, :D]
    keys, values = (
        lax.all_gather(projected[:, D : 2 * D], "seq", axis=0, tiled=True),
        lax.all_gather(projected[:, 2 * D :], "seq", axis=0, tiled=True),
    )
    attended, log_total = attention_forward(query, keys, values, offsets, first_row)
    attended_low = attended.astype(bf16)
    section_two = section_one + matmul(attended_low, out_w)
    normed_out3, normed3, inverse3 = layer_norm(section_two, gains[:, 2])
    lifted3 = normed_out3.astype(bf16)
    gates = matmul(lifted3, glu_w)
    first_half = gates[:, :D]
    sig_gate = jax.nn.sigmoid(gates[:, D:])
    glu = first_half * sig_gate
    glu_wide = with_halo(glu, (("seq", 0),), K // 2)
    conv = depthwise(glu_wide, kernel, row_count)
    mean = lax.psum(jnp.sum(conv, axis=0), ("dp", "seq", "shard")) / token_total
    centred = conv - mean
    variance = lax.psum(jnp.sum(centred * centred, axis=0), ("dp", "seq", "shard")) / token_total
    inv_std = lax.rsqrt(variance + EPS_BATCH)
    normed_bn = centred * inv_std
    batch_out = normed_bn * gains[:, 5] + gains[:, 6]
    swish_low = jax.nn.silu(batch_out).astype(bf16)
    section_three = section_two + matmul(swish_low, point_w)
    section_four, tail_saved = ffn_forward(
        section_three, gains[:, 3], up_all[:, FF:], down_all[:, FF:]
    )
    outputs, normed5, inverse5 = layer_norm(section_four, gains[:, 4])
    again = (
        lax.all_gather(w_up.astype(bf16), ("dp", "seq", "shard"), axis=0, tiled=True),
        lax.all_gather(w_down.astype(bf16), ("dp", "seq", "shard"), axis=0, tiled=True),
        lax.all_gather(w_qkv.astype(bf16), ("dp", "seq", "shard"), axis=0, tiled=True),
        lax.all_gather(w_out.astype(bf16), ("dp", "seq", "shard"), axis=0, tiled=True),
        lax.all_gather(w_glu.astype(bf16), ("dp", "seq", "shard"), axis=0, tiled=True),
        lax.all_gather(w_point.astype(bf16), ("dp", "seq", "shard"), axis=0, tiled=True),
        lax.all_gather(vectors.astype(bf16), ("dp", "seq", "shard"), axis=0, tiled=True),
        lax.all_gather(depth_kernel.astype(bf16), ("dp", "seq", "shard"), axis=0, tiled=True),
    )
    up_back, down_back, qkv_back, out_back, glu_back, point_back, vec_back, kern_back = again
    gains_back = vec_back.astype(jnp.float32)
    kernel_back = kern_back.astype(jnp.float32)
    grad_four, gain_four = norm_back(cotangent[0], normed5, inverse5, gains_back[:, 4])
    grad_three, grad_up_two, grad_down_two, gain_three = ffn_backward(
        grad_four, tail_saved, gains_back[:, 3], up_back[:, FF:], down_back[:, FF:]
    )
    grad_three_low = grad_three.astype(bf16)
    grad_point = matmul_left_t(swish_low, grad_three_low)
    grad_batch = matmul_right_t(grad_three_low, point_back) * silu_slope(batch_out)
    grad_normed = grad_batch * gains_back[:, 5]
    sum_normed, sum_cross = lax.psum(
        (jnp.sum(grad_normed, axis=0), jnp.sum(grad_normed * normed_bn, axis=0)),
        ("dp", "seq", "shard"),
    )
    grad_conv = inv_std * (
        grad_normed - sum_normed / token_total - normed_bn * sum_cross / token_total
    )
    grad_wide = with_halo(grad_conv, (("seq", 0),), K // 2)
    grad_glu = grad_wide[K - 1 : K - 1 + row_count] * kernel_back[:, 0]
    for tap_idx in range(1, K):
        grad_glu = (
            grad_glu
            + grad_wide[K - 1 - tap_idx : K - 1 - tap_idx + row_count] * kernel_back[:, tap_idx]
        )
    grad_kernel = jnp.stack(
        [
            jnp.sum(grad_conv * glu_wide[tap_idx : tap_idx + row_count], axis=0)
            for tap_idx in range(K)
        ],
        axis=1,
    )
    grad_gates = jnp.concatenate(
        [grad_glu * sig_gate, grad_glu * first_half * sig_gate * (1.0 - sig_gate)], axis=1
    ).astype(bf16)
    grad_glu_w = matmul_left_t(lifted3, grad_gates)
    grad_two_part, gain_two = norm_back(
        matmul_right_t(grad_gates, glu_back), normed3, inverse3, gains_back[:, 2]
    )
    grad_two = grad_three + grad_two_part
    grad_two_low = grad_two.astype(bf16)
    grad_out_w = matmul_left_t(attended_low, grad_two_low)
    grad_attended = matmul_right_t(grad_two_low, out_back).astype(bf16)
    delta = jnp.sum(
        (grad_attended.astype(jnp.float32) * attended).reshape(row_count, H, DH), axis=2
    )
    query_grad, key_grad, value_grad, offset_grad = attention_backward(
        query, keys, values, offsets, first_row, log_total, grad_attended, delta
    )
    key_own, value_own = (
        lax.psum_scatter(key_grad, "seq", scatter_dimension=0, tiled=True),
        lax.psum_scatter(value_grad, "seq", scatter_dimension=0, tiled=True),
    )
    grad_proj = jnp.concatenate([query_grad, key_own, value_own], axis=1).astype(bf16)
    grad_qkv_w = matmul_left_t(lifted2, grad_proj)
    grad_one_part, gain_one = norm_back(
        matmul_right_t(grad_proj, qkv_back), normed2, inverse2, gains_back[:, 1]
    )
    grad_one = grad_two + grad_one_part
    input_grad, grad_up_one, grad_down_one, gain_zero = ffn_backward(
        grad_one, ffn_saved, gains_back[:, 0], up_back[:, :FF], down_back[:, :FF]
    )
    grad_up_local = jnp.concatenate([grad_up_one, grad_up_two], axis=1)
    grad_down_local = jnp.concatenate([grad_down_one, grad_down_two], axis=1)
    grad_vec_local = jnp.stack(
        [
            gain_zero,
            gain_one,
            gain_two,
            gain_three,
            gain_four,
            jnp.sum(grad_batch * normed_bn, axis=0),
            jnp.sum(grad_batch, axis=0),
        ],
        axis=1,
    )
    grad_rel_local = jnp.dot(bucket_hit.T, offset_grad.T, precision=HIGHEST)
    shares = (
        lax.psum_scatter(grad_up_local, ("dp", "seq", "shard"), scatter_dimension=0, tiled=True),
        lax.psum_scatter(grad_down_local, ("dp", "seq", "shard"), scatter_dimension=0, tiled=True),
        lax.psum_scatter(grad_qkv_w, ("dp", "seq", "shard"), scatter_dimension=0, tiled=True),
        lax.psum_scatter(grad_out_w, ("dp", "seq", "shard"), scatter_dimension=0, tiled=True),
        lax.psum_scatter(grad_glu_w, ("dp", "seq", "shard"), scatter_dimension=0, tiled=True),
        lax.psum_scatter(grad_point, ("dp", "seq", "shard"), scatter_dimension=0, tiled=True),
        lax.psum_scatter(grad_vec_local, ("dp", "seq", "shard"), scatter_dimension=0, tiled=True),
        lax.psum_scatter(grad_kernel, ("dp", "seq", "shard"), scatter_dimension=0, tiled=True),
        lax.psum_scatter(grad_rel_local, ("dp", "seq", "shard"), scatter_dimension=0, tiled=True),
    )
    (
        grad_up,
        grad_down,
        grad_qkv,
        grad_out,
        grad_glu,
        grad_pnt,
        grad_vectors,
        grad_depth,
        grad_rel,
    ) = shares
    next_m_up = MOMENTUM * m_up + grad_up
    next_m_down = MOMENTUM * m_down + grad_down
    next_m_qkv = MOMENTUM * m_qkv + grad_qkv
    next_m_out = MOMENTUM * m_out + grad_out
    next_m_glu = MOMENTUM * m_glu + grad_glu
    next_m_point = MOMENTUM * m_point + grad_pnt
    width = max(FF, 3 * D)
    stacked = jnp.stack(
        [
            pad_columns(next_m_up[:, :FF], width),
            pad_columns(next_m_up[:, FF:], width),
            pad_columns(next_m_down[:, :FF], width),
            pad_columns(next_m_down[:, FF:], width),
            pad_columns(next_m_qkv, width),
            pad_columns(next_m_out, width),
            pad_columns(next_m_glu, width),
            pad_columns(next_m_point, width),
        ],
        axis=0,
    )
    copies = lax.axis_size(("dp", "seq", "shard")) // 8
    part_width = width // copies
    outgoing = jnp.repeat(stacked, copies, axis=0)
    owned = lax.all_to_all(
        outgoing, ("dp", "seq", "shard"), split_axis=0, concat_axis=1, tiled=True
    )
    column_start = lax.axis_index(("dp", "seq", "shard")) % copies * part_width
    ortho_part = orthogonalize_columns(owned[0], column_start, part_width)
    returned = lax.all_to_all(
        ortho_part[None], ("dp", "seq", "shard"), split_axis=1, concat_axis=0, tiled=True
    )
    own_rows = returned.shape[1]
    mine = (
        returned.reshape(8, copies, own_rows, part_width)
        .transpose(0, 2, 1, 3)
        .reshape(8, own_rows, width)
    )
    new_up = w_up - RATE_MATRIX * jnp.concatenate([mine[0, :, :FF], mine[1, :, :FF]], axis=1)
    new_down = w_down - RATE_MATRIX * jnp.concatenate([mine[2, :, :FF], mine[3, :, :FF]], axis=1)
    new_qkv = w_qkv - RATE_MATRIX * mine[4, :, : 3 * D]
    new_out = w_out - RATE_MATRIX * mine[5, :, :D]
    new_glu = w_glu - RATE_MATRIX * mine[6, :, : 2 * D]
    new_point = w_point - RATE_MATRIX * mine[7, :, :D]
    next_m_vectors = MOMENTUM * m_vectors + grad_vectors
    next_m_depth = MOMENTUM * m_depth + grad_depth
    next_m_rel = MOMENTUM * m_rel + grad_rel
    square_vec, square_depth, square_rel = lax.psum(
        (
            jnp.sum(next_m_vectors * next_m_vectors, axis=0),
            jnp.sum(next_m_depth * next_m_depth, axis=0),
            jnp.sum(next_m_rel * next_m_rel, axis=0),
        ),
        ("dp", "seq", "shard"),
    )
    new_vectors = vectors - RATE_VECTOR * next_m_vectors * lax.rsqrt(square_vec / D + EPS_SCALE)
    new_depth = depth_kernel - RATE_VECTOR * next_m_depth * lax.rsqrt(square_depth / D + EPS_SCALE)
    new_rel = rel_bias - RATE_VECTOR * next_m_rel * lax.rsqrt(square_rel / NB + EPS_SCALE)
    return (
        outputs[None],
        input_grad[None],
        grad_up,
        grad_down,
        grad_qkv,
        grad_out,
        grad_glu,
        grad_pnt,
        grad_vectors,
        grad_depth,
        grad_rel,
        new_up,
        new_down,
        new_qkv,
        new_out,
        new_glu,
        new_point,
        new_vectors,
        new_depth,
        new_rel,
        next_m_up,
        next_m_down,
        next_m_qkv,
        next_m_out,
        next_m_glu,
        next_m_point,
        next_m_vectors,
        next_m_depth,
        next_m_rel,
    )


def solution(mesh):
    placed = (
        P(("dp", "shard"), "seq", None),
        P(("dp", "shard"), "seq", None),
        P(("dp", "seq", "shard"), None),
        P(("dp", "seq", "shard"), None),
        P(("dp", "seq", "shard"), None),
        P(("dp", "seq", "shard"), None),
        P(("dp", "seq", "shard"), None),
        P(("dp", "seq", "shard"), None),
        P(("dp", "seq", "shard"), None),
        P(("dp", "seq", "shard"), None),
        P(("dp", "seq", "shard"), None),
        P(),
        P(("dp", "seq", "shard"), None),
        P(("dp", "seq", "shard"), None),
        P(("dp", "seq", "shard"), None),
        P(("dp", "seq", "shard"), None),
        P(("dp", "seq", "shard"), None),
        P(("dp", "seq", "shard"), None),
        P(("dp", "seq", "shard"), None),
        P(("dp", "seq", "shard"), None),
        P(("dp", "seq", "shard"), None),
    )
    return jax.shard_map(
        local,
        mesh=mesh,
        in_specs=placed,
        out_specs=(
            P(("dp", "shard"), "seq", None),
            P(("dp", "shard"), "seq", None),
            P(("dp", "seq", "shard"), None),
            P(("dp", "seq", "shard"), None),
            P(("dp", "seq", "shard"), None),
            P(("dp", "seq", "shard"), None),
            P(("dp", "seq", "shard"), None),
            P(("dp", "seq", "shard"), None),
            P(("dp", "seq", "shard"), None),
            P(("dp", "seq", "shard"), None),
            P(("dp", "seq", "shard"), None),
            P(("dp", "seq", "shard"), None),
            P(("dp", "seq", "shard"), None),
            P(("dp", "seq", "shard"), None),
            P(("dp", "seq", "shard"), None),
            P(("dp", "seq", "shard"), None),
            P(("dp", "seq", "shard"), None),
            P(("dp", "seq", "shard"), None),
            P(("dp", "seq", "shard"), None),
            P(("dp", "seq", "shard"), None),
            P(("dp", "seq", "shard"), None),
            P(("dp", "seq", "shard"), None),
            P(("dp", "seq", "shard"), None),
            P(("dp", "seq", "shard"), None),
            P(("dp", "seq", "shard"), None),
            P(("dp", "seq", "shard"), None),
            P(("dp", "seq", "shard"), None),
            P(("dp", "seq", "shard"), None),
            P(("dp", "seq", "shard"), None),
        ),
        check_vma=False,
    )
```

profile of v0, /device:TPU:31, one launch (start us, length us, event | category | flops | bytes accessed | tf_op | source)
XLA Modules:
  0.0 1618.9 jit_solution(16593069092009664031)
XLA Ops:
  14.5 36.6 %all_gather.50 = bf16[512,31]{1,0:T(8,128)(2,1)S(1)} all-gather(bf16[16,31]{1,0:T(8,128)(2,1)S(1)} %convert_element_type.199), channel_id=1, replica_groups=mesh['dp'=8,'seq'=2,'shard'=2] {'dp','seq','shard'}, dimensions={0}, use_global_device_ids=true | all-gather | bytes 32736 | tf_op jit(solution)/shard_map/all_gather | solution.py:229
  57.1 39.1 %all-gather.1 = bf16[32,4,8]{2,1,0:T(4,128)(2,1)S(1)} all-gather(bf16[1,4,8]{2,1,0:T(4,128)(2,1)S(1)} %convert_bitcast_fusion.1), channel_id=1, replica_groups=mesh['dp'=8,'seq'=2,'shard'=2] {'dp','seq','shard'}, dimensions={0}, use_global_device_ids=true | all-gather | bytes 2112 | tf_op jit(solution)/shard_map/all_gather | solution.py:230
  97.2 37.5 %all-gather = bf16[32,16,7]{1,2,0:T(8,128)(2,1)S(1)} all-gather(bf16[1,16,7]{1,2,0:T(8,128)(2,1)S(1)} %convert_bitcast_fusion), channel_id=1, replica_groups=mesh['dp'=8,'seq'=2,'shard'=2] {'dp','seq','shard'}, dimensions={0}, use_global_device_ids=true | all-gather | bytes 7392 | tf_op jit(solution)/shard_map/all_gather | solution.py:228
  143.0 42.3 %all_gather.51 = bf16[512,512]{1,0:T(8,128)(2,1)} all-gather(bf16[16,512]{1,0:T(8,128)(2,1)S(1)} %convert_element_type.202), channel_id=1, replica_groups=mesh['dp'=8,'seq'=2,'shard'=2] {'dp','seq','shard'}, dimensions={0}, use_global_device_ids=true | all-gather | bytes 540672 | tf_op jit(solution)/shard_map/all_gather | solution.py:227
  185.3 38.1 %all_gather.48 = bf16[512,512]{1,0:T(8,128)(2,1)S(1)} all-gather(bf16[16,512]{1,0:T(8,128)(2,1)S(1)} %convert_element_type.196), channel_id=1, replica_groups=mesh['dp'=8,'seq'=2,'shard'=2] {'dp','seq','shard'}, dimensions={0}, use_global_device_ids=true | all-gather | bytes 540672 | tf_op jit(solution)/shard_map/all_gather | solution.py:225
  236.1 8.1 all_gather.45
  274.4 40.7 %psum.49 = f32[512]{0:T(512)S(1)} all-reduce(f32[512]{0:T(512)S(1)} %get-tuple-element.241), channel_id=1, replica_groups=mesh['dp'=8,'seq'=2,'shard'=2] {'dp','seq','shard'}, use_global_device_ids=true, to_apply=%region_23.24 | all-reduce | flops 512 | bytes 4096 | tf_op jit(solution)/shard_map/psum | solution.py:263
  315.1 40.7 %psum.50 = f32[512]{0:T(512)S(1)} all-reduce(f32[512]{0:T(512)S(1)} %multiply_reduce_fusion.45), channel_id=1, replica_groups=mesh['dp'=8,'seq'=2,'shard'=2] {'dp','seq','shard'}, use_global_device_ids=true, to_apply=%region_25.26 | all-reduce | flops 512 | bytes 4096 | tf_op jit(solution)/shard_map/psum | solution.py:265
  368.3 39.2 %all-reduce.22 = (f32[512]{0:T(512)S(1)}, f32[512]{0:T(512)S(1)}) all-reduce(f32[512]{0:T(512)S(1)} %get-tuple-element.176, f32[512]{0:T(512)S(1)} %get-tuple-element.193), channel_id=1, replica_groups=mesh['dp'=8,'seq'=2,'shard'=2] {'dp','seq','shard'}, use_global_device_ids=true, to_apply=%region_37.38 | all-reduce | flops 1024 | bytes 8192 | tf_op jit(solution)/shard_map/psum | solution.py:296
  460.7 10.6 reduce-scatter.17.cloned.1.call-done
  492.4 113.0 %reduce-scatter.29.cloned.1.call-done = f32[16,512]{1,0:T(8,128)} async-done(((f32[512,512]{1,0:T(8,128)}), f32[16,512]{1,0:T(8,128)}) %reduce-scatter.29.cloned.1.call-update) | async-done | bytes 32784 | tf_op jit(solution)/shard_map/reduce_scatter | solution.py:368
  606.2 132.9 %reduce-scatter.25.cloned.1.call-done = f32[16,512]{1,0:T(8,128)} async-done(((f32[512,512]{1,0:T(8,128)}), f32[16,512]{1,0:T(8,128)}) %reduce-scatter.25.cloned.1.call-update) | async-done | bytes 32784 | tf_op jit(solution)/shard_map/reduce_scatter | solution.py:366
  739.8 134.7 %reduce-scatter.27.cloned.1.call-done = f32[16,1024]{1,0:T(8,128)} async-done(((f32[512,1024]{1,0:T(8,128)}), f32[16,1024]{1,0:T(8,128)}) %reduce-scatter.27.cloned.1.call-update) | async-done | bytes 65552 | tf_op jit(solution)/shard_map/reduce_scatter | solution.py:367
  875.4 104.9 %reduce-scatter.23.cloned.1.call-done = f32[16,1536]{1,0:T(8,128)} async-done(((f32[512,1536]{1,0:T(8,128)}), f32[16,1536]{1,0:T(8,128)}) %reduce-scatter.23.cloned.1.call-update) | async-done | bytes 98320 | tf_op jit(solution)/shard_map/reduce_scatter | solution.py:365
  981.2 148.4 %reduce-scatter.19.cloned.1.call-done = f32[16,4096]{1,0:T(8,128)} async-done(((f32[512,4096]{1,0:T(8,128)}), f32[16,4096]{1,0:T(8,128)}) %reduce-scatter.19.cloned.1.call-update) | async-done | bytes 262160 | tf_op jit(solution)/shard_map/reduce_scatter | solution.py:363
  1130.6 146.5 %reduce-scatter.21.cloned.1.call-done = f32[16,4096]{1,0:T(8,128)} async-done(((f32[512,4096]{1,0:T(8,128)}), f32[16,4096]{1,0:T(8,128)}) %reduce-scatter.21.cloned.1.call-update) | async-done | bytes 262160 | tf_op jit(solution)/shard_map/reduce_scatter | solution.py:364
  1281.0 8.7 all-to-all-start
  1298.9 103.6 %all-reduce.20 = f32[128,8]{1,0:T(8,128)S(1)} all-reduce(f32[128,8]{1,0:T(8,128)S(1)} %fusion.200), channel_id=12, replica_groups=mesh['dp'=8,'seq'=2,'shard'=2] {'dp','seq','shard'}, use_global_device_ids=true, to_apply=%region_101.102.clone | all-reduce | flops 1024 | bytes 8192
  1403.1 24.8 %reduce-scatter.33.cloned.1.call-done = f32[16,31]{1,0:T(8,128)} async-done(((f32[512,31]{1,0:T(8,128)}), f32[16,31]{1,0:T(8,128)}) %reduce-scatter.33.cloned.1.call-update) | async-done | bytes 2000
  1471.9 7.3 fusion.391
  1497.1 7.2 multiply_add_fusion
  1517.3 7.7 all-to-all-start.1
  1525.9 39.6 %reduce-scatter.31.cloned.1.call-done = f32[16,7]{1,0:T(8,128)} async-done(((f32[512,7]{1,0:T(8,128)}), f32[16,7]{1,0:T(8,128)}) %reduce-scatter.31.cloned.1.call-update) | async-done | bytes 464
  1566.4 39.3 %all-reduce.21 = (f32[7]{0:T(128)S(1)}, f32[31]{0:T(128)S(1)}, f32[8]{0:T(128)S(1)}) all-reduce(f32[7]{0:T(128)S(1)} %get-tuple-element.236, f32[31]{0:T(128)S(1)} %get-tuple-element.234, f32[8]{0:T(128)S(1)} %get-tuple-element.231), channel_id=1, replica_groups=mesh['dp'=8,'seq'=2,'shard'=2] {'dp','seq','shard'}, use_global_device_ids=true, to_apply=%region_104.105 | all-reduce | flops 46 | bytes 368 | tf_op jit(solution)/shard_map/psum | solution.py:430
  (720 shorter events, 249.1 us)
Async XLA Ops:
  7.2 216.2 %all-gather.7.cloned.1.call-start = ((), (), s32[]{:S(2)}) async-start(), calls=%async_computation.12 | async-start | bytes 4325376 | tf_op jit(solution)/shard_map/all_gather | solution.py:222
  8.9 216.6 %all-gather.9.cloned.1.call-start = ((), (), s32[]{:S(2)}) async-start(), calls=%async_computation.13 | async-start | bytes 4325376 | tf_op jit(solution)/shard_map/all_gather | solution.py:223
  10.6 218.0 %all-gather.11.cloned.1.call-start = ((), (), s32[]{:S(2)}) async-start(), calls=%async_computation.14 | async-start | bytes 1622016 | tf_op jit(solution)/shard_map/all_gather | solution.py:224
  12.2 253.2 %all-gather.13.cloned.1.call-start = ((), (), s32[]{:S(2)}) async-start(), calls=%async_computation.15 | async-start | bytes 1081344 | tf_op jit(solution)/shard_map/all_gather | solution.py:226
  13.7 445.4 %reduce-scatter.15.cloned.1.call-start = ((), (), s32[]{:S(2)}) async-start(), calls=%async_computation.16 | async-start | bytes 786432 | tf_op jit(solution)/shard_map/reduce_scatter | solution.py:335
  267.1 5.9 collective-permute-start
  268.4 5.0 collective-permute-start.1
  409.6 3.9 collective-permute-start.2
  412.0 4.7 collective-permute-start.3
  436.1 35.2 %reduce-scatter.17.cloned.1.call-start = ((), (), s32[]{:S(2)}) async-start(), calls=%async_computation.17 | async-start | bytes 786432 | tf_op jit(solution)/shard_map/reduce_scatter | solution.py:336
  444.9 160.5 %reduce-scatter.29.cloned.1.call-start = ((), (), s32[]{:S(2)}) async-start(), calls=%async_computation.23 | async-start | bytes 1081344 | tf_op jit(solution)/shard_map/reduce_scatter | solution.py:368
  447.0 292.0 %reduce-scatter.25.cloned.1.call-start = ((), (), s32[]{:S(2)}) async-start(), calls=%async_computation.21 | async-start | bytes 1081344 | tf_op jit(solution)/shard_map/reduce_scatter | solution.py:366
  449.4 425.1 %reduce-scatter.27.cloned.1.call-start = ((), (), s32[]{:S(2)}) async-start(), calls=%async_computation.22 | async-start | bytes 2162688 | tf_op jit(solution)/shard_map/reduce_scatter | solution.py:367
  452.4 527.9 %reduce-scatter.23.cloned.1.call-start = ((), (), s32[]{:S(2)}) async-start(), calls=%async_computation.20 | async-start | bytes 3244032 | tf_op jit(solution)/shard_map/reduce_scatter | solution.py:365
  476.3 653.2 %reduce-scatter.19.cloned.1.call-start = ((), (), s32[]{:S(2)}) async-start(), calls=%async_computation.18 | async-start | bytes 8650752 | tf_op jit(solution)/shard_map/reduce_scatter | solution.py:363
  485.8 791.3 %reduce-scatter.21.cloned.1.call-start = ((), (), s32[]{:S(2)}) async-start(), calls=%async_computation.19 | async-start | bytes 8650752 | tf_op jit(solution)/shard_map/reduce_scatter | solution.py:364
  492.4 637.2 %copy-start.69 = (f32[16,4096]{1,0:T(8,128)S(1)}, f32[16,4096]{1,0:T(8,128)}, u32[]{:S(2)}) copy-start(f32[16,4096]{1,0:T(8,128)} %param.33) | copy-start | bytes 786436
  492.4 784.7 %copy-start.70 = (f32[16,4096]{1,0:T(8,128)S(1)}, f32[16,4096]{1,0:T(8,128)}, u32[]{:S(2)}) copy-start(f32[16,4096]{1,0:T(8,128)} %param.34) | copy-start | bytes 786436
  606.2 674.6 %copy-start.73 = (f32[16,512]{1,0:T(8,128)}, f32[16,512]{1,0:T(8,128)S(1)}, u32[]{:S(2)}) copy-start(f32[16,512]{1,0:T(8,128)S(1)} %multiply_add_fusion.13) | copy-start | bytes 98308
  739.8 541.0 %copy-start.74 = (f32[16,512]{1,0:T(8,128)}, f32[16,512]{1,0:T(8,128)S(1)}, u32[]{:S(2)}) copy-start(f32[16,512]{1,0:T(8,128)S(1)} %multiply_add_fusion.14) | copy-start | bytes 98308
  1281.0 152.0 %all-to-all-start = ((f32[32,16,2048]{2,1,0:T(8,128)}), f32[32,16,2048]{2,1,0:T(8,128)}, u32[]{:S(2)}, u32[]{:S(2)}) async-start(f32[32,16,2048]{2,1,0:T(8,128)} %bitcast.230), calls=%async_computation.8 | async-start | bytes 8388608 | tf_op jit(solution)/shard_map/all_to_all | solution.py:407
  1289.8 138.1 %reduce-scatter.33.cloned.1.call-start = ((), (), s32[]{:S(2)}) async-start(), calls=%async_computation.25 | async-start | bytes 270336
  1292.0 273.5 %reduce-scatter.31.cloned.1.call-start = ((), (), s32[]{:S(2)}) async-start(), calls=%async_computation.24 | async-start | bytes 270336
  1517.3 90.4 %all-to-all-start.1 = ((f32[1,512,512]{2,0,1:T(1,128)}), f32[1,512,512]{2,0,1:T(1,128)S(1)}, u32[]{:S(2)}, u32[]{:S(2)}) async-start(f32[1,512,512]{2,0,1:T(1,128)} %copy.97), calls=%async_computation.9 | async-start | bytes 2097152 | tf_op jit(solution)/shard_map/all_to_all | solution.py:412
  (171 other events, 7119.4 us)
Sparse Core Ops, SparseCore 0:
  11.5 61.0 all-gather.6
  75.9 60.8 all-gather.8
  140.3 54.1 all-gather.10
  197.8 54.0 all-gather.12
  436.3 18.2 reduce-scatter.14
  456.7 14.5 reduce-scatter.16
  474.2 131.2 reduce-scatter.28
  608.3 130.6 reduce-scatter.24
  741.9 132.5 reduce-scatter.26
  881.2 99.0 reduce-scatter.22
  983.3 146.2 reduce-scatter.18
  1132.4 144.6 reduce-scatter.20
  1293.5 134.2 reduce-scatter.32
  1433.1 132.3 reduce-scatter.30
where the time goes:
time: 1630 us; the launch traced here: 1620 us
  waiting for transfers between devices  859 us (53%)
  blocking collectives  471 us (29%)
  matrix products  159 us (10%)
  other arithmetic  51.6 us (3%)
  local copies, waits for them, and re-layouts  33.4 us (2%)
  starting transfers between devices  26.3 us (2%)
  between operations  18.5 us (1%)
    reduce_scatter x1, waiting for transfers between devices, local(): lax.psum_scatter(grad_up_local, ('dp', 'seq', 'shard'), scatter_dimension...  148 us
    reduce_scatter x1, waiting for transfers between devices, local(): lax.psum_scatter(grad_down_local, ('dp', 'seq', 'shard'), scatter_dimensi...  146 us
    reduce_scatter x1, waiting for transfers between devices, local(): lax.psum_scatter(grad_glu_w, ('dp', 'seq', 'shard'), scatter_dimension=0,...  135 us
    reduce_scatter x1, waiting for transfers between devices, local(): lax.psum_scatter(grad_out_w, ('dp', 'seq', 'shard'), scatter_dimension=0,...  133 us
    reduce_scatter x1, waiting for transfers between devices, local(): lax.psum_scatter(grad_point, ('dp', 'seq', 'shard'), scatter_dimension=0,...  113 us
    reduce_scatter x1, waiting for transfers between devices, local(): lax.psum_scatter(grad_qkv_w, ('dp', 'seq', 'shard'), scatter_dimension=0,...  105 us
    unnamed x1, blocking collectives  104 us
    unnamed x16, waiting for transfers between devices  64.6 us
  transfers between devices with their start and end apart: 20, of which 11 were waited for; matrix products, arithmetic and copies ran while one was open for 12% of the time, Pallas kernels for 0%

commit v1 on v0

--- a/solution.py
+++ b/solution.py
@@ -1,6 +1,10 @@
+import functools
+
 import jax
 import jax.numpy as jnp
 from jax import lax
+from jax.experimental import pallas as pl
+from jax.experimental.pallas import tpu as pltpu
 from jax.sharding import PartitionSpec as P
 
 D = 512
@@ -22,6 +26,532 @@
 COEF_C = 2.0315
 HIGHEST = lax.Precision.HIGHEST
 
+
+AXES = ("dp", "seq", "shard")
+MESH = pl.DeviceIdType.MESH
+WIDTHS = (FF, FF, FF, FF, 3 * D, D, 2 * D, D)
+STARTS = tuple(sum(WIDTHS[:i]) for i in range(9))
+BLOCK = 512
+
+
+class Cube:
+    def __init__(self, dp_size):
+        self.dp_size = dp_size
+        self.levels = dp_size.bit_length() - 1
+        self.digits = self.levels + 2
+        self.total = dp_size * 4
+        high = list(range(self.levels - 1))
+        low, seq, core = self.levels - 1, self.levels, self.levels + 1
+        self.gather_orders = (high + [low, seq, core], high + [seq, low, core])
+        self.scatter_orders = tuple(order[::-1] for order in self.gather_orders)
+
+    def mine(self):
+        d = lax.axis_index("dp")
+        bits = [lax.rem(d // (1 << (self.levels - 1 - k)), 2) for k in range(self.levels)]
+        return bits + [lax.axis_index("seq"), lax.axis_index("shard")]
+
+    def partner(self, k):
+        d, s, c = lax.axis_index("dp"), lax.axis_index("seq"), lax.axis_index("shard")
+        if k == self.levels:
+            return (d, 1 - s, c)
+        if k == self.levels + 1:
+            return (d, s, 1 - c)
+        step = 1 << (self.levels - 1 - k)
+        bit = lax.rem(d // step, 2)
+        return (d + (1 - 2 * bit) * step, s, c)
+
+    def index(self):
+        return (lax.axis_index("dp") * 2 + lax.axis_index("seq")) * 2 + lax.axis_index("shard")
+
+    def coords(self, index):
+        return (index // 4, lax.rem(index // 2, 2), lax.rem(index, 2))
+
+    def greet_partners(self):
+        barrier = pltpu.get_barrier_semaphore()
+        for k in range(self.digits):
+            pl.semaphore_signal(barrier, inc=1, device_id=self.partner(k), device_id_type=MESH)
+        pl.semaphore_wait(barrier, self.digits)
+
+    def greet_all(self):
+        barrier = pltpu.get_barrier_semaphore()
+        me = self.index()
+
+        @pl.loop(1, self.total)
+        def _(i):
+            peer = self.coords(lax.rem(me + i, self.total))
+            pl.semaphore_signal(barrier, inc=1, device_id=peer, device_id_type=MESH)
+
+        pl.semaphore_wait(barrier, self.total - 1)
+
+
+def halves(width):
+    cut = (width // 128 + 1) // 2 * 128
+    return ((0, cut), (cut, width - cut))
+
+
+def remote(src, dst, send_sem, recv_sem, peer):
+    return pltpu.make_async_remote_copy(
+        src_ref=src,
+        dst_ref=dst,
+        send_sem=send_sem,
+        recv_sem=recv_sem,
+        device_id=peer,
+        device_id_type=MESH,
+    )
+
+
+def gather_kernel(cube, groups, *refs):
+    shards, outs = refs[:groups], refs[groups : 2 * groups]
+    own_sem, send_sem, recv_sem = refs[2 * groups :]
+    cube.greet_partners()
+    mine = cube.mine()
+    locals_ = []
+    for g in range(groups):
+        copy = pltpu.make_async_copy(shards[g], outs[g].at[tuple(mine)], own_sem.at[g])
+        copy.start()
+        locals_.append(copy)
+
+    def make(g, half, stage):
+        order = cube.gather_orders[half]
+        columns = pl.ds(*halves(shards[g].shape[-1])[half])
+        done = order[:stage]
+        index = tuple(slice(None) if k in done else mine[k] for k in range(cube.digits))
+        place = outs[g].at[index + (slice(None), columns)]
+        source = shards[g].at[:, columns] if stage == 0 else place
+        return remote(
+            source,
+            place,
+            send_sem.at[g, half, stage],
+            recv_sem.at[g, half, stage],
+            cube.partner(order[stage]),
+        )
+
+    copies = {}
+    for g in range(groups):
+        for half in range(2):
+            copies[g, half, 0] = make(g, half, 0)
+            copies[g, half, 0].start()
+    for tick in range(cube.digits + 2 * (groups - 1)):
+        for g in range(groups):
+            stage = tick - 2 * g
+            if not 0 <= stage < cube.digits:
+                continue
+            for half in range(2):
+                copies[g, half, stage].wait_recv()
+                if stage == 0 and half == 0:
+                    locals_[g].wait()
+                if stage + 1 < cube.digits:
+                    copies[g, half, stage + 1] = make(g, half, stage + 1)
+                    copies[g, half, stage + 1].start()
+    for copy in copies.values():
+        copy.wait_send()
+
+
+def gather_groups(cube, shards, collective_id):
+    groups = len(shards)
+    lead = (2,) * cube.digits
+    return pl.pallas_call(
+        functools.partial(gather_kernel, cube, groups),
+        out_shape=[jax.ShapeDtypeStruct(lead + s.shape, s.dtype) for s in shards],
+        in_specs=[pl.BlockSpec(memory_space=pl.ANY)] * groups,
+        out_specs=[pl.BlockSpec(memory_space=pl.ANY)] * groups,
+        scratch_shapes=[
+            pltpu.SemaphoreType.DMA((groups,)),
+            pltpu.SemaphoreType.DMA((groups, 2, cube.digits)),
+            pltpu.SemaphoreType.DMA((groups, 2, cube.digits)),
+        ],
+        compiler_params=pltpu.CompilerParams(
+            collective_id=collective_id, has_side_effects=True
+        ),
+        name="gather_weights",
+    )(*shards)
+
+
+def scatter_kernel(cube, groups, *refs):
+    parts, outs = refs[:groups], refs[groups : 2 * groups]
+    rest = refs[2 * groups :]
+    sums = rest[:groups]
+    landed = rest[groups : groups + groups * 2 * cube.digits]
+    own_sem, send_sem, recv_sem = rest[groups + groups * 2 * cube.digits :]
+    cube.greet_partners()
+    mine = cube.mine()
+    last = cube.digits - 1
+
+    def slot(g, half, stage):
+        return landed[(g * 2 + half) * cube.digits + stage]
+
+    def place(g, half, stage, bit_of):
+        order = cube.scatter_orders[half]
+        columns = pl.ds(*halves(outs[g].shape[-1])[half])
+        index = []
+        for k in range(cube.digits - 1):
+            at = order.index(k)
+            if at > stage:
+                index.append(slice(None))
+            else:
+                index.append(bit_of(k) if at == stage else mine[k])
+        return tuple(index) + (slice(None), columns)
+
+    def make(g, half, stage):
+        order = cube.scatter_orders[half]
+        if stage == 0:
+            index = (slice(None),) * last + (1 - mine[last],)
+            columns = pl.ds(*halves(outs[g].shape[-1])[half])
+            source = parts[g].at[index + (slice(None), columns)]
+        else:
+            source = sums[g].at[place(g, half, stage, lambda k: 1 - mine[k])]
+        return remote(
+            source,
+            slot(g, half, stage),
+            send_sem.at[g, half, stage],
+            recv_sem.at[g, half, stage],
+            cube.partner(order[stage]),
+        )
+
+    copies = {}
+    locals_ = []
+    for g in range(groups):
+        copy = pltpu.make_async_copy(
+            parts[g].at[(slice(None),) * last + (mine[last],)], sums[g], own_sem.at[g]
+        )
+        copy.start()
+        locals_.append(copy)
+        for half in range(2):
+            copies[g, half, 0] = make(g, half, 0)
+            copies[g, half, 0].start()
+
+    def add(g, half, stage):
+        order = cube.scatter_orders[half]
+        columns = pl.ds(*halves(outs[g].shape[-1])[half])
+        free = [k for k in range(last) if order.index(k) > stage]
+        count = 1 << len(free)
+        target, extra = sums[g], slot(g, half, stage)
+
+        def one(i):
+            digit = {k: lax.rem(i // (1 << (len(free) - 1 - n)), 2) for n, k in enumerate(free)}
+            full = tuple(digit.get(k, mine[k]) for k in range(last)) + (slice(None), columns)
+            short = tuple(digit[k] for k in free)
+            total = target[full].astype(jnp.float32) + extra[short + (slice(None), slice(None))].astype(jnp.float32)
+            if stage == last:
+                outs[g][:, columns] = total
+            else:
+                target[full] = total.astype(target.dtype)
+
+        if count == 1:
+            one(0)
+        else:
+            pl.loop(0, count)(one)
+
+    for stage in range(cube.digits):
+        for g in range(groups):
+            if stage == 0:
+                locals_[g].wait()
+            for half in range(2):
+                copies[g, half, stage].wait_recv()
+                add(g, half, stage)
+                if stage < last:
+                    copies[g, half, stage + 1] = make(g, half, stage + 1)
+                    copies[g, half, stage + 1].start()
+    for copy in copies.values():
+        copy.wait_send()
+
+
+def scatter_groups(cube, parts, collective_id):
+    groups = len(parts)
+    scratch = [pltpu.VMEM((2,) * (cube.digits - 1) + p.shape[-2:], p.dtype) for p in parts]
+    for p in parts:
+        for half in range(2):
+            for stage in range(cube.digits):
+                lead = (2,) * (cube.digits - 1 - stage)
+                scratch.append(pltpu.VMEM(lead + (p.shape[-2], halves(p.shape[-1])[half][1]), p.dtype))
+    scratch += [
+        pltpu.SemaphoreType.DMA((groups,)),
+        pltpu.SemaphoreType.DMA((groups, 2, cube.digits)),
+        pltpu.SemaphoreType.DMA((groups, 2, cube.digits)),
+    ]
+    return pl.pallas_call(
+        functools.partial(scatter_kernel, cube, groups),
+        out_shape=[jax.ShapeDtypeStruct(p.shape[-2:], jnp.float32) for p in parts],
+        in_specs=[pl.BlockSpec(memory_space=pl.ANY)] * groups,
+        out_specs=[pl.BlockSpec(memory_space=pltpu.VMEM)] * groups,
+        scratch_shapes=scratch,
+        compiler_params=pltpu.CompilerParams(
+            collective_id=collective_id, has_side_effects=True, vmem_limit_bytes=48 << 20
+        ),
+        name="scatter_grads",
+    )(*parts)
+
+
+def collect_kernel(cube, x_ref, o_ref, send_sem, recv_sem):
+    me = cube.index()
+    cube.greet_all()
+
+    def make(i):
+        to = lax.rem(me + i, cube.total)
+        return remote(x_ref, o_ref.at[i], send_sem.at[i], recv_sem.at[i], cube.coords(to))
+
+    @pl.loop(1, cube.total)
+    def _(i):
+        make(i).start()
+
+    o_ref[0] = x_ref[...]
+
+    @pl.loop(1, cube.total)
+    def _(i):
+        make(i).wait()
+
+
+def collect(cube, x, collective_id):
+    return pl.pallas_call(
+        functools.partial(collect_kernel, cube),
+        out_shape=jax.ShapeDtypeStruct((cube.total,) + x.shape, x.dtype),
+        in_specs=[pl.BlockSpec(memory_space=pltpu.VMEM)],
+        out_specs=pl.BlockSpec(memory_space=pltpu.VMEM),
+        scratch_shapes=[
+            pltpu.SemaphoreType.DMA((cube.total,)),
+            pltpu.SemaphoreType.DMA((cube.total,)),
+        ],
+        compiler_params=pltpu.CompilerParams(
+            collective_id=collective_id, has_side_effects=True
+        ),
+        name="collect_stats",
+    )(x)
+
+
+def by_matrix(j, action):
+    for width in sorted(set(WIDTHS)):
+        members = [i for i in range(8) if WIDTHS[i] == width]
+        hit = functools.reduce(jnp.logical_or, [j == i for i in members])
+        pl.when(hit)(functools.partial(action, width // 4))
+
+
+def quarter_start(t):
+    j, q = t // 4, lax.rem(t, 4)
+    start = 0
+    for i in range(8):
+        start = start + jnp.where(j == i, STARTS[i] + q * (WIDTHS[i] // 4), 0)
+    return pl.multiple_of(start, 128)
+
+
+def owner_coords(cube, t):
+    return ((t // 4) * (cube.dp_size // 8), lax.rem(t // 2, 2), lax.rem(t, 2))
+
+
+def spread_kernel(cube, x_ref, o_ref, own_sem, send_sem, recv_sem):
+    me = cube.index()
+    repeat = cube.dp_size // 8
+    d, s, c = lax.axis_index("dp"), lax.axis_index("seq"), lax.axis_index("shard")
+    owner = lax.rem(d, repeat) == 0
+    mine = ((d // repeat) * 2 + s) * 2 + c
+    cube.greet_all()
+
+    def send(i, wait):
+        t = lax.rem(mine + i, 32)
+        peer = owner_coords(cube, t)
+        other = jnp.logical_or(jnp.logical_not(owner), i > 0)
+
+        def go(width):
+            src = x_ref.at[:, pl.ds(quarter_start(t), width)]
+            dst = o_ref.at[me, :, pl.ds(0, width)]
+            copy = remote(src, dst, send_sem.at[i], recv_sem.at[me], peer)
+            if wait:
+                copy.wait_send()
+            else:
+                copy.start()
+
+        pl.when(other)(lambda: by_matrix(t // 4, go))
+
+    pl.loop(0, 32)(functools.partial(send, wait=False))
+
+    def keep(width):
+        copy = pltpu.make_async_copy(
+            x_ref.at[:, pl.ds(quarter_start(mine), width)],
+            o_ref.at[me, :, pl.ds(0, width)],
+            own_sem,
+        )
+        copy.start()
+        copy.wait()
+
+    def receive(width):
+        @pl.loop(1, cube.total)
+        def _(i):
+            source = lax.rem(me + i, cube.total)
+            place = o_ref.at[source, :, pl.ds(0, width)]
+            remote(
+                place, place, send_sem.at[0], recv_sem.at[source], cube.coords(source)
+            ).wait_recv()
+
+    @pl.when(owner)
+    def _():
+        by_matrix(mine // 4, keep)
+        by_matrix(mine // 4, receive)
+
+    pl.loop(0, 32)(functools.partial(send, wait=True))
+
+
+def spread(cube, x, collective_id):
+    return pl.pallas_call(
+        functools.partial(spread_kernel, cube),
+        out_shape=jax.ShapeDtypeStruct((cube.total, x.shape[0], BLOCK), x.dtype),
+        in_specs=[pl.BlockSpec(memory_space=pl.ANY)],
+        out_specs=pl.BlockSpec(memory_space=pl.ANY),
+        scratch_shapes=[
+            pltpu.SemaphoreType.DMA,
+            pltpu.SemaphoreType.DMA((32,)),
+            pltpu.SemaphoreType.DMA((cube.total,)),
+        ],
+        compiler_params=pltpu.CompilerParams(
+            collective_id=collective_id, has_side_effects=True
+        ),
+        name="spread_momentum",
+    )(x)
+
+
+def restore_kernel(cube, x_ref, o_ref, own_sem, send_sem, recv_sem):
+    me = cube.index()
+    repeat = cube.dp_size // 8
+    d, s, c = lax.axis_index("dp"), lax.axis_index("seq"), lax.axis_index("shard")
+    owner = lax.rem(d, repeat) == 0
+    mine = ((d // repeat) * 2 + s) * 2 + c
+    cube.greet_all()
+
+    def send_all(wait, width):
+        @pl.loop(1, cube.total)
+        def _(i):
+            to = lax.rem(me + i, cube.total)
+            src = x_ref.at[to, :, pl.ds(0, width)]
+            dst = o_ref.at[:, pl.ds(quarter_start(mine), width)]
+            copy = remote(src, dst, send_sem.at[i], recv_sem.at[mine], cube.coords(to))
+            if wait:
+                copy.wait_send()
+            else:
+                copy.start()
+
+    def keep(width):
+        copy = pltpu.make_async_copy(
+            x_ref.at[me, :, pl.ds(0, width)],
+            o_ref.at[:, pl.ds(quarter_start(mine), width)],
+            own_sem,
+        )
+        copy.start()
+        copy.wait()
+
+    @pl.when(owner)
+    def _():
+        by_matrix(mine // 4, functools.partial(send_all, False))
+        by_matrix(mine // 4, keep)
+
+    def receive(i):
+        t = lax.rem(mine + i, 32)
+        other = jnp.logical_or(jnp.logical_not(owner), i > 0)
+
+        def go(width):
+            place = o_ref.at[:, pl.ds(quarter_start(t), width)]
+            remote(
+                place, place, send_sem.at[0], recv_sem.at[t], owner_coords(cube, t)
+            ).wait_recv()
+
+        pl.when(other)(lambda: by_matrix(t // 4, go))
+
+    pl.loop(0, 32)(receive)
+
+    @pl.when(owner)
+    def _():
+        by_matrix(mine // 4, functools.partial(send_all, True))
+
+
+def restore(cube, x, collective_id):
+    return pl.pallas_call(
+        functools.partial(restore_kernel, cube),
+        out_shape=jax.ShapeDtypeStruct((x.shape[1], STARTS[8]), x.dtype),
+        in_specs=[pl.BlockSpec(memory_space=pl.ANY)],
+        out_specs=pl.BlockSpec(memory_space=pl.ANY),
+        scratch_shapes=[
+            pltpu.SemaphoreType.DMA,
+            pltpu.SemaphoreType.DMA((cube.total,)),
+            pltpu.SemaphoreType.DMA((32,)),
+        ],
+        compiler_params=pltpu.CompilerParams(
+            collective_id=collective_id, has_side_effects=True
+        ),
+        name="restore_rows",
+    )(x)
+
+
+def split(value):
+    high = value.astype(jnp.bfloat16)
+    low = (value - high.astype(jnp.float32)).astype(jnp.bfloat16)
+    return high, low
+
+
+def product(left, right):
+    (lh, ll), (rh, rl) = left, right
+    dot = functools.partial(jnp.dot, preferred_element_type=jnp.float32)
+    return dot(lh, rh) + (dot(lh, rl) + dot(ll, rh))
+
+
+def orthogonalize_kernel(cube, x_ref, o_ref, gram_ref, work, landed, send_sem, recv_sem):
+    barrier = pltpu.get_barrier_semaphore()
+    peers = (cube.partner(cube.levels + 1), cube.partner(cube.levels))
+    for peer in peers:
+        pl.semaphore_signal(barrier, inc=1, device_id=peer, device_id_type=MESH)
+    pl.semaphore_wait(barrier, 2)
+    repeat = cube.dp_size // 8
+    j = lax.axis_index("dp") // repeat
+    width = 0
+    for i in range(8):
+        width = width + jnp.where(j == i, WIDTHS[i] // 4, 0)
+    column = lax.broadcasted_iota(jnp.int32, (D, BLOCK), 1)
+    block = jnp.where(column < width, x_ref[...].astype(jnp.float32), 0.0)
+    bh, bl = split(block)
+    dot_t = lambda a, b: lax.dot_general(
+        a, b, (((1,), (1,)), ((), ())), preferred_element_type=jnp.float32
+    )
+    gram_ref[0] = dot_t(bh, bh) + (dot_t(bh, bl) + dot_t(bl, bh))
+    for step in range(2):
+        copy = remote(
+            gram_ref.at[step], landed.at[step], send_sem.at[step], recv_sem.at[step], peers[step]
+        )
+        copy.start()
+        copy.wait()
+        gram_ref[step + 1] = gram_ref[step] + landed[step]
+    gram = gram_ref[2]
+    row = lax.broadcasted_iota(jnp.int32, (D, D), 0)
+    col = lax.broadcasted_iota(jnp.int32, (D, D), 1)
+    eye = row == col
+    square = jnp.sum(jnp.sum(jnp.where(eye, gram, 0.0), axis=1, keepdims=True), axis=0, keepdims=True)
+    scale = 1.0 / (jnp.sqrt(square) + 1e-07)
+    gram = gram * (scale * scale)
+    block = block * scale
+    for step in range(5):
+        parts = split(gram)
+        mixed = COEF_B * gram + COEF_C * product(parts, parts)
+        mixed = jnp.where(eye, mixed + COEF_A, mixed)
+        mixed_parts = split(mixed)
+        block = product(mixed_parts, split(block))
+        if step < 4:
+            gram = product(mixed_parts, split(product(mixed_parts, parts)))
+    o_ref[...] = block.astype(o_ref.dtype)
+
+
+def orthogonalize_blocks(cube, x, out_dtype, collective_id):
+    return pl.pallas_call(
+        functools.partial(orthogonalize_kernel, cube),
+        out_shape=jax.ShapeDtypeStruct((D, BLOCK), out_dtype),
+        in_specs=[pl.BlockSpec(memory_space=pltpu.VMEM)],
+        out_specs=pl.BlockSpec(memory_space=pltpu.VMEM),
+        scratch_shapes=[
+            pltpu.VMEM((3, D, D), jnp.float32),
+            pltpu.VMEM((8, 128), jnp.float32),
+            pltpu.VMEM((2, D, D), jnp.float32),
+            pltpu.SemaphoreType.DMA((2,)),
+            pltpu.SemaphoreType.DMA((2,)),
+        ],
+        compiler_params=pltpu.CompilerParams(
+            collective_id=collective_id, has_side_effects=True, vmem_limit_bytes=48 << 20
+        ),
+        name="orthogonalize",
+    )(x)
 
 def with_halo(value, sides, width):
     for axis, dim in sides:
@@ -178,23 +708,8 @@
     )
 
 
-def orthogonalize_columns(matrix, start, part_width):
-    iterate = matrix / (jnp.sqrt(jnp.sum(matrix * matrix)) + 1e-07)
-    for iter_step in range(4):
-        gram = jnp.dot(iterate, iterate.T, precision=HIGHEST)
-        mixed = COEF_B * gram + COEF_C * jnp.dot(gram, gram, precision=HIGHEST)
-        iterate = COEF_A * iterate + jnp.dot(mixed, iterate, precision=HIGHEST)
-    gram = jnp.dot(iterate, iterate.T, precision=HIGHEST)
-    mixed = COEF_B * gram + COEF_C * jnp.dot(gram, gram, precision=HIGHEST)
-    columns = lax.dynamic_slice_in_dim(iterate, start, part_width, 1)
-    return COEF_A * columns + jnp.dot(mixed, columns, precision=HIGHEST)
-
-
-def pad_columns(matrix, width):
-    return jnp.pad(matrix, ((0, 0), (0, width - matrix.shape[1])))
-
-
 def local(
+    cube,
     inputs,
     cotangent,
     w_up,
@@ -218,20 +733,25 @@
     m_rel,
 ):
     bf16 = jnp.bfloat16
-    gathered = (
-        lax.all_gather(w_up.astype(bf16), ("dp", "seq", "shard"), axis=0, tiled=True),
-        lax.all_gather(w_down.astype(bf16), ("dp", "seq", "shard"), axis=0, tiled=True),
-        lax.all_gather(w_qkv.astype(bf16), ("dp", "seq", "shard"), axis=0, tiled=True),
-        lax.all_gather(w_out.astype(bf16), ("dp", "seq", "shard"), axis=0, tiled=True),
-        lax.all_gather(w_glu.astype(bf16), ("dp", "seq", "shard"), axis=0, tiled=True),
-        lax.all_gather(w_point.astype(bf16), ("dp", "seq", "shard"), axis=0, tiled=True),
-        lax.all_gather(vectors.astype(bf16), ("dp", "seq", "shard"), axis=0, tiled=True),
-        lax.all_gather(depth_kernel.astype(bf16), ("dp", "seq", "shard"), axis=0, tiled=True),
-        lax.all_gather(rel_bias.astype(bf16), ("dp", "seq", "shard"), axis=0, tiled=True),
-    )
-    up_all, down_all, qkv_w, out_w, glu_w, point_w, vec_low, kern_low, rel_low = gathered
-    gains = vec_low.astype(jnp.float32)
-    kernel = kern_low.astype(jnp.float32)
+    rows = w_up.shape[0]
+    small = jnp.concatenate([vectors, depth_kernel, rel_bias.reshape(rows, -1)], axis=1)
+    small_count = small.shape[1]
+    small = jnp.pad(small, ((0, 0), (0, 128 - small_count)))
+    shard_groups = (
+        jnp.concatenate([w_up[:, :FF], w_down[:, :FF], small], axis=1).astype(bf16),
+        jnp.concatenate([w_qkv, w_out, w_glu, w_point], axis=1).astype(bf16),
+        jnp.concatenate([w_up[:, FF:], w_down[:, FF:]], axis=1).astype(bf16),
+    )
+    first, middle, second = [
+        full.reshape(D, -1) for full in gather_groups(cube, shard_groups, 0)
+    ]
+    up_first, down_first, small_low = first[:, :FF], first[:, FF : 2 * FF], first[:, 2 * FF :]
+    qkv_w, out_w = middle[:, : 3 * D], middle[:, 3 * D : 4 * D]
+    glu_w, point_w = middle[:, 4 * D : 6 * D], middle[:, 6 * D :]
+    up_second, down_second = second[:, :FF], second[:, FF:]
+    gains = small_low[:, :7].astype(jnp.float32)
+    kernel = small_low[:, 7 : 7 + K].astype(jnp.float32)
+    rel_low = small_low[:, 7 + K : small_count].reshape(NB, H)
     bucket_hit = (bucket_table[:, None] == jnp.arange(NB, dtype=jnp.int32)[None, :]).astype(
         jnp.float32
     )
@@ -240,15 +760,22 @@
     row_count = seq_rows.shape[0]
     first_row = lax.axis_index("seq") * row_count
     token_total = row_count * lax.axis_size(("dp", "seq", "shard"))
-    section_one, ffn_saved = ffn_forward(seq_rows, gains[:, 0], up_all[:, :FF], down_all[:, :FF])
+    section_one, ffn_saved = ffn_forward(seq_rows, gains[:, 0], up_first, down_first)
     normed_out2, normed2, inverse2 = layer_norm(section_one, gains[:, 1])
     lifted2 = normed_out2.astype(bf16)
     projected = matmul(lifted2, qkv_w).astype(bf16)
     query = projected[:, :D]
-    keys, values = (
-        lax.all_gather(projected[:, D : 2 * D], "seq", axis=0, tiled=True),
-        lax.all_gather(projected[:, 2 * D :], "seq", axis=0, tiled=True),
-    )
+    pair = [(0, 1), (1, 0)]
+    other = lax.ppermute(projected[:, D:], "seq", pair)
+    early = lax.axis_index("seq") == 0
+    both = jnp.concatenate(
+        [
+            jnp.where(early, projected[:, D:], other),
+            jnp.where(early, other, projected[:, D:]),
+        ],
+        axis=0,
+    )
+    keys, values = both[:, :D], both[:, D:]
     attended, log_total = attention_forward(query, keys, values, offsets, first_row)
     attended_low = attended.astype(bf16)
     section_two = section_one + matmul(attended_low, out_w)
@@ -260,52 +787,46 @@
     glu = first_half * sig_gate
     glu_wide = with_halo(glu, (("seq", 0),), K // 2)
     conv = depthwise(glu_wide, kernel, row_count)
-    mean = lax.psum(jnp.sum(conv, axis=0), ("dp", "seq", "shard")) / token_total
+    part_sum = jnp.sum(conv, axis=0)
+    part_mean = part_sum / row_count
+    part_square = jnp.sum(jnp.square(conv - part_mean), axis=0)
+    stats = collect(cube, jnp.concatenate([part_sum, part_square]).reshape(8, 128), 1)
+    stats = stats.reshape(cube.total, 2, D)
+    mean = jnp.sum(stats[:, 0], axis=0) / token_total
+    spread_of_means = jnp.square(stats[:, 0] / row_count - mean) * row_count
+    variance = jnp.sum(stats[:, 1] + spread_of_means, axis=0) / token_total
     centred = conv - mean
-    variance = lax.psum(jnp.sum(centred * centred, axis=0), ("dp", "seq", "shard")) / token_total
     inv_std = lax.rsqrt(variance + EPS_BATCH)
     normed_bn = centred * inv_std
     batch_out = normed_bn * gains[:, 5] + gains[:, 6]
     swish_low = jax.nn.silu(batch_out).astype(bf16)
     section_three = section_two + matmul(swish_low, point_w)
     section_four, tail_saved = ffn_forward(
-        section_three, gains[:, 3], up_all[:, FF:], down_all[:, FF:]
+        section_three, gains[:, 3], up_second, down_second
     )
     outputs, normed5, inverse5 = layer_norm(section_four, gains[:, 4])
-    again = (
-        lax.all_gather(w_up.astype(bf16), ("dp", "seq", "shard"), axis=0, tiled=True),
-        lax.all_gather(w_down.astype(bf16), ("dp", "seq", "shard"), axis=0, tiled=True),
-        lax.all_gather(w_qkv.astype(bf16), ("dp", "seq", "shard"), axis=0, tiled=True),
-        lax.all_gather(w_out.astype(bf16), ("dp", "seq", "shard"), axis=0, tiled=True),
-        lax.all_gather(w_glu.astype(bf16), ("dp", "seq", "shard"), axis=0, tiled=True),
-        lax.all_gather(w_point.astype(bf16), ("dp", "seq", "shard"), axis=0, tiled=True),
-        lax.all_gather(vectors.astype(bf16), ("dp", "seq", "shard"), axis=0, tiled=True),
-        lax.all_gather(depth_kernel.astype(bf16), ("dp", "seq", "shard"), axis=0, tiled=True),
-    )
-    up_back, down_back, qkv_back, out_back, glu_back, point_back, vec_back, kern_back = again
-    gains_back = vec_back.astype(jnp.float32)
-    kernel_back = kern_back.astype(jnp.float32)
-    grad_four, gain_four = norm_back(cotangent[0], normed5, inverse5, gains_back[:, 4])
+    grad_four, gain_four = norm_back(cotangent[0], normed5, inverse5, gains[:, 4])
     grad_three, grad_up_two, grad_down_two, gain_three = ffn_backward(
-        grad_four, tail_saved, gains_back[:, 3], up_back[:, FF:], down_back[:, FF:]
+        grad_four, tail_saved, gains[:, 3], up_second, down_second
     )
     grad_three_low = grad_three.astype(bf16)
     grad_point = matmul_left_t(swish_low, grad_three_low)
-    grad_batch = matmul_right_t(grad_three_low, point_back) * silu_slope(batch_out)
-    grad_normed = grad_batch * gains_back[:, 5]
-    sum_normed, sum_cross = lax.psum(
-        (jnp.sum(grad_normed, axis=0), jnp.sum(grad_normed * normed_bn, axis=0)),
-        ("dp", "seq", "shard"),
-    )
+    grad_batch = matmul_right_t(grad_three_low, point_w) * silu_slope(batch_out)
+    grad_normed = grad_batch * gains[:, 5]
+    sums = jnp.concatenate(
+        [jnp.sum(grad_normed, axis=0), jnp.sum(grad_normed * normed_bn, axis=0)]
+    )
+    sums = jnp.sum(collect(cube, sums.reshape(8, 128), 2), axis=0).reshape(2, D)
+    sum_normed, sum_cross = sums[0], sums[1]
     grad_conv = inv_std * (
         grad_normed - sum_normed / token_total - normed_bn * sum_cross / token_total
     )
     grad_wide = with_halo(grad_conv, (("seq", 0),), K // 2)
-    grad_glu = grad_wide[K - 1 : K - 1 + row_count] * kernel_back[:, 0]
+    grad_glu = grad_wide[K - 1 : K - 1 + row_count] * kernel[:, 0]
     for tap_idx in range(1, K):
         grad_glu = (
             grad_glu
-            + grad_wide[K - 1 - tap_idx : K - 1 - tap_idx + row_count] * kernel_back[:, tap_idx]
+            + grad_wide[K - 1 - tap_idx : K - 1 - tap_idx + row_count] * kernel[:, tap_idx]
         )
     grad_kernel = jnp.stack(
         [
@@ -319,33 +840,32 @@
     ).astype(bf16)
     grad_glu_w = matmul_left_t(lifted3, grad_gates)
     grad_two_part, gain_two = norm_back(
-        matmul_right_t(grad_gates, glu_back), normed3, inverse3, gains_back[:, 2]
+        matmul_right_t(grad_gates, glu_w), normed3, inverse3, gains[:, 2]
     )
     grad_two = grad_three + grad_two_part
     grad_two_low = grad_two.astype(bf16)
     grad_out_w = matmul_left_t(attended_low, grad_two_low)
-    grad_attended = matmul_right_t(grad_two_low, out_back).astype(bf16)
+    grad_attended = matmul_right_t(grad_two_low, out_w).astype(bf16)
     delta = jnp.sum(
         (grad_attended.astype(jnp.float32) * attended).reshape(row_count, H, DH), axis=2
     )
     query_grad, key_grad, value_grad, offset_grad = attention_backward(
         query, keys, values, offsets, first_row, log_total, grad_attended, delta
     )
-    key_own, value_own = (
-        lax.psum_scatter(key_grad, "seq", scatter_dimension=0, tiled=True),
-        lax.psum_scatter(value_grad, "seq", scatter_dimension=0, tiled=True),
-    )
+    keys_grad = jnp.concatenate([key_grad, value_grad], axis=1)
+    theirs = lax.dynamic_slice_in_dim(keys_grad, row_count - first_row, row_count, 0)
+    own = lax.dynamic_slice_in_dim(keys_grad, first_row, row_count, 0)
+    own = own + lax.ppermute(theirs, "seq", pair)
+    key_own, value_own = own[:, :D], own[:, D:]
     grad_proj = jnp.concatenate([query_grad, key_own, value_own], axis=1).astype(bf16)
     grad_qkv_w = matmul_left_t(lifted2, grad_proj)
     grad_one_part, gain_one = norm_back(
-        matmul_right_t(grad_proj, qkv_back), normed2, inverse2, gains_back[:, 1]
+        matmul_right_t(grad_proj, qkv_w), normed2, inverse2, gains[:, 1]
     )
     grad_one = grad_two + grad_one_part
     input_grad, grad_up_one, grad_down_one, gain_zero = ffn_backward(
-        grad_one, ffn_saved, gains_back[:, 0], up_back[:, :FF], down_back[:, :FF]
-    )
-    grad_up_local = jnp.concatenate([grad_up_one, grad_up_two], axis=1)
-    grad_down_local = jnp.concatenate([grad_down_one, grad_down_two], axis=1)
+        grad_one, ffn_saved, gains[:, 0], up_first, down_first
+    )
     grad_vec_local = jnp.stack(
         [
             gain_zero,
@@ -359,82 +879,59 @@
         axis=1,
     )
     grad_rel_local = jnp.dot(bucket_hit.T, offset_grad.T, precision=HIGHEST)
-    shares = (
-        lax.psum_scatter(grad_up_local, ("dp", "seq", "shard"), scatter_dimension=0, tiled=True),
-        lax.psum_scatter(grad_down_local, ("dp", "seq", "shard"), scatter_dimension=0, tiled=True),
-        lax.psum_scatter(grad_qkv_w, ("dp", "seq", "shard"), scatter_dimension=0, tiled=True),
-        lax.psum_scatter(grad_out_w, ("dp", "seq", "shard"), scatter_dimension=0, tiled=True),
-        lax.psum_scatter(grad_glu_w, ("dp", "seq", "shard"), scatter_dimension=0, tiled=True),
-        lax.psum_scatter(grad_point, ("dp", "seq", "shard"), scatter_dimension=0, tiled=True),
-        lax.psum_scatter(grad_vec_local, ("dp", "seq", "shard"), scatter_dimension=0, tiled=True),
-        lax.psum_scatter(grad_kernel, ("dp", "seq", "shard"), scatter_dimension=0, tiled=True),
-        lax.psum_scatter(grad_rel_local, ("dp", "seq", "shard"), scatter_dimension=0, tiled=True),
-    )
-    (
-        grad_up,
-        grad_down,
-        grad_qkv,
-        grad_out,
-        grad_glu,
-        grad_pnt,
-        grad_vectors,
-        grad_depth,
-        grad_rel,
-    ) = shares
+    small_grads = jnp.concatenate(
+        [grad_vec_local, grad_kernel, grad_rel_local.reshape(D, -1)], axis=1
+    )
+    small_grads = jnp.pad(small_grads, ((0, 0), (0, 128 - small_count)))
+    lead = (2,) * cube.digits
+    grad_groups = [
+        jnp.concatenate(group, axis=1).astype(bf16).reshape(lead + (rows, -1))
+        for group in (
+            (grad_up_two, grad_down_two),
+            (grad_qkv_w, grad_out_w, grad_glu_w, grad_point),
+            (grad_up_one, grad_down_one, small_grads),
+        )
+    ]
+    share_second, share_middle, share_first = scatter_groups(cube, grad_groups, 3)
+    grad_up = jnp.concatenate([share_first[:, :FF], share_second[:, :FF]], axis=1)
+    grad_down = jnp.concatenate([share_first[:, FF : 2 * FF], share_second[:, FF:]], axis=1)
+    grad_qkv, grad_out = share_middle[:, : 3 * D], share_middle[:, 3 * D : 4 * D]
+    grad_glu, grad_pnt = share_middle[:, 4 * D : 6 * D], share_middle[:, 6 * D :]
+    grad_vectors = share_first[:, 2 * FF : 2 * FF + 7]
+    grad_depth = share_first[:, 2 * FF + 7 : 2 * FF + 7 + K]
+    grad_rel = share_first[:, 2 * FF + 7 + K : 2 * FF + small_count].reshape(-1, H)
     next_m_up = MOMENTUM * m_up + grad_up
     next_m_down = MOMENTUM * m_down + grad_down
     next_m_qkv = MOMENTUM * m_qkv + grad_qkv
     next_m_out = MOMENTUM * m_out + grad_out
     next_m_glu = MOMENTUM * m_glu + grad_glu
     next_m_point = MOMENTUM * m_point + grad_pnt
-    width = max(FF, 3 * D)
-    stacked = jnp.stack(
-        [
-            pad_columns(next_m_up[:, :FF], width),
-            pad_columns(next_m_up[:, FF:], width),
-            pad_columns(next_m_down[:, :FF], width),
-            pad_columns(next_m_down[:, FF:], width),
-            pad_columns(next_m_qkv, width),
-            pad_columns(next_m_out, width),
-            pad_columns(next_m_glu, width),
-            pad_columns(next_m_point, width),
-        ],
-        axis=0,
-    )
-    copies = lax.axis_size(("dp", "seq", "shard")) // 8
-    part_width = width // copies
-    outgoing = jnp.repeat(stacked, copies, axis=0)
-    owned = lax.all_to_all(
-        outgoing, ("dp", "seq", "shard"), split_axis=0, concat_axis=1, tiled=True
-    )
-    column_start = lax.axis_index(("dp", "seq", "shard")) % copies * part_width
-    ortho_part = orthogonalize_columns(owned[0], column_start, part_width)
-    returned = lax.all_to_all(
-        ortho_part[None], ("dp", "seq", "shard"), split_axis=1, concat_axis=0, tiled=True
-    )
-    own_rows = returned.shape[1]
-    mine = (
-        returned.reshape(8, copies, own_rows, part_width)
-        .transpose(0, 2, 1, 3)
-        .reshape(8, own_rows, width)
-    )
-    new_up = w_up - RATE_MATRIX * jnp.concatenate([mine[0, :, :FF], mine[1, :, :FF]], axis=1)
-    new_down = w_down - RATE_MATRIX * jnp.concatenate([mine[2, :, :FF], mine[3, :, :FF]], axis=1)
-    new_qkv = w_qkv - RATE_MATRIX * mine[4, :, : 3 * D]
-    new_out = w_out - RATE_MATRIX * mine[5, :, :D]
-    new_glu = w_glu - RATE_MATRIX * mine[6, :, : 2 * D]
-    new_point = w_point - RATE_MATRIX * mine[7, :, :D]
+    stacked = jnp.concatenate(
+        [next_m_up, next_m_down, next_m_qkv, next_m_out, next_m_glu, next_m_point], axis=1
+    )
+    owned = spread(cube, stacked, 4).reshape(D, BLOCK)
+    ortho = orthogonalize_blocks(cube, owned, bf16, 5)
+    mine = restore(cube, ortho.reshape(cube.total, rows, BLOCK), 6).astype(jnp.float32)
+    new_up = w_up - RATE_MATRIX * mine[:, : 2 * FF]
+    new_down = w_down - RATE_MATRIX * mine[:, 2 * FF : 4 * FF]
+    new_qkv = w_qkv - RATE_MATRIX * mine[:, STARTS[4] : STARTS[5]]
+    new_out = w_out - RATE_MATRIX * mine[:, STARTS[5] : STARTS[6]]
+    new_glu = w_glu - RATE_MATRIX * mine[:, STARTS[6] : STARTS[7]]
+    new_point = w_point - RATE_MATRIX * mine[:, STARTS[7] :]
     next_m_vectors = MOMENTUM * m_vectors + grad_vectors
     next_m_depth = MOMENTUM * m_depth + grad_depth
     next_m_rel = MOMENTUM * m_rel + grad_rel
-    square_vec, square_depth, square_rel = lax.psum(
-        (
+    squares = jnp.concatenate(
+        [
             jnp.sum(next_m_vectors * next_m_vectors, axis=0),
             jnp.sum(next_m_depth * next_m_depth, axis=0),
             jnp.sum(next_m_rel * next_m_rel, axis=0),
-        ),
-        ("dp", "seq", "shard"),
-    )
+        ]
+    )
+    squares = jnp.pad(squares, (0, 128 - squares.shape[0])).reshape(1, 128)
+    squares = jnp.sum(collect(cube, jnp.pad(squares, ((0, 7), (0, 0))), 7), axis=0)[0]
+    square_vec, square_depth = squares[:7], squares[7 : 7 + K]
+    square_rel = squares[7 + K : 7 + K + H]
     new_vectors = vectors - RATE_VECTOR * next_m_vectors * lax.rsqrt(square_vec / D + EPS_SCALE)
     new_depth = depth_kernel - RATE_VECTOR * next_m_depth * lax.rsqrt(square_depth / D + EPS_SCALE)
     new_rel = rel_bias - RATE_VECTOR * next_m_rel * lax.rsqrt(square_rel / NB + EPS_SCALE)
@@ -496,7 +993,7 @@
         P(("dp", "seq", "shard"), None),
     )
     return jax.shard_map(
-        local,
+        functools.partial(local, Cube(mesh.shape["dp"])),
         mesh=mesh,
         in_specs=placed,
         out_specs=(

time: 1630 us -> 482 us (0.30)
  waiting for transfers between devices: 859 us -> 0.02 us
  blocking collectives: 471 us -> 0 us
  Pallas kernels: 0 us -> 288 us
  matrix products: 159 us -> 60.3 us
  local copies, waits for them, and re-layouts: 33.4 us -> 54.8 us
    reduce_scatter x8 -> x0, waiting for transfers between devices: 791 us -> none  [the longest x1 148 us: local(): lax.psum_scatter(grad_up_local, ('dp', 'seq', 'shard'), scatter_dimension...]
    pallas_call x0 -> x8, Pallas kernels: none -> 288 us  [the longest x1 80.7 us: gather_groups(): pl.pallas_call(functools.partial(gather_kernel, cube, groups), out_shape=...]
    all_gather x7 -> x0, blocking collectives: 207 us -> none  [the longest x1 42.3 us: local(): lax.all_gather(w_point.astype(bf16), ('dp', 'seq', 'shard'), axis=0, tile...]
    psum x4 -> x0, blocking collectives: 160 us -> none  [the longest x1 40.7 us: local(): lax.psum(jnp.sum(centred * centred, axis=0), ('dp', 'seq', 'shard'))]
    unnamed x1 -> x0, blocking collectives: 104 us -> none
    dot_general x15 -> x0, matrix products: 75.1 us -> none  [the longest x5 35.3 us: orthogonalize_columns(): gram = jnp.dot(iterate, iterate.T, precision=HIGHEST)]
    unnamed x16 -> x0, waiting for transfers between devices: 64.6 us -> none
    another operation x1 -> x31, local copies, waits for them, and re-layouts: 0.15 us -> 18.1 us  [local(): jnp.stack([jnp.sum(grad_conv * glu_wide[tap_idx:tap_idx + row_count], axi...]
  transfers between devices with their start and end apart: 20 -> 6, of which waited for: 11 -> 0; matrix products, arithmetic and copies ran while one was open for 12% -> 11% of each run, Pallas kernels for 0% -> 0%
where the time goes in v1:
time: 482 us; the launch traced here: 473 us
  Pallas kernels  288 us (60%)
  matrix products  60.3 us (13%)
  local copies, waits for them, and re-layouts  54.8 us (11%)
  other arithmetic  53.7 us (11%)
  starting transfers between devices  12.5 us (3%)
    pallas_call x1, Pallas kernels, gather_groups(): pl.pallas_call(functools.partial(gather_kernel, cube, groups), out_shape=...  80.7 us
    pallas_call x1, Pallas kernels, scatter_groups(): pl.pallas_call(functools.partial(scatter_kernel, cube, groups), out_shape...  78.4 us
    pallas_call x1, Pallas kernels, orthogonalize_blocks(): pl.pallas_call(functools.partial(orthogonalize_kernel, cube), out_shape=j...  44.9 us
    pallas_call x3, Pallas kernels, collect(): pl.pallas_call(functools.partial(collect_kernel, cube), out_shape=jax.Sha...  35.7 us
    pallas_call x1, Pallas kernels, restore(): pl.pallas_call(functools.partial(restore_kernel, cube), out_shape=jax.Sha...  28.8 us
    dot_general x24, matrix products, matmul(): return jnp.dot(left, right, preferred_element_type=jnp.float32)  22.2 us
    dot_general x24, matrix products, matmul_right_t(): lax.dot_general(left, right, (((1,), (1,)), ((), ())), preferred_element_...  21.3 us
    pallas_call x1, Pallas kernels, spread(): pl.pallas_call(functools.partial(spread_kernel, cube), out_shape=jax.Shap...  19.2 us
  transfers between devices with their start and end apart: 6, of which 0 were waited for; matrix products, arithmetic and copies ran while one was open for 11% of the time, Pallas kernels for 0%

profile of v1, /device:TPU:31, one launch (start us, length us, event | category | flops | bytes accessed | tf_op | source)
XLA Modules:
  0.0 473.3 jit_solution(8035415655535791851)
XLA Ops:
  10.3 80.7 %gather_weights.1 = (bf16[2,2,2,2,2,16,4224]{6,5,4,3,2,1,0:T(8,128)(2,1)}, bf16[2,2,2,2,2,16,3584]{6,5,4,3,2,1,0:T(8,128)(2,1)}, bf16[2,2,2,2,2,16,4096]{6,5,4,3,2,1,0:T(8,128)(2,1)}) custom-call(bf16[16,4224]{1,0:T(8,128)(2,1)} %pad_maximum_fusion.12.refs_0_, bf16[16,3584]{1,0:T(8,128)(2,1)} %pad_maximum_fusion.14.refs_1_, ...), custom_call_target="tpu_custom_call" | custom-call | tf_op jit(solution)/shard_map/gather_weights/pallas_call | solution.py:153
  96.0 2.9 fusion.392
  125.0 4.5 collective-permute-start.2
  132.6 14.6 %collect_stats.3 = f32[32,8,128]{2,1,0:T(8,128)} custom-call(f32[8,128]{1,0:T(8,128)} %pad_maximum_fusion.24.x_ref), custom_call_target="tpu_custom_call" | custom-call | tf_op jit(solution)/shard_map/collect_stats/pallas_call | solution.py:305
  150.1 2.1 fusion.7
  157.2 2.8 multiply_reduce_fusion.31
  162.0 2.1 convolution_convert_fusion.2
  164.8 10.6 %collect_stats.4 = f32[32,8,128]{2,1,0:T(8,128)} custom-call(f32[8,128]{1,0:T(8,128)} %pad_maximum_fusion.25.x_ref), custom_call_target="tpu_custom_call" | custom-call | tf_op jit(solution)/shard_map/collect_stats/pallas_call | solution.py:305
  179.3 2.9 collective-permute-start.3
  183.8 4.0 pad_maximum_fusion.1.refs_0_
  209.4 2.3 multiply_convert_fusion.4
  212.6 2.4 multiply_reduce_fusion.33
  240.6 2.6 convolution_convert_fusion.6
  245.0 2.8 multiply_reduce_fusion.34
  248.6 2.2 fusion.1
  250.9 2.1 convolution_convert_fusion
  254.9 2.4 fusion.12
  261.3 6.8 %concatenate.299 = bf16[512,40]{0,1:T(8,128)(2,1)} concatenate(bf16[512,1]{0,1:T(2,128)(2,1)S(1)} %stack.181, bf16[512,1]{0,1:T(2,128)(2,1)S(1)} %stack.182, bf16[512,1]{0,1:T(2,128)(2,1)} %stack.183, bf16[512,1]{0,1:T(2,128)(2,1)} %stack.184, bf16[512,1]{0,1:T(2,128)(2,1)} %stack.185, bf16[512,1]{0,1:T(2,128)(2,1)} %stack.186, bf16[512,1]{0,1:T(2,128)(2,1)} %stack.187, ...), dimensions={1} | concatenate | bytes 81920 | tf_op jit(solution)/shard_map/concatenate | solution.py:882
  269.0 3.5 pad_maximum_fusion.refs_2_
  273.0 78.4 %scatter_grads.1 = (f32[16,4096]{1,0:T(8,128)S(1)}, f32[16,3584]{1,0:T(8,128)S(1)}, f32[16,4224]{1,0:T(8,128)S(1)}) custom-call(bf16[2,2,2,2,2,16,4096]{6,5,4,3,2,1,0:T(8,128)(2,1)} %pad_maximum_fusion.1.refs_0_, bf16[2,2,2,2,2,16,3584]{6,5,4,3,2,1,0:T(8,128)(2,1)S(1)} %pad_maximum_fusion.2.refs_1_, bf16[2,2,2,2,2,16,4224]{6,5,4,3,2,1,0:T(8,128)(2,1)} %pad_maximum_fusion.refs_2_), custom_call_target="tpu_custom_call" | custom-call | tf_op jit(solution)/shard_map/scatter_grads/pallas_call | solution.py:272
  353.0 10.6 %collect_stats.5 = f32[32,8,128]{2,1,0:T(8,128)} custom-call(f32[8,128]{1,0:T(8,128)} %pad.37.x_ref), custom_call_target="tpu_custom_call" | custom-call | tf_op jit(solution)/shard_map/collect_stats/pallas_call | solution.py:305
  370.0 19.2 %spread_momentum.1 = f32[32,16,512]{2,1,0:T(8,128)} custom-call(f32[16,11776]{1,0:T(8,128)} %copy-done.28), custom_call_target="tpu_custom_call" | custom-call | tf_op jit(solution)/shard_map/spread_momentum/pallas_call | solution.py:393
  390.5 44.9 %orthogonalize.1 = bf16[512,512]{1,0:T(8,128)(2,1)S(1)} custom-call(f32[512,512]{1,0:T(8,128)S(1)} %bitcast.166), custom_call_target="tpu_custom_call" | custom-call | tf_op jit(solution)/shard_map/orthogonalize/pallas_call | solution.py:538
  436.2 28.8 %restore_rows.1 = bf16[16,11776]{1,0:T(8,128)(2,1)} custom-call(bf16[32,16,512]{2,1,0:T(8,128)(2,1)} %bitcast.167), custom_call_target="tpu_custom_call" | custom-call | tf_op jit(solution)/shard_map/restore_rows/pallas_call | solution.py:464
  (679 shorter events, 132.8 us)
Async XLA Ops:
  0.7 93.0 %copy-start.2 = (f32[1,128,512]{2,1,0:T(8,128)S(1)}, f32[1,128,512]{2,1,0:T(8,128)}, u32[]{:S(2)}) copy-start(f32[1,128,512]{2,1,0:T(8,128)} %param.21) | copy-start | bytes 786436
  101.1 8.5 %collective-permute-start = (bf16[128,1024]{1,0:T(8,128)(2,1)S(1)}, bf16[128,1024]{1,0:T(8,128)(2,1)S(1)}, u32[]{:S(2)}, u32[]{:S(2)}) collective-permute-start(bf16[128,1024]{1,0:T(8,128)(2,1)S(1)} %slice.1116), channel_id=1, source_target_pairs={{0,2},{2,0},{1,3},{3,1},{4,6},{6,4},{5,7},{7,5},{8,10},{10,8},{9,1... | collective-permute-start | bytes 786440 | tf_op jit(solution)/shard_map/ppermute | solution.py:769
  123.7 6.3 %collective-permute-start.1 = (f32[15,512]{1,0:T(8,128)S(1)}, f32[15,512]{1,0:T(8,128)S(1)}, u32[]{:S(2)}, u32[]{:S(2)}) collective-permute-start(f32[15,512]{1,0:T(8,128)S(1)} %get-tuple-element.282), channel_id=1, source_target_pairs={{0,2},{1,3},{4,6},{5,7},{8,10},{9,11},{12,14},{13,15},{16,18},{17,... | collective-permute-start | bytes 92168 | tf_op jit(solution)/shard_map/ppermute | solution.py:563
  125.0 5.0 %collective-permute-start.2 = (f32[15,512]{1,0:T(8,128)S(1)}, f32[15,512]{1,0:T(8,128)S(1)}, u32[]{:S(2)}, u32[]{:S(2)}) collective-permute-start(f32[15,512]{1,0:T(8,128)S(1)} %get-tuple-element.283), channel_id=1, source_target_pairs={{2,0},{3,1},{6,4},{7,5},{10,8},{11,9},{14,12},{15,13},{18,16},{19,... | collective-permute-start | bytes 92168 | tf_op jit(solution)/shard_map/ppermute | solution.py:564
  179.3 29.9 %collective-permute-start.3 = (f32[15,512]{1,0:T(8,128)S(1)}, f32[15,512]{1,0:T(8,128)S(1)}, u32[]{:S(2)}, u32[]{:S(2)}) collective-permute-start(f32[15,512]{1,0:T(8,128)S(1)} %get-tuple-element.280), channel_id=1, source_target_pairs={{2,0},{3,1},{6,4},{7,5},{10,8},{11,9},{14,12},{15,13},{18,16},{19,... | collective-permute-start | bytes 92168 | tf_op jit(solution)/shard_map/ppermute | solution.py:564
  182.2 26.9 %collective-permute-start.4 = (f32[15,512]{1,0:T(8,128)S(1)}, f32[15,512]{1,0:T(8,128)S(1)}, u32[]{:S(2)}, u32[]{:S(2)}) collective-permute-start(f32[15,512]{1,0:T(8,128)S(1)} %get-tuple-element.281), channel_id=1, source_target_pairs={{0,2},{1,3},{4,6},{5,7},{8,10},{9,11},{12,14},{13,15},{16,18},{17,... | collective-permute-start | bytes 92168 | tf_op jit(solution)/shard_map/ppermute | solution.py:563
  224.0 19.2 %collective-permute-start.5 = (f32[128,1024]{0,1:T(8,128)}, f32[128,1024]{0,1:T(8,128)S(1)}, u32[]{:S(2)}, u32[]{:S(2)}) collective-permute-start(f32[128,1024]{0,1:T(8,128)} %constant_dynamic-slice_fusion), channel_id=1, source_target_pairs={{0,2},{2,0},{1,3},{3,1},{4,6},{6,4},{5,7},{7,5},{8,10},{10,8},{9,1... | collective-permute-start | bytes 1572872 | tf_op jit(solution)/shard_map/ppermute | solution.py:858
  272.9 91.8 %copy-start.49 = (f32[16,4096]{1,0:T(8,128)S(1)}, f32[16,4096]{1,0:T(8,128)}, u32[]{:S(2)}) copy-start(f32[16,4096]{1,0:T(8,128)} %param.33) | copy-start | bytes 786436
  273.0 92.6 %copy-start.50 = (f32[16,4096]{1,0:T(8,128)S(1)}, f32[16,4096]{1,0:T(8,128)}, u32[]{:S(2)}) copy-start(f32[16,4096]{1,0:T(8,128)} %param.34) | copy-start | bytes 786436
  352.2 119.3 %copy-start.61 = (f32[16,31]{1,0:T(8,128)}, f32[16,31]{1,0:T(8,128)S(1)}, u32[]{:S(2)}) copy-start(f32[16,31]{1,0:T(8,128)S(1)} %get-tuple-element.239) | copy-start | bytes 5956
  352.3 118.5 %copy-start.124 = (f32[4,8]{1,0:T(4,128)}, f32[4,8]{1,0:T(4,128)S(1)}, u32[]{:S(2)}) copy-start(f32[4,8]{1,0:T(4,128)S(1)} %get-tuple-element.242) | copy-start | bytes 388
  365.6 100.4 %copy-start.34 = (f32[16,4096]{1,0:T(8,128)S(1)}, f32[16,4096]{1,0:T(8,128)}, u32[]{:S(2)}) copy-start(f32[16,4096]{1,0:T(8,128)} %param.23) | copy-start | bytes 786436
  365.6 100.4 %copy-start.35 = (f32[16,4096]{1,0:T(8,128)S(1)}, f32[16,4096]{1,0:T(8,128)}, u32[]{:S(2)}) copy-start(f32[16,4096]{1,0:T(8,128)} %param.24) | copy-start | bytes 786436
  367.8 99.1 %copy-start.44 = (f32[16,1536]{1,0:T(8,128)S(1)}, f32[16,1536]{1,0:T(8,128)}, u32[]{:S(2)}) copy-start(f32[16,1536]{1,0:T(8,128)} %param.25) | copy-start | bytes 294916
  369.1 98.5 %copy-start.54 = (f32[16,512]{1,0:T(8,128)S(1)}, f32[16,512]{1,0:T(8,128)}, u32[]{:S(2)}) copy-start(f32[16,512]{1,0:T(8,128)} %param.28) | copy-start | bytes 98308
  369.1 98.5 %copy-start.55 = (f32[16,512]{1,0:T(8,128)S(1)}, f32[16,512]{1,0:T(8,128)}, u32[]{:S(2)}) copy-start(f32[16,512]{1,0:T(8,128)} %param.26) | copy-start | bytes 98308
  370.0 98.2 %copy-start.51 = (f32[16,1024]{1,0:T(8,128)S(1)}, f32[16,1024]{1,0:T(8,128)}, u32[]{:S(2)}) copy-start(f32[16,1024]{1,0:T(8,128)} %param.27) | copy-start | bytes 196612
  370.0 100.9 %copy-start.158 = (f32[128]{0:T(128)S(1)}, f32[128]{0:T(128)}, u32[]{:S(2)}) copy-start(f32[128]{0:T(128)} %get-tuple-element.227) | copy-start | bytes 1540
  370.0 100.9 %copy-start.157 = (f32[128]{0:T(128)S(1)}, f32[128]{0:T(128)}, u32[]{:S(2)}) copy-start(f32[128]{0:T(128)} %get-tuple-element.229) | copy-start | bytes 1540
  370.0 100.9 %copy-start.123 = (f32[4,8]{1,0:T(4,128)S(1)}, f32[4,8]{1,0:T(4,128)}, u32[]{:S(2)}) copy-start(f32[4,8]{1,0:T(4,128)} %param.31) | copy-start | bytes 388
  370.0 101.5 %copy-start.60 = (f32[16,31]{1,0:T(8,128)S(1)}, f32[16,31]{1,0:T(8,128)}, u32[]{:S(2)}) copy-start(f32[16,31]{1,0:T(8,128)} %param.30) | copy-start | bytes 5956
  370.0 102.1 %copy-start.64 = (f32[512,1]{0,1:T(1,128)S(1)}, f32[512,1]{0,1:T(1,128)}, u32[]{:S(2)}) copy-start(f32[512,1]{0,1:T(1,128)} %copy-done.62) | copy-start | bytes 6148
  370.0 102.1 %copy-start.128 = (f32[128]{0:T(128)S(1)}, f32[128]{0:T(128)}, u32[]{:S(2)}) copy-start(f32[128]{0:T(128)} %copy-done.126) | copy-start | bytes 1540
  370.0 102.0 %copy-start.136 = (f32[128]{0:T(128)S(1)}, f32[128]{0:T(128)}, u32[]{:S(2)}) copy-start(f32[128]{0:T(128)} %copy-done.134) | copy-start | bytes 1540
  (143 other events, 2304.4 us)

commit v2 on v1

--- a/solution.py
+++ b/solution.py
@@ -1,4 +1,5 @@
 import functools
+import types
 
 import jax
 import jax.numpy as jnp
@@ -708,7 +709,682 @@
     )
 
 
-def local(
+def mean_last(value):
+    return jnp.mean(value, axis=-1, keepdims=True)
+
+
+def normalize(field):
+    shifted = field - mean_last(field)
+    inverse = lax.rsqrt(mean_last(shifted * shifted) + EPS_NORM)
+    return shifted * inverse, inverse
+
+
+def norm_grad(grad_out, normed, inverse, gain):
+    scaled = grad_out * gain
+    grad_in = inverse * (scaled - mean_last(scaled) - normed * mean_last(scaled * normed))
+    return grad_in, jnp.sum(grad_out * normed, axis=0, keepdims=True)
+
+
+def row_to_tile(ref, base, row):
+    for k in range(4):
+        ref[base + k : base + k + 1, :] = row[:, 128 * k : 128 * (k + 1)]
+
+
+def tile_to_row(tile):
+    return jnp.concatenate([tile[k : k + 1, :] for k in range(4)], axis=1)
+
+
+def skew(row, count):
+    sub = lax.broadcasted_iota(jnp.int32, (8, 512), 0)
+    block = jnp.broadcast_to(row, (8, 512))
+    for bit in (1, 2, 4):
+        block = jnp.where((sub // bit) % 2 == 1, pltpu.roll(block, bit, 1), block)
+    size = 8
+    while size < count:
+        block = jnp.concatenate([block, pltpu.roll(block, size, 1)], axis=0)
+        size *= 2
+    return block
+
+
+def unskew_sum(grid):
+    size = grid.shape[0] // 2
+    while size >= 8:
+        grid = grid[:size] + pltpu.roll(grid[size:], 512 - size, 1)
+        size //= 2
+    sub = lax.broadcasted_iota(jnp.int32, (8, 512), 0)
+    for bit in (1, 2, 4):
+        grid = jnp.where((sub // bit) % 2 == 1, pltpu.roll(grid, 512 - bit, 1), grid)
+    return jnp.sum(grid, axis=0, keepdims=True)
+
+
+class Gather:
+    def __init__(self, cube, mine, bands, send_sem, recv_sem):
+        self.cube, self.mine, self.bands = cube, mine, bands
+        self.send_sem, self.recv_sem = send_sem, recv_sem
+        self.copies = {}
+
+    def start(self, g, stage):
+        for half in range(2):
+            order = self.cube.gather_orders[half]
+            columns = pl.ds(*halves(self.bands[g].shape[-1])[half])
+            done = order[:stage]
+            index = tuple(
+                slice(None) if k in done else self.mine[k] for k in range(self.cube.digits)
+            )
+            place = self.bands[g].at[index + (slice(None), columns)]
+            copy = remote(
+                place,
+                place,
+                self.send_sem.at[g, half, stage],
+                self.recv_sem.at[g, half, stage],
+                self.cube.partner(order[stage]),
+            )
+            copy.start()
+            self.copies[g, half, stage] = copy
+
+    def arrive(self, g, stage):
+        for half in range(2):
+            self.copies[g, half, stage].wait_recv()
+
+    def advance(self, g, stage):
+        self.arrive(g, stage)
+        self.start(g, stage + 1)
+
+    def finish(self):
+        for copy in self.copies.values():
+            copy.wait_send()
+
+
+class Scatter:
+    def __init__(self, cube, mine, bands, landed, outs, send_sem, recv_sem):
+        self.cube, self.mine, self.bands, self.landed, self.outs = cube, mine, bands, landed, outs
+        self.send_sem, self.recv_sem = send_sem, recv_sem
+        self.copies = {}
+
+    def columns(self, g, half):
+        return pl.ds(*halves(self.bands[g].shape[-1])[half])
+
+    def start(self, g, stage):
+        for half in range(2):
+            order = self.cube.scatter_orders[half]
+            index = []
+            for k in range(self.cube.digits):
+                at = order.index(k)
+                if at > stage:
+                    index.append(slice(None))
+                else:
+                    index.append(1 - self.mine[k] if at == stage else self.mine[k])
+            source = self.bands[g].at[tuple(index) + (slice(None), self.columns(g, half))]
+            copy = remote(
+                source,
+                self.landed[g, half, stage],
+                self.send_sem.at[g, half, stage],
+                self.recv_sem.at[g, half, stage],
+                self.cube.partner(order[stage]),
+            )
+            copy.start()
+            self.copies[g, half, stage] = copy
+
+    def add(self, g, half, stage):
+        order = self.cube.scatter_orders[half]
+        columns = self.columns(g, half)
+        free = [k for k in range(self.cube.digits) if order.index(k) > stage]
+        target, extra = self.bands[g], self.landed[g, half, stage]
+        everything = (slice(None), columns)
+
+        def one(i):
+            digit = {
+                k: lax.rem(i // (1 << (len(free) - 1 - n)), 2) for n, k in enumerate(free)
+            }
+            full = tuple(digit.get(k, self.mine[k]) for k in range(self.cube.digits)) + everything
+            short = tuple(digit[k] for k in free) + (slice(None), slice(None))
+            total = target[full].astype(jnp.float32) + extra[short].astype(jnp.float32)
+            if free:
+                target[full] = total.astype(target.dtype)
+            else:
+                self.outs[g][:, columns] = total
+
+        if free:
+            pl.loop(0, 1 << len(free))(one)
+        else:
+            one(0)
+
+    def advance(self, g, stage):
+        for half in range(2):
+            self.copies[g, half, stage].wait_recv()
+            self.add(g, half, stage)
+        if stage + 1 < self.cube.digits:
+            self.start(g, stage + 1)
+
+    def finish(self):
+        for copy in self.copies.values():
+            copy.wait_send()
+
+
+class Collect:
+    def __init__(self, cube, tile, slots, send_sem, recv_sem):
+        self.cube, self.tile, self.slots = cube, tile, slots
+        self.send_sem, self.recv_sem = send_sem, recv_sem
+
+    def make(self, i):
+        to = self.cube.coords(lax.rem(self.cube.index() + i, self.cube.total))
+        return remote(
+            self.tile, self.slots.at[i], self.send_sem.at[i], self.recv_sem.at[i], to
+        )
+
+    def start(self):
+        pl.loop(1, self.cube.total)(lambda i: self.make(i).start())
+        self.slots[0] = self.tile[...]
+
+    def arrive(self):
+        pl.loop(1, self.cube.total)(lambda i: self.make(i).wait())
+
+    def total(self):
+        result = self.slots[0]
+        for i in range(1, self.cube.total):
+            result = result + self.slots[i]
+        return result
+
+
+SMALL_REL, SMALL_VEC, SMALL_DEPTH = 0, H, H + 7
+SMALL_END = H + 7 + K
+EDGE = 16
+
+
+def step_kernel(cube, rel_rows, r):
+    bf16, f32 = jnp.bfloat16, jnp.float32
+    x_ref, cot_ref, bucket_ref = r.inputs, r.cotangent, r.bucket
+    tokens = x_ref.shape[0]
+    token_total = tokens * cube.total
+    rows = r.small.shape[0]
+    mine = cube.mine()
+    seq = lax.axis_index("seq")
+    early = seq == 0
+    first_row = pl.multiple_of(seq * tokens, tokens)
+    other_row = pl.multiple_of((1 - seq) * tokens, tokens)
+    across = cube.partner(cube.levels)
+    lengths = [ref.shape[-1] for ref in (r.first, r.middle, r.second)]
+    first, middle, second, d_first, d_middle, d_second = (
+        ref.reshape(D, ref.shape[-1])
+        for ref in (r.first, r.middle, r.second, r.d_first, r.d_middle, r.d_second)
+    )
+    a, xh = r.a, r.xh
+
+    barrier = pltpu.get_barrier_semaphore()
+    me = cube.index()
+
+    @pl.loop(1, cube.total)
+    def _(i):
+        peer = cube.coords(lax.rem(me + i, cube.total))
+        pl.semaphore_signal(barrier, inc=1, device_id=peer, device_id_type=MESH)
+
+    own = tuple(mine)
+    r.first[own + (slice(None), slice(0, FF))] = r.w_up[:, :FF].astype(bf16)
+    r.first[own + (slice(None), slice(FF, 2 * FF))] = r.w_down[:, :FF].astype(bf16)
+    r.first[own + (slice(None), slice(2 * FF, lengths[0]))] = r.small[...].astype(bf16)
+    r.middle[own + (slice(None), slice(0, 3 * D))] = r.w_qkv[...].astype(bf16)
+    r.middle[own + (slice(None), slice(3 * D, 4 * D))] = r.w_out[...].astype(bf16)
+    r.middle[own + (slice(None), slice(4 * D, 6 * D))] = r.w_glu[...].astype(bf16)
+    r.middle[own + (slice(None), slice(6 * D, 7 * D))] = r.w_point[...].astype(bf16)
+    r.second[own + (slice(None), slice(0, FF))] = r.w_up[:, FF:].astype(bf16)
+    r.second[own + (slice(None), slice(FF, 2 * FF))] = r.w_down[:, FF:].astype(bf16)
+    pl.semaphore_wait(barrier, cube.total - 1)
+
+    gather = Gather(
+        cube, mine, (r.first, r.middle, r.second), r.g_send, r.g_recv
+    )
+    landed = {
+        (g, half, stage): r.land[(g * 2 + half) * cube.digits + stage]
+        for g in range(3)
+        for half in range(2)
+        for stage in range(cube.digits)
+    }
+    scatter = Scatter(
+        cube,
+        mine,
+        (r.d_second, r.d_middle, r.d_first),
+        landed,
+        (r.share_second, r.share_middle, r.share_first),
+        r.s_send,
+        r.s_recv,
+    )
+
+    gather.start(0, 0)
+    xh0, inv0 = normalize(x_ref[...])
+    xh[0] = xh0
+    rho = lax.broadcasted_iota(jnp.int32, (D, 2 * 256), 0)
+    bucket_of = jnp.where(rho % rows < rel_rows, (rho // rows) * rel_rows + rho % rows, -2)
+    r.hit[...] = (bucket_ref[...] == bucket_of).astype(f32).astype(bf16)
+    gather.advance(0, 0)
+    gather.start(1, 0)
+    gather.advance(0, 1)
+    gather.advance(1, 0)
+    gather.start(2, 0)
+    gather.advance(0, 2)
+    gather.advance(1, 1)
+    gather.advance(2, 0)
+    gather.advance(0, 3)
+    gather.advance(1, 2)
+    gather.advance(2, 1)
+    gather.arrive(0, 4)
+
+    small = r.small_t
+    small[...] = jnp.transpose(first[:, 2 * FF : 2 * FF + 128].astype(f32))
+    gains = [small[SMALL_VEC + i : SMALL_VEC + i + 1, :] for i in range(7)]
+    taps = [small[SMALL_DEPTH + k : SMALL_DEPTH + k + 1, :] for k in range(K)]
+    CH = 512
+
+    def ffn_forward_fused(index, field, normed, weights, u_ref, s_ref):
+        low = (normed * gains[(0, 1, 2, 3)[index]]).astype(bf16)
+        a[index] = low
+        for c in range(0, FF, CH):
+            u = matmul(low, weights[:, c : c + CH])
+            u_ref[:, c : c + CH] = u
+            s_ref[:, c : c + CH] = (u * jax.nn.sigmoid(u)).astype(bf16)
+        return field + 0.5 * matmul_right_t(s_ref[...], weights[:, FF : 2 * FF])
+
+    section1 = ffn_forward_fused(0, x_ref[...], xh[0], first, r.u1, r.s1)
+    r.sec1[...] = section1
+    xh1, inv1 = normalize(section1)
+    xh[1] = xh1
+    a[1] = (xh1 * gains[1]).astype(bf16)
+    gather.advance(1, 3)
+    offsets = matmul(small[0:8, :].astype(bf16), r.hit[...])
+    offsets = jnp.where(
+        early, pltpu.roll(offsets, 257, 1), pltpu.roll(offsets, (tokens + 257) % 512, 1)
+    )
+    for h in range(H):
+        r.bias[h] = skew(offsets[h : h + 1, :], tokens)[:, : 2 * tokens]
+    gather.arrive(1, 4)
+
+    q_ref, kv = r.q, r.kv
+    kv[pl.ds(first_row, tokens), :] = matmul(a[1], middle[:, D : 3 * D]).astype(bf16)
+    kv_copy = remote(
+        kv.at[pl.ds(first_row, tokens)],
+        kv.at[pl.ds(first_row, tokens)],
+        r.kv_send,
+        r.kv_recv,
+        across,
+    )
+    kv_copy.start()
+    gather.advance(2, 2)
+    q_ref[...] = matmul(a[1], middle[:, :D]).astype(bf16)
+    kv_copy.wait_recv()
+    lane = lax.broadcasted_iota(jnp.int32, (1, 128), 1)
+    lane_masks = [(lane // DH == e).astype(f32) for e in range(2)]
+    low_masks = [m.astype(bf16) for m in lane_masks]
+    scale = DH ** (-0.5)
+    for p in range(H // 2):
+        columns = slice(128 * p, 128 * (p + 1))
+        k_pair, v_pair = kv[:, columns], kv[:, D + 128 * p : D + 128 * (p + 1)]
+        merged = None
+        for e in range(2):
+            q_head = q_ref[:, columns] * low_masks[e]
+            scores = matmul_right_t(q_head, k_pair) * scale + r.bias[2 * p + e]
+            shifted = jnp.exp(scores - jnp.max(scores, axis=1, keepdims=True))
+            prob = shifted / jnp.sum(shifted, axis=1, keepdims=True)
+            r.prob[2 * p + e] = prob
+            out = matmul(prob.astype(bf16), v_pair) * lane_masks[e]
+            merged = out if merged is None else merged + out
+        r.att[:, columns] = merged
+    att_low = r.att[...].astype(bf16)
+    r.att_low[...] = att_low
+    gather.advance(2, 3)
+    section2 = r.sec1[...] + matmul(att_low, middle[:, 3 * D : 4 * D])
+    r.sec2[...] = section2
+    xh2, inv2 = normalize(section2)
+    xh[2] = xh2
+    a[2] = (xh2 * gains[2]).astype(bf16)
+    gate_first = matmul(a[2], middle[:, 4 * D : 5 * D])
+    sig = jax.nn.sigmoid(matmul(a[2], middle[:, 5 * D : 6 * D]))
+    r.gate[...] = gate_first
+    r.sig[...] = sig
+    wide = r.wide
+    wide[EDGE : EDGE + tokens, :] = gate_first * sig
+    edge_row = pl.multiple_of(EDGE + (1 - seq) * (tokens - EDGE), EDGE)
+    halo_copy = remote(
+        wide.at[pl.ds(edge_row, EDGE)], r.halo, r.halo_send, r.halo_recv, across
+    )
+    halo_copy.start()
+    zero_edge = jnp.zeros((EDGE, D), f32)
+    halo_copy.wait()
+    wide[0:EDGE, :] = jnp.where(early, zero_edge, r.halo[...])
+    wide[EDGE + tokens :, :] = jnp.where(early, r.halo[...], zero_edge)
+    conv_ref = r.conv
+    for b in range(D // 128):
+        cols = slice(128 * b, 128 * (b + 1))
+        total = jnp.zeros((tokens, 128), f32)
+        for k in range(K):
+            total = total + wide[k + 1 : k + 1 + tokens, cols] * taps[k][:, cols]
+        conv_ref[:, cols] = total
+    conv = conv_ref[...]
+    part_sum = jnp.sum(conv, axis=0, keepdims=True)
+    part_off = conv - part_sum * (1.0 / tokens)
+    part_square = jnp.sum(part_off * part_off, axis=0, keepdims=True)
+    row_to_tile(r.tile1, 0, part_sum)
+    row_to_tile(r.tile1, 4, part_square)
+    stats = Collect(cube, r.tile1, r.slots1, r.c1_send, r.c1_recv)
+    stats.start()
+    gather.arrive(2, 4)
+    stats.arrive()
+    sums = stats.total()
+    mean4 = sums[0:4] * (1.0 / token_total)
+    spread4 = jnp.zeros((4, 128), f32)
+    for i in range(cube.total):
+        off = r.slots1[i][0:4] * (1.0 / tokens) - mean4
+        spread4 = spread4 + off * off
+    var4 = (sums[4:8] + spread4 * tokens) * (1.0 / token_total)
+    mean = tile_to_row(mean4)
+    inv_std = tile_to_row(lax.rsqrt(var4 + EPS_BATCH))
+
+    xb = (conv_ref[...] - mean) * inv_std
+    r.xb[...] = xb
+    bn = xb * gains[5] + gains[6]
+    r.bn[...] = bn
+    sw = (bn * jax.nn.sigmoid(bn)).astype(bf16)
+    r.sw[...] = sw
+    section3 = r.sec2[...] + matmul(sw, middle[:, 6 * D : 7 * D])
+    xh3, inv3 = normalize(section3)
+    xh[3] = xh3
+    section4 = ffn_forward_fused(3, section3, xh3, second, r.u2, r.s2)
+    xh4, inv4 = normalize(section4)
+    r.outputs[...] = xh4 * gains[4]
+
+    sg = r.small_grad
+    sg[...] = jnp.zeros_like(sg)
+    cot = cot_ref[...]
+    d4, sg[SMALL_VEC + 4 : SMALL_VEC + 5, :] = norm_grad(cot, xh4, inv4, gains[4])
+
+    def slope(value):
+        sigma = jax.nn.sigmoid(value)
+        return sigma * (1.0 + value * (1.0 - sigma))
+
+    def ffn_backward_fused(grad, weights, u_ref, du_ref):
+        low = (0.5 * grad).astype(bf16)
+        for c in range(0, FF, CH):
+            act = matmul(low, weights[:, FF + c : FF + c + CH])
+            du_ref[:, c : c + CH] = (act * slope(u_ref[:, c : c + CH])).astype(bf16)
+        return low, matmul_right_t(du_ref[...], weights[:, :FF])
+
+    def weight_grad(left, right_ref, target, start, width):
+        for c in range(0, width, CH):
+            target[:, start + c : start + c + CH] = matmul_left_t(
+                left, right_ref[:, c : c + CH]
+            ).astype(bf16)
+
+    e2, back = ffn_backward_fused(d4, second, r.u2, r.du)
+    r.e_low[...] = e2
+    part, sg[SMALL_VEC + 3 : SMALL_VEC + 4, :] = norm_grad(back, xh[3], inv3, gains[3])
+    d3 = d4 + part
+    r.d[...] = d3
+    e3 = d3.astype(bf16)
+    r.e3[...] = e3
+    dbn = matmul_right_t(e3, middle[:, 6 * D : 7 * D]) * slope(r.bn[...])
+    xb = r.xb[...]
+    sg[SMALL_VEC + 5 : SMALL_VEC + 6, :] = jnp.sum(dbn * xb, axis=0, keepdims=True)
+    sg[SMALL_VEC + 6 : SMALL_VEC + 7, :] = jnp.sum(dbn, axis=0, keepdims=True)
+    dxb = dbn * gains[5]
+    r.dxb[...] = dxb
+    row_to_tile(r.tile2, 0, jnp.sum(dxb, axis=0, keepdims=True))
+    row_to_tile(r.tile2, 4, jnp.sum(dxb * xb, axis=0, keepdims=True))
+    sums2 = Collect(cube, r.tile2, r.slots2, r.c2_send, r.c2_recv)
+    sums2.start()
+    token_edge = pl.multiple_of((1 - seq) * (tokens - EDGE), EDGE)
+    edges = r.edges
+    edges[0:EDGE, :] = r.dxb[pl.ds(token_edge, EDGE), :]
+    edges[EDGE:, :] = r.xb[pl.ds(token_edge, EDGE), :]
+    edge_copy = remote(edges, r.edges_in, r.edge_send, r.edge_recv, across)
+    edge_copy.start()
+
+    weight_grad(r.e_low[...], r.s2, d_second, FF, FF)
+    weight_grad(a[3], r.du, d_second, 0, FF)
+    scatter.start(0, 0)
+    weight_grad(r.sw[...], r.e3, d_middle, 6 * D, D)
+    edge_copy.wait()
+    sums2.arrive()
+    total2 = sums2.total()
+    mean1 = tile_to_row(total2[0:4] * (1.0 / token_total))
+    mean2 = tile_to_row(total2[4:8] * (1.0 / token_total))
+    dwide = r.dwide
+    dwide[EDGE : EDGE + tokens, :] = inv_std * (r.dxb[...] - mean1 - r.xb[...] * mean2)
+    edge = inv_std * (r.edges_in[0:EDGE, :] - mean1 - r.edges_in[EDGE:, :] * mean2)
+    dwide[0:EDGE, :] = jnp.where(early, zero_edge, edge)
+    dwide[EDGE + tokens :, :] = jnp.where(early, edge, zero_edge)
+    dglu_ref = r.conv
+    for b in range(D // 128):
+        cols = slice(128 * b, 128 * (b + 1))
+        total = jnp.zeros((tokens, 128), f32)
+        for k in range(K):
+            total = total + dwide[31 - k : 31 - k + tokens, cols] * taps[k][:, cols]
+        dglu_ref[:, cols] = total
+    dglu, sig = dglu_ref[...], r.sig[...]
+    r.dgates[:, :D] = (dglu * sig).astype(bf16)
+    r.dgates[:, D:] = (dglu * r.gate[...] * sig * (1.0 - sig)).astype(bf16)
+    scatter.advance(0, 0)
+    back = matmul_right_t(r.dgates[...], middle[:, 4 * D : 6 * D])
+    part, sg[SMALL_VEC + 2 : SMALL_VEC + 3, :] = norm_grad(back, xh[2], inv2, gains[2])
+    d2 = r.d[...] + part
+    r.d[...] = d2
+    e1 = d2.astype(bf16)
+    r.e_low[...] = e1
+    dob = matmul_right_t(e1, middle[:, 3 * D : 4 * D]).astype(bf16)
+    r.dob[...] = dob
+
+    off_rows = []
+    give, keep, got = r.give, r.keep, r.got
+    kv_grads = []
+    for p in range(H // 2):
+        columns = slice(128 * p, 128 * (p + 1))
+        k_pair, v_pair = kv[:, columns], kv[:, D + 128 * p : D + 128 * (p + 1)]
+        att_pair = r.att[:, columns]
+        dq = dk = dv = None
+        for e in range(2):
+            h = 2 * p + e
+            dob_head = r.dob[:, columns] * low_masks[e]
+            q_head = q_ref[:, columns] * low_masks[e]
+            delta = jnp.sum(dob_head.astype(f32) * att_pair, axis=1, keepdims=True)
+            prob = r.prob[h]
+            ds = prob * (matmul_right_t(dob_head, v_pair) - delta)
+            ds_low = ds.astype(bf16)
+            dv_head = matmul_left_t(prob.astype(bf16), dob_head)
+            dk_head = matmul_left_t(ds_low, q_head) * scale
+            dq_head = matmul(ds_low, k_pair) * (lane_masks[e] * scale)
+            dv = dv_head if dv is None else dv + dv_head
+            dk = dk_head if dk is None else dk + dk_head
+            dq = dq_head if dq is None else dq + dq_head
+            padded = jnp.concatenate([ds, jnp.zeros((tokens, 512 - 2 * tokens), f32)], axis=1)
+            off_rows.append(unskew_sum(padded))
+        r.dqkv[:, columns] = dq.astype(bf16)
+        for n, value in enumerate((dk, dv)):
+            r.dkv[n] = value
+            give[p, n] = r.dkv[n, pl.ds(other_row, tokens), :].astype(bf16)
+            keep[p, n] = r.dkv[n, pl.ds(first_row, tokens), :]
+        copy = remote(
+            give.at[p], got.at[p], r.dkv_send.at[p], r.dkv_recv.at[p], across
+        )
+        copy.start()
+        kv_grads.append(copy)
+        if p == 1:
+            scatter.advance(0, 1)
+    off = jnp.concatenate(off_rows, axis=0)
+    off = jnp.where(early, pltpu.roll(off, 255, 1), pltpu.roll(off, 255 - tokens, 1))
+    off_high, off_low = split(off)
+    sg[0:8, :] = matmul_right_t(off_high, r.hit[...]) + matmul_right_t(off_low, r.hit[...])
+    weight_grad(r.att_low[...], r.e_low, d_middle, 3 * D, D)
+    weight_grad(a[2], r.dgates, d_middle, 4 * D, 2 * D)
+    for p in range(H // 2):
+        kv_grads[p].wait()
+        for n in range(2):
+            at = D * (n + 1) + 128 * p
+            r.dqkv[:, at : at + 128] = (keep[p, n] + got[p, n].astype(f32)).astype(bf16)
+    scatter.advance(0, 2)
+    weight_grad(a[1], r.dqkv, d_middle, 0, 3 * D)
+    scatter.start(1, 0)
+    back = matmul_right_t(r.dqkv[...], middle[:, : 3 * D])
+    part, sg[SMALL_VEC + 1 : SMALL_VEC + 2, :] = norm_grad(back, xh[1], inv1, gains[1])
+    d1 = r.d[...] + part
+    scatter.advance(0, 3)
+    e0, back = ffn_backward_fused(d1, first, r.u1, r.du)
+    scatter.advance(1, 0)
+    part, sg[SMALL_VEC : SMALL_VEC + 1, :] = norm_grad(back, xh[0], inv0, gains[0])
+    r.input_grad[...] = d1 + part
+    for b in range(D // 128):
+        cols = slice(128 * b, 128 * (b + 1))
+        dconv = dwide[EDGE : EDGE + tokens, cols]
+        for k in range(K):
+            sg[SMALL_DEPTH + k : SMALL_DEPTH + k + 1, cols] = jnp.sum(
+                dconv * wide[k + 1 : k + 1 + tokens, cols], axis=0, keepdims=True
+            )
+    d_first[:, 2 * FF : 2 * FF + 128] = jnp.transpose(sg[...]).astype(bf16)
+    weight_grad(e0, r.s1, d_first, FF, FF)
+    weight_grad(a[0], r.du, d_first, 0, FF)
+    scatter.start(2, 0)
+    scatter.advance(0, 4)
+    scatter.advance(1, 1)
+    scatter.advance(2, 0)
+    scatter.advance(1, 2)
+    scatter.advance(2, 1)
+    scatter.advance(1, 3)
+    scatter.advance(2, 2)
+    scatter.advance(1, 4)
+    scatter.advance(2, 3)
+    scatter.advance(2, 4)
+    gather.finish()
+    scatter.finish()
+    kv_copy.wait_send()
+
+
+def fused_step(cube, inputs, cotangent, weights, small, bucket, rel_rows, collective_id):
+    bf16, f32 = jnp.bfloat16, jnp.float32
+    tokens, rows = inputs.shape[0], small.shape[0]
+    widths = (2 * FF + 128, 7 * D, 2 * FF)
+    lead = (2,) * cube.digits
+    named = dict(
+        inputs=inputs,
+        cotangent=cotangent,
+        w_up=weights[0],
+        w_down=weights[1],
+        w_qkv=weights[2],
+        w_out=weights[3],
+        w_glu=weights[4],
+        w_point=weights[5],
+        small=small,
+        bucket=bucket,
+    )
+    outs = dict(
+        outputs=(tokens, D),
+        input_grad=(tokens, D),
+        share_first=(rows, widths[0]),
+        share_middle=(rows, widths[1]),
+        share_second=(rows, widths[2]),
+    )
+    field = pltpu.VMEM((tokens, D), f32)
+    low = pltpu.VMEM((tokens, D), bf16)
+    wide_low = pltpu.VMEM((tokens, FF), bf16)
+    wide_field = pltpu.VMEM((tokens + 2 * EDGE, D), f32)
+    grid = pltpu.VMEM((H, tokens, 2 * tokens), f32)
+    pairs = pltpu.VMEM((H // 2, 2, tokens, 128), bf16)
+    tile = pltpu.VMEM((8, 128), f32)
+    slots = pltpu.VMEM((cube.total, 8, 128), f32)
+    stages = pltpu.SemaphoreType.DMA((3, 2, cube.digits))
+    everyone = pltpu.SemaphoreType.DMA((cube.total,))
+    single = pltpu.SemaphoreType.DMA
+    bands = [pltpu.VMEM(lead + (rows, w), bf16) for w in widths]
+    land = []
+    for w in (widths[2], widths[1], widths[0]):
+        for half in range(2):
+            for stage in range(cube.digits):
+                shape = (2,) * (cube.digits - 1 - stage) + (rows, halves(w)[half][1])
+                land.append(pltpu.VMEM(shape, bf16))
+    scratch = dict(
+        first=bands[0],
+        middle=bands[1],
+        second=bands[2],
+        d_first=bands[0],
+        d_middle=bands[1],
+        d_second=bands[2],
+        land=tuple(land),
+        sec1=field,
+        sec2=field,
+        att=field,
+        gate=field,
+        sig=field,
+        conv=field,
+        xb=field,
+        bn=field,
+        dxb=field,
+        d=field,
+        q=low,
+        att_low=low,
+        sw=low,
+        e_low=low,
+        e3=low,
+        dob=low,
+        a=pltpu.VMEM((4, tokens, D), bf16),
+        xh=pltpu.VMEM((4, tokens, D), f32),
+        u1=pltpu.VMEM((tokens, FF), f32),
+        u2=pltpu.VMEM((tokens, FF), f32),
+        s1=wide_low,
+        s2=wide_low,
+        du=wide_low,
+        kv=pltpu.VMEM((2 * tokens, 2 * D), bf16),
+        bias=grid,
+        prob=grid,
+        wide=wide_field,
+        dwide=wide_field,
+        halo=pltpu.VMEM((EDGE, D), f32),
+        edges=pltpu.VMEM((2 * EDGE, D), f32),
+        edges_in=pltpu.VMEM((2 * EDGE, D), f32),
+        dgates=pltpu.VMEM((tokens, 2 * D), bf16),
+        dqkv=pltpu.VMEM((tokens, 3 * D), bf16),
+        dkv=pltpu.VMEM((2, 2 * tokens, 128), f32),
+        give=pairs,
+        got=pairs,
+        keep=pltpu.VMEM((H // 2, 2, tokens, 128), f32),
+        hit=pltpu.VMEM((D, 512), bf16),
+        small_t=pltpu.VMEM((128, D), f32),
+        small_grad=pltpu.VMEM((128, D), f32),
+        tile1=tile,
+        tile2=tile,
+        slots1=slots,
+        slots2=slots,
+        g_send=stages,
+        g_recv=stages,
+        s_send=stages,
+        s_recv=stages,
+        c1_send=everyone,
+        c1_recv=everyone,
+        c2_send=everyone,
+        c2_recv=everyone,
+        kv_send=single,
+        kv_recv=single,
+        halo_send=single,
+        halo_recv=single,
+        edge_send=single,
+        edge_recv=single,
+        dkv_send=pltpu.SemaphoreType.DMA((H // 2,)),
+        dkv_recv=pltpu.SemaphoreType.DMA((H // 2,)),
+    )
+
+    def body(*refs):
+        count = len(named) + len(outs)
+        r = dict(zip(list(named) + list(outs), refs[:count])) | dict(zip(scratch, refs[count:]))
+        step_kernel(cube, rel_rows, types.SimpleNamespace(**r))
+
+    return pl.pallas_call(
+        body,
+        out_shape=[jax.ShapeDtypeStruct(shape, f32) for shape in outs.values()],
+        in_specs=[pl.BlockSpec(memory_space=pltpu.VMEM)] * len(named),
+        out_specs=[pl.BlockSpec(memory_space=pltpu.VMEM)] * len(outs),
+        scratch_shapes=list(scratch.values()),
+        compiler_params=pltpu.CompilerParams(
+            collective_id=collective_id, has_side_effects=True, vmem_limit_bytes=60 << 20
+        ),
+        name="block_step",
+    )(*named.values())
+
+
+def unfused_step(
     cube,
     inputs,
     cotangent,
@@ -718,25 +1394,12 @@
     w_out,
     w_glu,
     w_point,
-    vectors,
-    depth_kernel,
-    rel_bias,
+    small,
     bucket_table,
-    m_up,
-    m_down,
-    m_qkv,
-    m_out,
-    m_glu,
-    m_point,
-    m_vectors,
-    m_depth,
-    m_rel,
 ):
     bf16 = jnp.bfloat16
     rows = w_up.shape[0]
-    small = jnp.concatenate([vectors, depth_kernel, rel_bias.reshape(rows, -1)], axis=1)
-    small_count = small.shape[1]
-    small = jnp.pad(small, ((0, 0), (0, 128 - small_count)))
+    rel_rows = NB // cube.total
     shard_groups = (
         jnp.concatenate([w_up[:, :FF], w_down[:, :FF], small], axis=1).astype(bf16),
         jnp.concatenate([w_qkv, w_out, w_glu, w_point], axis=1).astype(bf16),
@@ -749,9 +1412,9 @@
     qkv_w, out_w = middle[:, : 3 * D], middle[:, 3 * D : 4 * D]
     glu_w, point_w = middle[:, 4 * D : 6 * D], middle[:, 6 * D :]
     up_second, down_second = second[:, :FF], second[:, FF:]
-    gains = small_low[:, :7].astype(jnp.float32)
-    kernel = small_low[:, 7 : 7 + K].astype(jnp.float32)
-    rel_low = small_low[:, 7 + K : small_count].reshape(NB, H)
+    gains = small_low[:, SMALL_VEC : SMALL_VEC + 7].astype(jnp.float32)
+    kernel = small_low[:, SMALL_DEPTH : SMALL_DEPTH + K].astype(jnp.float32)
+    rel_low = small_low[:, :H].reshape(cube.total, rows, H)[:, :rel_rows].reshape(NB, H)
     bucket_hit = (bucket_table[:, None] == jnp.arange(NB, dtype=jnp.int32)[None, :]).astype(
         jnp.float32
     )
@@ -879,10 +1542,13 @@
         axis=1,
     )
     grad_rel_local = jnp.dot(bucket_hit.T, offset_grad.T, precision=HIGHEST)
+    rel_padded = jnp.pad(
+        grad_rel_local.reshape(cube.total, rel_rows, H), ((0, 0), (0, rows - rel_rows), (0, 0))
+    )
     small_grads = jnp.concatenate(
-        [grad_vec_local, grad_kernel, grad_rel_local.reshape(D, -1)], axis=1
-    )
-    small_grads = jnp.pad(small_grads, ((0, 0), (0, 128 - small_count)))
+        [rel_padded.reshape(D, H), grad_vec_local, grad_kernel], axis=1
+    )
+    small_grads = jnp.pad(small_grads, ((0, 0), (0, 128 - SMALL_END)))
     lead = (2,) * cube.digits
     grad_groups = [
         jnp.concatenate(group, axis=1).astype(bf16).reshape(lead + (rows, -1))
@@ -893,13 +1559,57 @@
         )
     ]
     share_second, share_middle, share_first = scatter_groups(cube, grad_groups, 3)
+    return outputs, input_grad, share_first, share_middle, share_second
+
+
+def local(
+    cube,
+    inputs,
+    cotangent,
+    w_up,
+    w_down,
+    w_qkv,
+    w_out,
+    w_glu,
+    w_point,
+    vectors,
+    depth_kernel,
+    rel_bias,
+    bucket_table,
+    m_up,
+    m_down,
+    m_qkv,
+    m_out,
+    m_glu,
+    m_point,
+    m_vectors,
+    m_depth,
+    m_rel,
+):
+    bf16 = jnp.bfloat16
+    rows, rel_rows = w_up.shape[0], rel_bias.shape[0]
+    small = jnp.concatenate(
+        [jnp.pad(rel_bias, ((0, rows - rel_rows), (0, 0))), vectors, depth_kernel], axis=1
+    )
+    small = jnp.pad(small, ((0, 0), (0, 128 - SMALL_END)))
+    weights = (w_up, w_down, w_qkv, w_out, w_glu, w_point)
+    if rows % 16 == 0:
+        bucket = jnp.pad(bucket_table, (0, 1), constant_values=-1)[None]
+        outputs, input_grad, share_first, share_middle, share_second = fused_step(
+            cube, inputs[0], cotangent[0], weights, small, bucket, rel_rows, 0
+        )
+    else:
+        outputs, input_grad, share_first, share_middle, share_second = unfused_step(
+            cube, inputs, cotangent, *weights, small, bucket_table
+        )
     grad_up = jnp.concatenate([share_first[:, :FF], share_second[:, :FF]], axis=1)
     grad_down = jnp.concatenate([share_first[:, FF : 2 * FF], share_second[:, FF:]], axis=1)
     grad_qkv, grad_out = share_middle[:, : 3 * D], share_middle[:, 3 * D : 4 * D]
     grad_glu, grad_pnt = share_middle[:, 4 * D : 6 * D], share_middle[:, 6 * D :]
-    grad_vectors = share_first[:, 2 * FF : 2 * FF + 7]
-    grad_depth = share_first[:, 2 * FF + 7 : 2 * FF + 7 + K]
-    grad_rel = share_first[:, 2 * FF + 7 + K : 2 * FF + small_count].reshape(-1, H)
+    share_small = share_first[:, 2 * FF :]
+    grad_vectors = share_small[:, SMALL_VEC : SMALL_VEC + 7]
+    grad_depth = share_small[:, SMALL_DEPTH : SMALL_DEPTH + K]
+    grad_rel = share_small[: rel_bias.shape[0], :H]
     next_m_up = MOMENTUM * m_up + grad_up
     next_m_down = MOMENTUM * m_down + grad_down
     next_m_qkv = MOMENTUM * m_qkv + grad_qkv

time: 482 us -> 315 us (0.65); the launches traced: 473 us -> 314 us
  matrix products: 60.3 us -> 0 us
  local copies, waits for them, and re-layouts: 54.8 us -> 12.9 us
  other arithmetic: 53.7 us -> 14 us
  starting transfers between devices: 12.5 us -> 0 us
    dot_general x74 -> x0, matrix products: 60.3 us -> none  [the longest x24 22.2 us: matmul(): return jnp.dot(left, right, preferred_element_type=jnp.float32)]
    another operation x57 -> x0, local copies, waits for them, and re-layouts: 22.7 us -> none  [the longest x31 18.1 us: local(): jnp.stack([jnp.sum(grad_conv * glu_wide[tap_idx:tap_idx + row_count], axi...]
    pallas_call x3 -> x1, Pallas kernels: 35.7 us -> 18.3 us  [collect(): pl.pallas_call(functools.partial(collect_kernel, cube), out_shape=jax.Sha...]
    pallas_call x2 -> x1, Pallas kernels: 159 us -> 176 us  [fused_step(): pl.pallas_call(body, out_shape=[jax.ShapeDtypeStruct(shape, f32) for shap...]
    concatenate x19 -> x1, other arithmetic: 13.6 us -> 0.08 us  [local(): jnp.concatenate([jnp.pad(rel_bias, ((0, rows - rel_rows), (0, 0))), vecto...]
    ppermute x6 -> x0, starting transfers between devices: 12.5 us -> none  [the longest x2 7.4 us: with_halo(): after = lax.ppermute(first, axis, down)]
    reduce_sum x33 -> x0, other arithmetic: 10.9 us -> none  [the longest x4 2.43 us: local(): jnp.sum(grad_conv * glu_wide[tap_idx:tap_idx + row_count], axis=0)]
    another operation x11 -> x0, other arithmetic: 9.76 us -> none
  transfers between devices with their start and end apart: 6 -> 0, of which waited for: 0 -> 0; matrix products, arithmetic and copies ran while one was open for 11% -> 0% of each run, Pallas kernels for 0% -> 0%
where the time goes in v2:
time: 315 us; the launch traced here: 314 us
  Pallas kernels  286 us (91%)
  other arithmetic  14 us (4%)
  local copies, waits for them, and re-layouts  12.9 us (4%)
    pallas_call x1, Pallas kernels, fused_step(): pl.pallas_call(body, out_shape=[jax.ShapeDtypeStruct(shape, f32) for shap...  176 us
    pallas_call x1, Pallas kernels, orthogonalize_blocks(): pl.pallas_call(functools.partial(orthogonalize_kernel, cube), out_shape=j...  44.9 us
    pallas_call x1, Pallas kernels, restore(): pl.pallas_call(functools.partial(restore_kernel, cube), out_shape=jax.Sha...  28.5 us
    pallas_call x1, Pallas kernels, spread(): pl.pallas_call(functools.partial(spread_kernel, cube), out_shape=jax.Shap...  19.1 us
    pallas_call x1, Pallas kernels, collect(): pl.pallas_call(functools.partial(collect_kernel, cube), out_shape=jax.Sha...  18.3 us
    unnamed x61, local copies, waits for them, and re-layouts  9.95 us

profile of v2, /device:TPU:31, one launch (start us, length us, event | category | flops | bytes accessed | tf_op | source)
XLA Modules:
  0.0 314.1 jit_solution(11541224182863180543)
XLA Ops:
  3.5 175.6 %block_step.1 = (f32[128,512]{1,0:T(8,128)}, f32[128,512]{1,0:T(8,128)}, f32[16,4224]{1,0:T(8,128)}, f32[16,3584]{1,0:T(8,128)}, f32[16,4096]{1,0:T(8,128)}) custom-call(f32[128,512]{1,0:T(8,128)} %bitcast.17, f32[128,512]{1,0:T(8,128)} %bitcast.18, f32[16,4096]{1,0:T(8,128)} %refs_2_.1, f32[16,4096]{1,0:T(8,128)} %refs_3_.1, f32[16,1536]{1,0:T(8,128)} %refs_4_.1, ...), custom_call_target="tpu_custom_call" | custom-call | tf_op jit(solution)/shard_map/block_step/pallas_call | solution.py:1374
  179.1 0.7 copy-done.25
  179.8 1.3 multiply_reduce_fusion.2
  181.0 0.8 multiply_reduce_fusion.1
  181.8 0.7 copy.53
  182.5 0.7 copy.55
  183.2 1.4 multiply_reduce_fusion
  184.5 1.1 fusion.2
  186.4 18.3 %collect_stats.1 = f32[32,8,128]{2,1,0:T(8,128)} custom-call(f32[8,128]{1,0:T(8,128)} %pad.24.x_ref), custom_call_target="tpu_custom_call" | custom-call | tf_op jit(solution)/shard_map/collect_stats/pallas_call | solution.py:306
  204.7 0.9 reduce_sum.39
  205.8 0.7 copy.54
  207.6 0.8 constant_dynamic-update-slice_fusion.5
  208.6 0.8 constant_dynamic-update-slice_fusion.4
  209.8 0.7 constant_dynamic-update-slice_fusion.3
  212.8 0.9 copy-done.2
  213.7 19.1 %spread_momentum.1 = f32[32,16,512]{2,1,0:T(8,128)} custom-call(f32[16,11776]{1,0:T(8,128)} %copy-done.2), custom_call_target="tpu_custom_call" | custom-call | tf_op jit(solution)/shard_map/spread_momentum/pallas_call | solution.py:394
  232.9 1.2 copy-done
  234.1 44.9 %orthogonalize.1 = bf16[512,512]{1,0:T(8,128)(2,1)S(1)} custom-call(f32[512,512]{1,0:T(8,128)S(1)} %bitcast.15), custom_call_target="tpu_custom_call" | custom-call | tf_op jit(solution)/shard_map/orthogonalize/pallas_call | solution.py:539
  279.0 0.8 copy-done.1
  279.8 28.5 %restore_rows.1 = bf16[16,11776]{1,0:T(8,128)(2,1)} custom-call(bf16[32,16,512]{2,1,0:T(8,128)(2,1)} %bitcast.16), custom_call_target="tpu_custom_call" | custom-call | tf_op jit(solution)/shard_map/restore_rows/pallas_call | solution.py:465
  308.3 1.1 convert_element_type.11
  311.4 0.8 slice_subtract_fusion
  312.3 0.7 copy.63
  313.4 0.7 copy.64
  (69 shorter events, 10.1 us)
Async XLA Ops:
  0.7 1.3 copy-start.23
  1.9 0.7 copy-start.18
  1.9 0.7 copy-start.22
  181.0 25.4 %copy-start.20 = (f32[4,8]{1,0:T(4,128)}, f32[4,8]{1,0:T(4,128)S(1)}, u32[]{:S(2)}) copy-start(f32[4,8]{1,0:T(4,128)S(1)} %get-tuple-element.162) | copy-start | bytes 388
  182.5 0.7 copy-start.21
  184.5 22.5 %copy-start.19 = (f32[16,31]{1,0:T(8,128)}, f32[16,31]{1,0:T(8,128)S(1)}, u32[]{:S(2)}) copy-start(f32[16,31]{1,0:T(8,128)S(1)} %get-tuple-element.161) | copy-start | bytes 5956
  185.7 22.0 %copy-start.6 = (f32[16,4096]{1,0:T(8,128)S(1)}, f32[16,4096]{1,0:T(8,128)}, u32[]{:S(2)}) copy-start(f32[16,4096]{1,0:T(8,128)} %param.33) | copy-start | bytes 786436
  207.6 1.0 copy-start.7
  208.6 1.0 copy-start.11
  208.6 1.2 copy-start.14
  209.8 0.8 copy-start.16
  210.6 0.9 copy-start.15
  211.4 0.8 copy-start.17
  212.8 0.9 copy-start.2
  232.9 1.2 copy-start
  279.0 0.8 copy-start.1
  308.3 1.1 copy-start.8
  308.3 1.8 copy-start.12
  308.3 1.8 copy-start.13
  309.4 1.3 copy-start.5
  309.4 1.9 copy-start.4
  310.1 1.3 copy-start.3
  311.4 1.0 copy-start.10
  312.3 1.0 copy-start.9
  (3 other events, 2.1 us)

commit v3 on v2

--- a/solution.py
+++ b/solution.py
@@ -757,38 +757,54 @@
     return jnp.sum(grid, axis=0, keepdims=True)
 
 
+def chunk_pairs(width, pairs):
+    left, start, ranges = width // 128, 0, []
+    for n in range(2 * pairs, 0, -1):
+        count = -(-left // n)
+        ranges.append((start, 128 * count))
+        start, left = start + 128 * count, left - count
+    return [ranges[2 * n : 2 * n + 2] for n in range(pairs)]
+
+
 class Gather:
     def __init__(self, cube, mine, bands, send_sem, recv_sem):
-        self.cube, self.mine, self.bands = cube, mine, bands
+        self.cube, self.mine = cube, mine
+        self.chunks = [(band, pair) for band in bands for pair in chunk_pairs(band.shape[-1], PAIRS)]
         self.send_sem, self.recv_sem = send_sem, recv_sem
         self.copies = {}
-
-    def start(self, g, stage):
+        arrivals = [(GATHER_STEP * n + GATHER_AT[s], n, s) for n in range(len(self.chunks)) for s in range(5)]
+        self.events = [(n, s) for _, n, s in sorted(arrivals)]
+
+    def start(self, n, stage):
+        band, pair = self.chunks[n]
         for half in range(2):
             order = self.cube.gather_orders[half]
-            columns = pl.ds(*halves(self.bands[g].shape[-1])[half])
             done = order[:stage]
             index = tuple(
                 slice(None) if k in done else self.mine[k] for k in range(self.cube.digits)
             )
-            place = self.bands[g].at[index + (slice(None), columns)]
+            place = band.at[index + (slice(None), pl.ds(*pair[half]))]
             copy = remote(
                 place,
                 place,
-                self.send_sem.at[g, half, stage],
-                self.recv_sem.at[g, half, stage],
+                self.send_sem.at[n, half, stage],
+                self.recv_sem.at[n, half, stage],
                 self.cube.partner(order[stage]),
             )
             copy.start()
-            self.copies[g, half, stage] = copy
-
-    def arrive(self, g, stage):
+            self.copies[n, half, stage] = copy
+
+    def advance(self, n, stage):
         for half in range(2):
-            self.copies[g, half, stage].wait_recv()
-
-    def advance(self, g, stage):
-        self.arrive(g, stage)
-        self.start(g, stage + 1)
+            self.copies[n, half, stage].wait_recv()
+        if stage + 1 < self.cube.digits:
+            self.start(n, stage + 1)
+        if stage == 0 and n + 1 < len(self.chunks):
+            self.start(n + 1, 0)
+
+    def run_to(self, n, stage):
+        while (n, stage) in self.events:
+            self.advance(*self.events.pop(0))
 
     def finish(self):
         for copy in self.copies.values():
@@ -797,14 +813,17 @@
 
 class Scatter:
     def __init__(self, cube, mine, bands, landed, outs, send_sem, recv_sem):
-        self.cube, self.mine, self.bands, self.landed, self.outs = cube, mine, bands, landed, outs
+        self.cube, self.mine, self.landed = cube, mine, landed
+        self.chunks = [
+            (band, out, pair)
+            for band, out in zip(bands, outs)
+            for pair in chunk_pairs(band.shape[-1], PAIRS)
+        ]
         self.send_sem, self.recv_sem = send_sem, recv_sem
         self.copies = {}
 
-    def columns(self, g, half):
-        return pl.ds(*halves(self.bands[g].shape[-1])[half])
-
-    def start(self, g, stage):
+    def start(self, n, stage):
+        band, _, pair = self.chunks[n]
         for half in range(2):
             order = self.cube.scatter_orders[half]
             index = []
@@ -814,47 +833,47 @@
                     index.append(slice(None))
                 else:
                     index.append(1 - self.mine[k] if at == stage else self.mine[k])
-            source = self.bands[g].at[tuple(index) + (slice(None), self.columns(g, half))]
             copy = remote(
-                source,
-                self.landed[g, half, stage],
-                self.send_sem.at[g, half, stage],
-                self.recv_sem.at[g, half, stage],
+                band.at[tuple(index) + (slice(None), pl.ds(*pair[half]))],
+                self.landed[(n * 2 + half) * self.cube.digits + stage],
+                self.send_sem.at[n, half, stage],
+                self.recv_sem.at[n, half, stage],
                 self.cube.partner(order[stage]),
             )
             copy.start()
-            self.copies[g, half, stage] = copy
-
-    def add(self, g, half, stage):
+            self.copies[n, half, stage] = copy
+
+    def add(self, n, half, stage):
         order = self.cube.scatter_orders[half]
-        columns = self.columns(g, half)
+        band, out, pair = self.chunks[n]
+        columns = pl.ds(*pair[half])
         free = [k for k in range(self.cube.digits) if order.index(k) > stage]
-        target, extra = self.bands[g], self.landed[g, half, stage]
+        extra = self.landed[(n * 2 + half) * self.cube.digits + stage]
         everything = (slice(None), columns)
 
         def one(i):
             digit = {
-                k: lax.rem(i // (1 << (len(free) - 1 - n)), 2) for n, k in enumerate(free)
+                k: lax.rem(i // (1 << (len(free) - 1 - m)), 2) for m, k in enumerate(free)
             }
             full = tuple(digit.get(k, self.mine[k]) for k in range(self.cube.digits)) + everything
             short = tuple(digit[k] for k in free) + (slice(None), slice(None))
-            total = target[full].astype(jnp.float32) + extra[short].astype(jnp.float32)
+            total = band[full].astype(jnp.float32) + extra[short].astype(jnp.float32)
             if free:
-                target[full] = total.astype(target.dtype)
+                band[full] = total.astype(band.dtype)
             else:
-                self.outs[g][:, columns] = total
+                out[:, columns] = total
 
         if free:
             pl.loop(0, 1 << len(free))(one)
         else:
             one(0)
 
-    def advance(self, g, stage):
+    def advance(self, n, stage):
         for half in range(2):
-            self.copies[g, half, stage].wait_recv()
-            self.add(g, half, stage)
+            self.copies[n, half, stage].wait_recv()
+            self.add(n, half, stage)
         if stage + 1 < self.cube.digits:
-            self.start(g, stage + 1)
+            self.start(n, stage + 1)
 
     def finish(self):
         for copy in self.copies.values():
@@ -886,9 +905,177 @@
         return result
 
 
+class Momenta:
+    def __init__(self, cube, r):
+        self.cube, self.r = cube, r
+        self.me = cube.index()
+        self.repeat = cube.dp_size // 8
+        d = lax.axis_index("dp")
+        self.is_owner = lax.rem(d, self.repeat) == 0
+        self.matrix = d // self.repeat
+        self.quarter = lax.axis_index("seq") * 2 + lax.axis_index("shard")
+        self.owned_index = self.matrix * 4 + self.quarter
+
+    def holds(self, t):
+        return jnp.logical_and(self.is_owner, self.owned_index == t)
+
+    def rows(self, j):
+        r = self.r
+        if j < 4:
+            old, share = ((r.m_up, r.m_down)[j // 2], (r.share_first, r.share_second)[j % 2])
+            return old[:, FF * (j % 2) : FF * (j % 2 + 1)], share[:, FF * (j // 2) : FF * (j // 2 + 1)]
+        start = STARTS[j] - STARTS[4]
+        old = (r.m_qkv, r.m_out, r.m_glu, r.m_point)[j - 4]
+        return old[...], r.share_middle[:, start : start + WIDTHS[j]]
+
+    def copy(self, t):
+        width = WIDTHS[t // 4] // 4
+        r = self.r
+        return remote(
+            r.leaving.at[t, :, pl.ds(0, width)],
+            r.owned.at[self.me, :, pl.ds(0, width)],
+            r.m_send.at[t],
+            r.m_recv.at[self.me],
+            owner_coords(self.cube, t),
+        )
+
+    def send(self, j):
+        old, share = self.rows(j)
+        value = (MOMENTUM * old + share).astype(jnp.bfloat16)
+        width = WIDTHS[j] // 4
+        for q in range(4):
+            t = 4 * j + q
+            part = value[:, width * q : width * (q + 1)]
+            self.r.leaving[t, :, 0:width] = part
+            pl.when(jnp.logical_not(self.holds(t)))(lambda t=t: self.copy(t).start())
+
+            @pl.when(self.holds(t))
+            def _(part=part, width=width):
+                self.r.owned[self.me, :, 0:width] = part
+
+    def receive(self):
+        r, cube = self.r, self.cube
+
+        def go(width):
+            @pl.loop(1, cube.total)
+            def _(i):
+                source = lax.rem(self.me + i, cube.total)
+                place = r.owned.at[source, :, pl.ds(0, width)]
+                remote(
+                    place, place, r.m_send.at[0], r.m_recv.at[source], cube.coords(source)
+                ).wait_recv()
+
+        pl.when(self.is_owner)(lambda: by_matrix(self.matrix, go))
+
+    def back(self, i, width):
+        r, cube = self.r, self.cube
+        to = lax.rem(self.me + i, cube.total)
+        return remote(
+            r.solved.at[to, :, pl.ds(0, width)],
+            r.returned.at[self.owned_index, :, pl.ds(0, width)],
+            r.b_send.at[i],
+            r.b_recv.at[self.owned_index],
+            cube.coords(to),
+        )
+
+    def send_back(self):
+        r = self.r
+
+        def go(width):
+            pl.loop(1, self.cube.total)(lambda i: self.back(i, width).start())
+            r.returned[self.owned_index, :, 0:width] = r.solved[self.me, :, 0:width]
+
+        pl.when(self.is_owner)(lambda: by_matrix(self.matrix, go))
+
+    def receive_back(self):
+        r = self.r
+        for t in range(32):
+            place = r.returned.at[t, :, pl.ds(0, WIDTHS[t // 4] // 4)]
+            copy = remote(
+                place, place, r.b_send.at[0], r.b_recv.at[t], owner_coords(self.cube, t)
+            )
+            pl.when(jnp.logical_not(self.holds(t)))(copy.wait_recv)
+
+    def finish(self):
+        for t in range(32):
+            pl.when(jnp.logical_not(self.holds(t)))(lambda t=t: self.copy(t).wait_send())
+
+        def go(width):
+            pl.loop(1, self.cube.total)(lambda i: self.back(i, width).wait_send())
+
+        pl.when(self.is_owner)(lambda: by_matrix(self.matrix, go))
+
+
+GRAM_SHARES = (
+    ((0, 0), (0, 1), (0, 2), (0, 3), (3, 3)),
+    ((1, 1), (1, 2), (1, 3), (2, 2), (2, 3)),
+)
+
+
+def orthogonalize(cube, r):
+    f32 = jnp.float32
+    core, seq = lax.axis_index("shard"), lax.axis_index("seq")
+    block = r.owned.reshape(D, BLOCK)
+    lines = [slice(128 * i, 128 * (i + 1)) for i in range(4)]
+    for share in range(2):
+        for n, (i, j) in enumerate(GRAM_SHARES[share]):
+            r.packed[share, n] = matmul_right_t(block[lines[i], :], block[lines[j], :])
+    peers = (cube.partner(cube.levels + 1), cube.partner(cube.levels))
+    first = remote(
+        r.packed.at[1 - core], r.packed_in.at[0], r.n_send.at[0], r.n_recv.at[0], peers[0]
+    )
+    first.start()
+    first.wait()
+    r.summed[...] = r.packed[core] + r.packed_in[0]
+    second = remote(r.summed, r.packed_in.at[1], r.n_send.at[1], r.n_recv.at[1], peers[1])
+    second.start()
+    second.wait()
+    r.whole[core] = r.summed[...] + r.packed_in[1]
+    third = remote(
+        r.whole.at[core], r.whole.at[core], r.n_send.at[2], r.n_recv.at[2], peers[0]
+    )
+    third.start()
+    third.wait()
+    for share in range(2):
+        for n, (i, j) in enumerate(GRAM_SHARES[share]):
+            value = r.whole[share, n]
+            r.gram[lines[i], lines[j]] = value
+            if i != j:
+                r.gram[lines[j], lines[i]] = jnp.transpose(value)
+    row = lax.broadcasted_iota(jnp.int32, (D, D), 0)
+    col = lax.broadcasted_iota(jnp.int32, (D, D), 1)
+    eye = row == col
+    gram = r.gram[...]
+    square = jnp.sum(
+        jnp.sum(jnp.where(eye, gram, 0.0), axis=1, keepdims=True), axis=0, keepdims=True
+    )
+    scale = 1.0 / (jnp.sqrt(square) + 1e-07)
+    gram = gram * (scale * scale)
+    value = None
+    for step in range(5):
+        parts = split(gram)
+        mixed = COEF_B * gram + COEF_C * product(parts, parts)
+        mixed = jnp.where(eye, mixed + COEF_A, mixed)
+        high, low = split(mixed)
+        if step == 0:
+            start_high, start_low = split(mixed * scale)
+            value = matmul(start_high, block[...]) + matmul(start_low, block[...])
+        elif step < 4:
+            value = product((high, low), split(value))
+        else:
+            value = matmul(high, value.astype(jnp.bfloat16))
+        if step < 4:
+            gram = product((high, low), split(product((high, low), parts)))
+    r.solved.reshape(D, BLOCK)[...] = value.astype(jnp.bfloat16)
+
+
 SMALL_REL, SMALL_VEC, SMALL_DEPTH = 0, H, H + 7
 SMALL_END = H + 7 + K
 EDGE = 16
+PAIRS = 2
+GATHER_STEP = 8.0
+GATHER_AT = (4.0, 8.0, 13.0, 21.0, 24.0)
+SECOND, MIDDLE, FIRST = 0, PAIRS, 2 * PAIRS
 
 
 def step_kernel(cube, rel_rows, r):
@@ -912,6 +1099,11 @@
 
     barrier = pltpu.get_barrier_semaphore()
     me = cube.index()
+    momenta = Momenta(cube, r)
+
+    @pl.loop(0, cube.total)
+    def _(i):
+        r.owned[i] = jnp.zeros(r.owned.shape[1:], bf16)
 
     @pl.loop(1, cube.total)
     def _(i):
@@ -933,17 +1125,11 @@
     gather = Gather(
         cube, mine, (r.first, r.middle, r.second), r.g_send, r.g_recv
     )
-    landed = {
-        (g, half, stage): r.land[(g * 2 + half) * cube.digits + stage]
-        for g in range(3)
-        for half in range(2)
-        for stage in range(cube.digits)
-    }
     scatter = Scatter(
         cube,
         mine,
         (r.d_second, r.d_middle, r.d_first),
-        landed,
+        r.land,
         (r.share_second, r.share_middle, r.share_first),
         r.s_send,
         r.s_recv,
@@ -955,18 +1141,7 @@
     rho = lax.broadcasted_iota(jnp.int32, (D, 2 * 256), 0)
     bucket_of = jnp.where(rho % rows < rel_rows, (rho // rows) * rel_rows + rho % rows, -2)
     r.hit[...] = (bucket_ref[...] == bucket_of).astype(f32).astype(bf16)
-    gather.advance(0, 0)
-    gather.start(1, 0)
-    gather.advance(0, 1)
-    gather.advance(1, 0)
-    gather.start(2, 0)
-    gather.advance(0, 2)
-    gather.advance(1, 1)
-    gather.advance(2, 0)
-    gather.advance(0, 3)
-    gather.advance(1, 2)
-    gather.advance(2, 1)
-    gather.arrive(0, 4)
+    gather.run_to(PAIRS - 1, 4)
 
     small = r.small_t
     small[...] = jnp.transpose(first[:, 2 * FF : 2 * FF + 128].astype(f32))
@@ -988,14 +1163,13 @@
     xh1, inv1 = normalize(section1)
     xh[1] = xh1
     a[1] = (xh1 * gains[1]).astype(bf16)
-    gather.advance(1, 3)
     offsets = matmul(small[0:8, :].astype(bf16), r.hit[...])
     offsets = jnp.where(
         early, pltpu.roll(offsets, 257, 1), pltpu.roll(offsets, (tokens + 257) % 512, 1)
     )
     for h in range(H):
         r.bias[h] = skew(offsets[h : h + 1, :], tokens)[:, : 2 * tokens]
-    gather.arrive(1, 4)
+    gather.run_to(2 * PAIRS - 1, 4)
 
     q_ref, kv = r.q, r.kv
     kv[pl.ds(first_row, tokens), :] = matmul(a[1], middle[:, D : 3 * D]).astype(bf16)
@@ -1007,7 +1181,6 @@
         across,
     )
     kv_copy.start()
-    gather.advance(2, 2)
     q_ref[...] = matmul(a[1], middle[:, :D]).astype(bf16)
     kv_copy.wait_recv()
     lane = lax.broadcasted_iota(jnp.int32, (1, 128), 1)
@@ -1029,7 +1202,7 @@
         r.att[:, columns] = merged
     att_low = r.att[...].astype(bf16)
     r.att_low[...] = att_low
-    gather.advance(2, 3)
+    gather.run_to(3 * PAIRS - 1, 2)
     section2 = r.sec1[...] + matmul(att_low, middle[:, 3 * D : 4 * D])
     r.sec2[...] = section2
     xh2, inv2 = normalize(section2)
@@ -1065,7 +1238,7 @@
     row_to_tile(r.tile1, 4, part_square)
     stats = Collect(cube, r.tile1, r.slots1, r.c1_send, r.c1_recv)
     stats.start()
-    gather.arrive(2, 4)
+    gather.run_to(3 * PAIRS - 1, 4)
     stats.arrive()
     sums = stats.total()
     mean4 = sums[0:4] * (1.0 / token_total)
@@ -1138,7 +1311,8 @@
 
     weight_grad(r.e_low[...], r.s2, d_second, FF, FF)
     weight_grad(a[3], r.du, d_second, 0, FF)
-    scatter.start(0, 0)
+    for n in range(PAIRS):
+        scatter.start(SECOND + n, 0)
     weight_grad(r.sw[...], r.e3, d_middle, 6 * D, D)
     edge_copy.wait()
     sums2.arrive()
@@ -1160,7 +1334,8 @@
     dglu, sig = dglu_ref[...], r.sig[...]
     r.dgates[:, :D] = (dglu * sig).astype(bf16)
     r.dgates[:, D:] = (dglu * r.gate[...] * sig * (1.0 - sig)).astype(bf16)
-    scatter.advance(0, 0)
+    for n in range(PAIRS):
+        scatter.advance(SECOND + n, 0)
     back = matmul_right_t(r.dgates[...], middle[:, 4 * D : 6 * D])
     part, sg[SMALL_VEC + 2 : SMALL_VEC + 3, :] = norm_grad(back, xh[2], inv2, gains[2])
     d2 = r.d[...] + part
@@ -1205,7 +1380,7 @@
         copy.start()
         kv_grads.append(copy)
         if p == 1:
-            scatter.advance(0, 1)
+            scatter.advance(SECOND, 1)
     off = jnp.concatenate(off_rows, axis=0)
     off = jnp.where(early, pltpu.roll(off, 255, 1), pltpu.roll(off, 255 - tokens, 1))
     off_high, off_low = split(off)
@@ -1217,15 +1392,19 @@
         for n in range(2):
             at = D * (n + 1) + 128 * p
             r.dqkv[:, at : at + 128] = (keep[p, n] + got[p, n].astype(f32)).astype(bf16)
-    scatter.advance(0, 2)
+    scatter.advance(SECOND + 1, 1)
+    scatter.advance(SECOND, 2)
     weight_grad(a[1], r.dqkv, d_middle, 0, 3 * D)
-    scatter.start(1, 0)
+    for n in range(PAIRS):
+        scatter.start(MIDDLE + n, 0)
     back = matmul_right_t(r.dqkv[...], middle[:, : 3 * D])
     part, sg[SMALL_VEC + 1 : SMALL_VEC + 2, :] = norm_grad(back, xh[1], inv1, gains[1])
     d1 = r.d[...] + part
-    scatter.advance(0, 3)
+    scatter.advance(SECOND + 1, 2)
+    scatter.advance(SECOND, 3)
     e0, back = ffn_backward_fused(d1, first, r.u1, r.du)
-    scatter.advance(1, 0)
+    for n in range(PAIRS):
+        scatter.advance(MIDDLE + n, 0)
     part, sg[SMALL_VEC : SMALL_VEC + 1, :] = norm_grad(back, xh[0], inv0, gains[0])
     r.input_grad[...] = d1 + part
     for b in range(D // 128):
@@ -1238,23 +1417,53 @@
     d_first[:, 2 * FF : 2 * FF + 128] = jnp.transpose(sg[...]).astype(bf16)
     weight_grad(e0, r.s1, d_first, FF, FF)
     weight_grad(a[0], r.du, d_first, 0, FF)
-    scatter.start(2, 0)
-    scatter.advance(0, 4)
-    scatter.advance(1, 1)
-    scatter.advance(2, 0)
-    scatter.advance(1, 2)
-    scatter.advance(2, 1)
-    scatter.advance(1, 3)
-    scatter.advance(2, 2)
-    scatter.advance(1, 4)
-    scatter.advance(2, 3)
-    scatter.advance(2, 4)
+    for n in range(PAIRS):
+        scatter.start(FIRST + n, 0)
+    scatter.advance(SECOND + 1, 3)
+    scatter.advance(SECOND, 4)
+    for n in range(PAIRS):
+        scatter.advance(FIRST + n, 0)
+    scatter.advance(MIDDLE, 1)
+    scatter.advance(SECOND + 1, 4)
+    for j in (1, 3):
+        momenta.send(j)
+    scatter.advance(MIDDLE + 1, 1)
+    scatter.advance(MIDDLE, 2)
+    scatter.advance(FIRST, 1)
+    scatter.advance(MIDDLE + 1, 2)
+    scatter.advance(MIDDLE, 3)
+    scatter.advance(FIRST + 1, 1)
+    scatter.advance(MIDDLE, 4)
+    scatter.advance(MIDDLE + 1, 3)
+    scatter.advance(FIRST, 2)
+    scatter.advance(MIDDLE + 1, 4)
+    for j in (4, 5, 6, 7):
+        momenta.send(j)
+    scatter.advance(FIRST + 1, 2)
+    scatter.advance(FIRST, 3)
+    scatter.advance(FIRST + 1, 3)
+    scatter.advance(FIRST, 4)
+    scatter.advance(FIRST + 1, 4)
+    for j in (0, 2):
+        momenta.send(j)
+    next_small = MOMENTUM * r.m_small[...] + r.share_first[:, 2 * FF :]
+    r.tile3[...] = jnp.zeros_like(r.tile3)
+    r.tile3[0:1, :] = jnp.sum(next_small * next_small, axis=0, keepdims=True)
+    squares = Collect(cube, r.tile3, r.slots3, r.c3_send, r.c3_recv)
+    squares.start()
+    momenta.receive()
+    orthogonalize(cube, r)
+    momenta.send_back()
+    squares.arrive()
+    r.squares[...] = squares.total()
+    momenta.receive_back()
+    momenta.finish()
     gather.finish()
     scatter.finish()
     kv_copy.wait_send()
 
 
-def fused_step(cube, inputs, cotangent, weights, small, bucket, rel_rows, collective_id):
+def fused_step(cube, inputs, cotangent, weights, momenta, small, bucket, rel_rows, collective_id):
     bf16, f32 = jnp.bfloat16, jnp.float32
     tokens, rows = inputs.shape[0], small.shape[0]
     widths = (2 * FF + 128, 7 * D, 2 * FF)
@@ -1268,15 +1477,24 @@
         w_out=weights[3],
         w_glu=weights[4],
         w_point=weights[5],
+        m_up=momenta[0],
+        m_down=momenta[1],
+        m_qkv=momenta[2],
+        m_out=momenta[3],
+        m_glu=momenta[4],
+        m_point=momenta[5],
+        m_small=momenta[6],
         small=small,
         bucket=bucket,
     )
     outs = dict(
-        outputs=(tokens, D),
-        input_grad=(tokens, D),
-        share_first=(rows, widths[0]),
-        share_middle=(rows, widths[1]),
-        share_second=(rows, widths[2]),
+        outputs=jax.ShapeDtypeStruct((tokens, D), f32),
+        input_grad=jax.ShapeDtypeStruct((tokens, D), f32),
+        share_first=jax.ShapeDtypeStruct((rows, widths[0]), f32),
+        share_middle=jax.ShapeDtypeStruct((rows, widths[1]), f32),
+        share_second=jax.ShapeDtypeStruct((rows, widths[2]), f32),
+        returned=jax.ShapeDtypeStruct((32, rows, BLOCK), bf16),
+        squares=jax.ShapeDtypeStruct((8, 128), f32),
     )
     field = pltpu.VMEM((tokens, D), f32)
     low = pltpu.VMEM((tokens, D), bf16)
@@ -1286,16 +1504,17 @@
     pairs = pltpu.VMEM((H // 2, 2, tokens, 128), bf16)
     tile = pltpu.VMEM((8, 128), f32)
     slots = pltpu.VMEM((cube.total, 8, 128), f32)
-    stages = pltpu.SemaphoreType.DMA((3, 2, cube.digits))
+    stages = pltpu.SemaphoreType.DMA((3 * PAIRS, 2, cube.digits))
     everyone = pltpu.SemaphoreType.DMA((cube.total,))
     single = pltpu.SemaphoreType.DMA
     bands = [pltpu.VMEM(lead + (rows, w), bf16) for w in widths]
     land = []
     for w in (widths[2], widths[1], widths[0]):
-        for half in range(2):
-            for stage in range(cube.digits):
-                shape = (2,) * (cube.digits - 1 - stage) + (rows, halves(w)[half][1])
-                land.append(pltpu.VMEM(shape, bf16))
+        for pair in chunk_pairs(w, PAIRS):
+            for _, part in pair:
+                for stage in range(cube.digits):
+                    shape = (2,) * (cube.digits - 1 - stage) + (rows, part)
+                    land.append(pltpu.VMEM(shape, bf16))
     scratch = dict(
         first=bands[0],
         middle=bands[1],
@@ -1348,6 +1567,24 @@
         tile2=tile,
         slots1=slots,
         slots2=slots,
+        tile3=tile,
+        slots3=slots,
+        leaving=pltpu.VMEM((32, rows, BLOCK), bf16),
+        owned=pltpu.VMEM((cube.total, rows, BLOCK), bf16),
+        solved=pltpu.VMEM((cube.total, rows, BLOCK), bf16),
+        packed=pltpu.VMEM((2, 5, 128, 128), f32),
+        packed_in=pltpu.VMEM((2, 5, 128, 128), f32),
+        summed=pltpu.VMEM((5, 128, 128), f32),
+        whole=pltpu.VMEM((2, 5, 128, 128), f32),
+        gram=pltpu.VMEM((D, D), f32),
+        m_send=pltpu.SemaphoreType.DMA((32,)),
+        m_recv=everyone,
+        b_send=everyone,
+        b_recv=pltpu.SemaphoreType.DMA((32,)),
+        n_send=pltpu.SemaphoreType.DMA((3,)),
+        n_recv=pltpu.SemaphoreType.DMA((3,)),
+        c3_send=everyone,
+        c3_recv=everyone,
         g_send=stages,
         g_recv=stages,
         s_send=stages,
@@ -1373,7 +1610,7 @@
 
     return pl.pallas_call(
         body,
-        out_shape=[jax.ShapeDtypeStruct(shape, f32) for shape in outs.values()],
+        out_shape=list(outs.values()),
         in_specs=[pl.BlockSpec(memory_space=pltpu.VMEM)] * len(named),
         out_specs=[pl.BlockSpec(memory_space=pltpu.VMEM)] * len(outs),
         scratch_shapes=list(scratch.values()),
@@ -1382,6 +1619,73 @@
         ),
         name="block_step",
     )(*named.values())
+
+
+def finish_kernel(rel_rows, r):
+    f32 = jnp.float32
+    for j in range(8):
+        width = WIDTHS[j]
+        if j < 4:
+            columns = slice(FF * (j % 2), FF * (j % 2 + 1))
+            share = (r.share_first, r.share_second)[j % 2]
+            grad = share[:, FF * (j // 2) : FF * (j // 2 + 1)]
+        else:
+            columns = slice(0, width)
+            start = STARTS[j] - STARTS[4]
+            grad = r.share_middle[:, start : start + width]
+        n = j // 2 if j < 4 else j - 2
+        updated = MOMENTUM * r.moment[n][:, columns] + grad
+        r.grad[n][:, columns] = grad
+        r.next[n][:, columns] = updated
+        solved = [
+            r.returned[4 * j + q, :, 0 : width // 4].astype(f32) for q in range(4)
+        ]
+        r.new[n][:, columns] = r.weight[n][:, columns] - RATE_MATRIX * jnp.concatenate(
+            solved, axis=1
+        )
+    grad = r.share_first[:, 2 * FF :]
+    updated = MOMENTUM * r.m_small[...] + grad
+    lane = lax.broadcasted_iota(jnp.int32, (1, 128), 1)
+    count = jnp.where(lane < SMALL_VEC, float(NB), float(D))
+    scale = lax.rsqrt(r.squares[0:1, :] / count + EPS_SCALE)
+    new = r.small[...] - RATE_VECTOR * updated * scale
+    for value, outs in ((grad, r.grad), (new, r.new), (updated, r.next)):
+        outs[6][...] = value[:, SMALL_VEC : SMALL_VEC + 7]
+        outs[7][...] = value[:, SMALL_DEPTH : SMALL_DEPTH + K]
+        outs[8][...] = value[0:rel_rows, 0:H]
+
+
+def finish_step(shares, returned, squares, weights, momenta, small, shapes, rel_rows):
+    operands = (*shares, returned, squares, *weights, small, *momenta)
+
+    def body(*refs):
+        outs = refs[len(operands) :]
+        finish_kernel(
+            rel_rows,
+            types.SimpleNamespace(
+                share_first=refs[0],
+                share_middle=refs[1],
+                share_second=refs[2],
+                returned=refs[3],
+                squares=refs[4],
+                weight=refs[5:11],
+                small=refs[11],
+                moment=refs[12:18],
+                m_small=refs[18],
+                grad=outs[:9],
+                new=outs[9:18],
+                next=outs[18:],
+            ),
+        )
+
+    return pl.pallas_call(
+        body,
+        out_shape=[jax.ShapeDtypeStruct(s, jnp.float32) for s in shapes * 3],
+        in_specs=[pl.BlockSpec(memory_space=pltpu.VMEM)] * len(operands),
+        out_specs=[pl.BlockSpec(memory_space=pltpu.VMEM)] * 27,
+        compiler_params=pltpu.CompilerParams(vmem_limit_bytes=32 << 20),
+        name="finish_step",
+    )(*operands)
 
 
 def unfused_step(
@@ -1588,20 +1892,25 @@
 ):
     bf16 = jnp.bfloat16
     rows, rel_rows = w_up.shape[0], rel_bias.shape[0]
-    small = jnp.concatenate(
-        [jnp.pad(rel_bias, ((0, rows - rel_rows), (0, 0))), vectors, depth_kernel], axis=1
-    )
-    small = jnp.pad(small, ((0, 0), (0, 128 - SMALL_END)))
+    pack = lambda rel, vec, depth: jnp.pad(
+        jnp.concatenate([jnp.pad(rel, ((0, rows - rel_rows), (0, 0))), vec, depth], axis=1),
+        ((0, 0), (0, 128 - SMALL_END)),
+    )
+    small = pack(rel_bias, vectors, depth_kernel)
     weights = (w_up, w_down, w_qkv, w_out, w_glu, w_point)
-    if rows % 16 == 0:
+    if rows % 16 == 0 and cube.total % 32 == 0:
         bucket = jnp.pad(bucket_table, (0, 1), constant_values=-1)[None]
-        outputs, input_grad, share_first, share_middle, share_second = fused_step(
-            cube, inputs[0], cotangent[0], weights, small, bucket, rel_rows, 0
+        momenta = (m_up, m_down, m_qkv, m_out, m_glu, m_point)
+        momenta += (pack(m_rel, m_vectors, m_depth),)
+        outputs, input_grad, *shares, returned, squares = fused_step(
+            cube, inputs[0], cotangent[0], weights, momenta, small, bucket, rel_rows, 0
         )
-    else:
-        outputs, input_grad, share_first, share_middle, share_second = unfused_step(
-            cube, inputs, cotangent, *weights, small, bucket_table
-        )
+        shapes = [v.shape for v in weights + (vectors, depth_kernel, rel_bias)]
+        rest = finish_step(shares, returned, squares, weights, momenta, small, shapes, rel_rows)
+        return (outputs[None], input_grad[None], *rest)
+    outputs, input_grad, share_first, share_middle, share_second = unfused_step(
+        cube, inputs, cotangent, *weights, small, bucket_table
+    )
     grad_up = jnp.concatenate([share_first[:, :FF], share_second[:, :FF]], axis=1)
     grad_down = jnp.concatenate([share_first[:, FF : 2 * FF], share_second[:, FF:]], axis=1)
     grad_qkv, grad_out = share_middle[:, : 3 * D], share_middle[:, 3 * D : 4 * D]

time: 315 us -> 251 us (0.80)
  Pallas kernels: 286 us -> 236 us
  other arithmetic: 14 us -> 0.15 us
    pallas_call x5 -> x2, Pallas kernels: 286 us -> 236 us  [the longest x1 235 us: fused_step(): pl.pallas_call(body, out_shape=list(outs.values()), in_specs=[pl.BlockSpe...]
    reduce_sum x4 -> x0, other arithmetic: 4.35 us -> none  [the longest x1 1.37 us: local(): jnp.sum(next_m_depth * next_m_depth, axis=0)]
    sub x7 -> x0, other arithmetic: 3.96 us -> none  [the longest x1 0.84 us: local(): new_down = w_down - RATE_MATRIX * mine[:, 2 * FF:4 * FF]]
    unnamed x5 -> x0, other arithmetic: 3.66 us -> none
    unnamed x61 -> x63, local copies, waits for them, and re-layouts: 9.95 us -> 11.1 us
where the time goes in v3:
time: 251 us; the launch traced here: 250 us
  Pallas kernels  236 us (94%)
  local copies, waits for them, and re-layouts  12.9 us (5%)
    pallas_call x1, Pallas kernels, fused_step(): pl.pallas_call(body, out_shape=list(outs.values()), in_specs=[pl.BlockSpe...  235 us
    unnamed x63, local copies, waits for them, and re-layouts  11.1 us

profile of v3, /device:TPU:31, one launch (start us, length us, event | category | flops | bytes accessed | tf_op | source)
XLA Modules:
  0.0 250.4 jit_solution(9006018182514944736)
XLA Ops:
  0.7 0.7 copy-done.25
  1.4 0.6 pad.22
  1.9 0.1 copy.51
  2.0 0.6 copy-done.21
  2.6 0.1 fusion
  2.7 0.6 pad.21.refs_15_.refs_11_
  3.3 0.1 copy-done.24
  3.4 0.1 copy.50
  3.5 0.6 copy-done.22
  4.2 0.6 pad.19.refs_14_.refs_18_
  4.9 235.0 %block_step.1 = (f32[128,512]{1,0:T(8,128)}, f32[128,512]{1,0:T(8,128)}, f32[16,4224]{1,0:T(8,128)}, f32[16,3584]{1,0:T(8,128)}, f32[16,4096]{1,0:T(8,128)}, /*i...) custom-call(f32[128,512]{1,0:T(8,128)} %bitcast.5, f32[128,512]{1,0:T(8,128)} %bitcast.6, f32[16,4096]{1,0:T(8,128)} %refs_5_.3, ...), custom_call_target="tpu_custom_call" | custom-call | tf_op jit(solution)/shard_map/block_step/pallas_call | solution.py:1611
  240.1 0.6 copy-done.17
  240.7 1.0 copy-done.4
  241.7 1.0 copy-done.7
  242.7 0.9 copy-done.10
  243.6 0.9 copy-done.11
  244.5 0.7 copy-done.18
  245.2 1.4 finish_step.1
  246.6 0.7 copy.52
  247.3 0.7 copy.53
  248.0 0.7 copy.54
  248.6 0.7 copy.57
  249.4 0.3 copy-done.19
  249.7 0.7 copy.58
  (46 shorter events, 0.2 us)
Async XLA Ops:
  0.7 1.3 copy-start.23
  1.9 0.7 copy-start.21
  3.4 0.7 copy-start.22
  3.4 0.7 copy-start.27
  4.8 235.2 %copy-start = (f32[16,4096]{1,0:T(8,128)S(1)}, f32[16,4096]{1,0:T(8,128)}, u32[]{:S(2)}) copy-start(f32[16,4096]{1,0:T(8,128)} %refs_5_.3) | copy-start | bytes 786436
  4.8 235.2 %copy-start.1 = (f32[16,4096]{1,0:T(8,128)S(1)}, f32[16,4096]{1,0:T(8,128)}, u32[]{:S(2)}) copy-start(f32[16,4096]{1,0:T(8,128)} %refs_6_.3) | copy-start | bytes 786436
  4.8 235.2 %copy-start.2 = (f32[16,4096]{1,0:T(8,128)S(1)}, f32[16,4096]{1,0:T(8,128)}, u32[]{:S(2)}) copy-start(f32[16,4096]{1,0:T(8,128)} %refs_12_.3) | copy-start | bytes 786436
  4.8 235.2 %copy-start.3 = (f32[16,4096]{1,0:T(8,128)S(1)}, f32[16,4096]{1,0:T(8,128)}, u32[]{:S(2)}) copy-start(f32[16,4096]{1,0:T(8,128)} %refs_13_.3) | copy-start | bytes 786436
  4.8 235.2 %copy-start.5 = (f32[16,1536]{1,0:T(8,128)S(1)}, f32[16,1536]{1,0:T(8,128)}, u32[]{:S(2)}) copy-start(f32[16,1536]{1,0:T(8,128)} %refs_7_.3) | copy-start | bytes 294916
  4.8 235.2 %copy-start.6 = (f32[16,1536]{1,0:T(8,128)S(1)}, f32[16,1536]{1,0:T(8,128)}, u32[]{:S(2)}) copy-start(f32[16,1536]{1,0:T(8,128)} %refs_14_.1) | copy-start | bytes 294916
  4.8 235.2 %copy-start.8 = (f32[16,1024]{1,0:T(8,128)S(1)}, f32[16,1024]{1,0:T(8,128)}, u32[]{:S(2)}) copy-start(f32[16,1024]{1,0:T(8,128)} %refs_9_.3) | copy-start | bytes 196612
  4.8 235.2 %copy-start.9 = (f32[16,1024]{1,0:T(8,128)S(1)}, f32[16,1024]{1,0:T(8,128)}, u32[]{:S(2)}) copy-start(f32[16,1024]{1,0:T(8,128)} %refs_16_.1) | copy-start | bytes 196612
  4.8 235.2 %copy-start.12 = (f32[16,512]{1,0:T(8,128)S(1)}, f32[16,512]{1,0:T(8,128)}, u32[]{:S(2)}) copy-start(f32[16,512]{1,0:T(8,128)} %refs_8_.3) | copy-start | bytes 98308
  4.9 235.2 %copy-start.13 = (f32[16,512]{1,0:T(8,128)S(1)}, f32[16,512]{1,0:T(8,128)}, u32[]{:S(2)}) copy-start(f32[16,512]{1,0:T(8,128)} %refs_10_.3) | copy-start | bytes 98308
  4.9 235.2 %copy-start.14 = (f32[16,512]{1,0:T(8,128)S(1)}, f32[16,512]{1,0:T(8,128)}, u32[]{:S(2)}) copy-start(f32[16,512]{1,0:T(8,128)} %refs_15_.1) | copy-start | bytes 98308
  4.9 235.2 %copy-start.15 = (f32[16,512]{1,0:T(8,128)S(1)}, f32[16,512]{1,0:T(8,128)}, u32[]{:S(2)}) copy-start(f32[16,512]{1,0:T(8,128)} %refs_17_.1) | copy-start | bytes 98308
  239.9 0.7 copy-start.17
  240.0 0.7 copy-start.16
  240.7 1.0 copy-start.4
  241.7 1.0 copy-start.7
  242.7 0.9 copy-start.10
  243.6 0.9 copy-start.11
  245.2 3.4 %copy-start.20 = (f32[128,512]{1,0:T(8,128)S(1)}, f32[128,512]{1,0:T(8,128)}, u32[]{:S(2)}) copy-start(f32[128,512]{1,0:T(8,128)} %get-tuple-element.63) | copy-start | bytes 786436
  248.6 1.0 copy-start.19
  (4 other events, 2.8 us)

commit v4 on v3

--- a/solution.py
+++ b/solution.py
@@ -44,6 +44,7 @@
         high = list(range(self.levels - 1))
         low, seq, core = self.levels - 1, self.levels, self.levels + 1
         self.gather_orders = (high + [low, seq, core], high + [seq, low, core])
+        self.gather_late_orders = ([seq, low] + high + [core], [low, seq] + high + [core])
         self.scatter_orders = tuple(order[::-1] for order in self.gather_orders)
 
     def mine(self):
@@ -757,33 +758,45 @@
     return jnp.sum(grid, axis=0, keepdims=True)
 
 
-def chunk_pairs(width, pairs):
-    left, start, ranges = width // 128, 0, []
-    for n in range(2 * pairs, 0, -1):
-        count = -(-left // n)
-        ranges.append((start, 128 * count))
-        start, left = start + 128 * count, left - count
-    return [ranges[2 * n : 2 * n + 2] for n in range(pairs)]
+def tile_ranges(start, count, parts):
+    ranges = []
+    for n in range(parts, 0, -1):
+        size = -(-count // n)
+        ranges.append((128 * start, 128 * size))
+        start, count = start + size, count - size
+    return ranges
+
+
+def gather_chunks(widths):
+    chunks = []
+    for g in range(2):
+        ranges = tile_ranges(0, widths[g] // 128, 4)
+        chunks += [(g, ranges[0:2], 0), (g, ranges[2:4], 0)]
+    tiles = widths[2] // 128
+    cut = tiles * 2 // 5
+    chunks.append((2, tile_ranges(0, cut, 2), 0))
+    ranges = tile_ranges(cut, tiles - cut, 6)
+    return chunks + [(2, ranges[2 * n : 2 * n + 2], 1) for n in range(3)]
 
 
 class Gather:
     def __init__(self, cube, mine, bands, send_sem, recv_sem):
-        self.cube, self.mine = cube, mine
-        self.chunks = [(band, pair) for band in bands for pair in chunk_pairs(band.shape[-1], PAIRS)]
+        self.cube, self.mine, self.bands = cube, mine, bands
+        self.chunks = gather_chunks([band.shape[-1] for band in bands])
         self.send_sem, self.recv_sem = send_sem, recv_sem
         self.copies = {}
-        arrivals = [(GATHER_STEP * n + GATHER_AT[s], n, s) for n in range(len(self.chunks)) for s in range(5)]
-        self.events = [(n, s) for _, n, s in sorted(arrivals)]
+        self.events = list(GATHER_EVENTS)
+        self.last = cube.digits - 1
 
     def start(self, n, stage):
-        band, pair = self.chunks[n]
+        g, pair, kind = self.chunks[n]
         for half in range(2):
-            order = self.cube.gather_orders[half]
+            order = (self.cube.gather_orders, self.cube.gather_late_orders)[kind][half]
             done = order[:stage]
             index = tuple(
                 slice(None) if k in done else self.mine[k] for k in range(self.cube.digits)
             )
-            place = band.at[index + (slice(None), pl.ds(*pair[half]))]
+            place = self.bands[g].at[index + (slice(None), pl.ds(*pair[half]))]
             copy = remote(
                 place,
                 place,
@@ -794,13 +807,17 @@
             copy.start()
             self.copies[n, half, stage] = copy
 
+    def begin(self):
+        self.start(0, 0)
+        self.start(5, 0)
+
     def advance(self, n, stage):
         for half in range(2):
             self.copies[n, half, stage].wait_recv()
-        if stage + 1 < self.cube.digits:
+        if stage < self.last and (n, stage + 1) not in GATHER_HELD:
             self.start(n, stage + 1)
-        if stage == 0 and n + 1 < len(self.chunks):
-            self.start(n + 1, 0)
+        for other in GATHER_AFTER.get((n, stage), ()):
+            self.start(*other)
 
     def run_to(self, n, stage):
         while (n, stage) in self.events:
@@ -814,11 +831,7 @@
 class Scatter:
     def __init__(self, cube, mine, bands, landed, outs, send_sem, recv_sem):
         self.cube, self.mine, self.landed = cube, mine, landed
-        self.chunks = [
-            (band, out, pair)
-            for band, out in zip(bands, outs)
-            for pair in chunk_pairs(band.shape[-1], PAIRS)
-        ]
+        self.chunks = [(bands[g], outs[g], pair) for g, pair in SCATTER_CHUNKS]
         self.send_sem, self.recv_sem = send_sem, recv_sem
         self.copies = {}
 
@@ -905,6 +918,32 @@
         return result
 
 
+def share_columns(j):
+    place = j // 2 if j % 2 else 1 - j // 2
+    return slice(FF * place, FF * (place + 1))
+
+
+def matrix_of(d):
+    return sum(jnp.where(d == OWNER_PLACES[i], i, 0) for i in range(8))
+
+
+def pack_small(target, turn, rel, vec, depth):
+    rows = target.shape[0]
+    turn[...] = jnp.zeros_like(turn)
+    turn[0:7, 0:rows] = vec[...]
+    target[...] = jnp.zeros_like(target)
+    target[0 : rel.shape[0], SMALL_REL : SMALL_REL + H] = rel[...]
+    target[:, SMALL_VEC : SMALL_VEC + 7] = jnp.transpose(turn[...])[0:rows, 0:7]
+    target[:, SMALL_DEPTH : SMALL_DEPTH + K] = depth[...]
+
+
+OWNER_PLACES = (2, 3, 5, 4, 0, 1, 7, 6)
+
+
+def owner_place(cube, t):
+    return (OWNER_PLACES[t // 4] * (cube.dp_size // 8), t // 2 % 2, t % 2)
+
+
 class Momenta:
     def __init__(self, cube, r):
         self.cube, self.r = cube, r
@@ -912,7 +951,7 @@
         self.repeat = cube.dp_size // 8
         d = lax.axis_index("dp")
         self.is_owner = lax.rem(d, self.repeat) == 0
-        self.matrix = d // self.repeat
+        self.matrix = matrix_of(d // self.repeat)
         self.quarter = lax.axis_index("seq") * 2 + lax.axis_index("shard")
         self.owned_index = self.matrix * 4 + self.quarter
 
@@ -923,7 +962,7 @@
         r = self.r
         if j < 4:
             old, share = ((r.m_up, r.m_down)[j // 2], (r.share_first, r.share_second)[j % 2])
-            return old[:, FF * (j % 2) : FF * (j % 2 + 1)], share[:, FF * (j // 2) : FF * (j // 2 + 1)]
+            return old[:, FF * (j % 2) : FF * (j % 2 + 1)], share[:, share_columns(j)]
         start = STARTS[j] - STARTS[4]
         old = (r.m_qkv, r.m_out, r.m_glu, r.m_point)[j - 4]
         return old[...], r.share_middle[:, start : start + WIDTHS[j]]
@@ -936,7 +975,7 @@
             r.owned.at[self.me, :, pl.ds(0, width)],
             r.m_send.at[t],
             r.m_recv.at[self.me],
-            owner_coords(self.cube, t),
+            owner_place(self.cube, t),
         )
 
     def send(self, j):
@@ -978,12 +1017,20 @@
             cube.coords(to),
         )
 
+    def keep(self, width):
+        r = self.r
+        return pltpu.make_async_copy(
+            r.solved.at[self.me, :, pl.ds(0, width)],
+            r.returned.at[self.owned_index, :, pl.ds(0, width)],
+            r.k_sem,
+        )
+
     def send_back(self):
         r = self.r
 
         def go(width):
             pl.loop(1, self.cube.total)(lambda i: self.back(i, width).start())
-            r.returned[self.owned_index, :, 0:width] = r.solved[self.me, :, 0:width]
+            self.keep(width).start()
 
         pl.when(self.is_owner)(lambda: by_matrix(self.matrix, go))
 
@@ -992,7 +1039,7 @@
         for t in range(32):
             place = r.returned.at[t, :, pl.ds(0, WIDTHS[t // 4] // 4)]
             copy = remote(
-                place, place, r.b_send.at[0], r.b_recv.at[t], owner_coords(self.cube, t)
+                place, place, r.b_send.at[0], r.b_recv.at[t], owner_place(self.cube, t)
             )
             pl.when(jnp.logical_not(self.holds(t)))(copy.wait_recv)
 
@@ -1002,8 +1049,18 @@
 
         def go(width):
             pl.loop(1, self.cube.total)(lambda i: self.back(i, width).wait_send())
+            self.keep(width).wait()
 
         pl.when(self.is_owner)(lambda: by_matrix(self.matrix, go))
+
+
+def symmetric_product(left, right):
+    half = D // 2
+    (lh, ll), (rh, rl) = left, right
+    top = product((lh[:half], ll[:half]), right)
+    corner = product((lh[half:], ll[half:]), (rh[:, half:], rl[:, half:]))
+    low = jnp.concatenate([jnp.transpose(top[:, half:]), corner], axis=1)
+    return jnp.concatenate([top, low], axis=0)
 
 
 GRAM_SHARES = (
@@ -1054,7 +1111,7 @@
     value = None
     for step in range(5):
         parts = split(gram)
-        mixed = COEF_B * gram + COEF_C * product(parts, parts)
+        mixed = COEF_B * gram + COEF_C * symmetric_product(parts, parts)
         mixed = jnp.where(eye, mixed + COEF_A, mixed)
         high, low = split(mixed)
         if step == 0:
@@ -1065,25 +1122,59 @@
         else:
             value = matmul(high, value.astype(jnp.bfloat16))
         if step < 4:
-            gram = product((high, low), split(product((high, low), parts)))
+            inner = symmetric_product((high, low), parts)
+            gram = symmetric_product((high, low), split(inner))
     r.solved.reshape(D, BLOCK)[...] = value.astype(jnp.bfloat16)
 
 
 SMALL_REL, SMALL_VEC, SMALL_DEPTH = 0, H, H + 7
 SMALL_END = H + 7 + K
 EDGE = 16
-PAIRS = 2
-GATHER_STEP = 8.0
-GATHER_AT = (4.0, 8.0, 13.0, 21.0, 24.0)
-SECOND, MIDDLE, FIRST = 0, PAIRS, 2 * PAIRS
-
-
-def step_kernel(cube, rel_rows, r):
+GATHER_EVENTS = (
+    ((5, 0), (5, 1), (0, 0), (6, 0), (6, 1), (7, 0), (0, 1), (1, 0), (7, 1), (0, 2))
+    + ((1, 1), (2, 0), (2, 1), (3, 0), (1, 2), (0, 3), (3, 1), (4, 0), (0, 4), (4, 1))
+    + ((2, 2), (5, 2), (3, 2), (1, 3), (1, 4), (6, 2), (5, 3), (4, 2), (2, 3), (5, 4))
+    + ((2, 4), (3, 3), (7, 2), (6, 3), (3, 4), (6, 4), (4, 3), (7, 3), (4, 4), (7, 4))
+)
+SCATTER_EVENTS = (
+    ((0, 3), (4, 0), (2, 1), (5, 0), (0, 4), (1, 2), (1, 3), (3, 1), (1, 4), (4, 1), (2, 2))
+    + ((2, 3), (5, 1), (2, 4), (3, 2), (4, 2), (3, 3), (5, 2), (4, 3), (3, 4), (5, 3))
+    + ((4, 4), (5, 4))
+)
+SCATTER_STORES = ((), (4,), (), (3,), (), (2,))
+EARLY_LOADS = tuple("w_up w_down w_qkv w_out".split()) + tuple("w_glu w_point rel vec".split())
+EARLY_LOADS += tuple("depth m_rel m_vec m_depth".split())
+SCATTER_MATRICES = ((3,), (1,), (), (4, 5, 6, 7), (2,), (0,))
+GATHER_HELD = ((5, 2), (6, 2), (7, 2))
+GATHER_AFTER = {
+    (0, 0): [(1, 0)],
+    (1, 0): [(2, 0)],
+    (2, 0): [(3, 0)],
+    (3, 0): [(4, 0)],
+    (5, 0): [(6, 0)],
+    (6, 0): [(7, 0)],
+    (4, 1): [(5, 2)],
+    (5, 2): [(6, 2)],
+    (6, 2): [(7, 2)],
+}
+FIRST_READY, MIDDLE_READY, SECOND_READY = (1, 4), (3, 4), (7, 4)
+SCATTER_CHUNKS = (
+    (0, tile_ranges(16, 16, 2)),
+    (0, tile_ranges(0, 16, 2)),
+    (1, tile_ranges(12, 16, 2)),
+    (1, tile_ranges(0, 12, 2)),
+    (2, tile_ranges(0, 16, 2)),
+    (2, tile_ranges(16, 17, 2)),
+)
+
+
+def step_kernel(cube, r):
     bf16, f32 = jnp.bfloat16, jnp.float32
     x_ref, cot_ref, bucket_ref = r.inputs, r.cotangent, r.bucket
     tokens = x_ref.shape[0]
     token_total = tokens * cube.total
-    rows = r.small.shape[0]
+    rows = r.w_up.shape[0]
+    rel_rows = r.rel.shape[0]
     mine = cube.mine()
     seq = lax.axis_index("seq")
     early = seq == 0
@@ -1100,19 +1191,22 @@
     barrier = pltpu.get_barrier_semaphore()
     me = cube.index()
     momenta = Momenta(cube, r)
-
-    @pl.loop(0, cube.total)
-    def _(i):
-        r.owned[i] = jnp.zeros(r.owned.shape[1:], bf16)
+    for load in r.loads.values():
+        load.start()
+    r.owned[...] = jnp.zeros_like(r.owned)
 
     @pl.loop(1, cube.total)
     def _(i):
         peer = cube.coords(lax.rem(me + i, cube.total))
         pl.semaphore_signal(barrier, inc=1, device_id=peer, device_id_type=MESH)
 
+    for name in EARLY_LOADS:
+        r.loads[name].wait()
+    pack_small(r.small, r.turn, r.rel, r.vec, r.depth)
+    pack_small(r.m_small, r.turn, r.m_rel, r.m_vec, r.m_depth)
     own = tuple(mine)
-    r.first[own + (slice(None), slice(0, FF))] = r.w_up[:, :FF].astype(bf16)
-    r.first[own + (slice(None), slice(FF, 2 * FF))] = r.w_down[:, :FF].astype(bf16)
+    r.first[own + (slice(None), slice(FF, 2 * FF))] = r.w_up[:, :FF].astype(bf16)
+    r.first[own + (slice(None), slice(0, FF))] = r.w_down[:, :FF].astype(bf16)
     r.first[own + (slice(None), slice(2 * FF, lengths[0]))] = r.small[...].astype(bf16)
     r.middle[own + (slice(None), slice(0, 3 * D))] = r.w_qkv[...].astype(bf16)
     r.middle[own + (slice(None), slice(3 * D, 4 * D))] = r.w_out[...].astype(bf16)
@@ -1135,13 +1229,17 @@
         r.s_recv,
     )
 
-    gather.start(0, 0)
+    gather.begin()
+    for name in [name for name in r.loads if name not in EARLY_LOADS]:
+        r.loads[name].wait()
     xh0, inv0 = normalize(x_ref[...])
     xh[0] = xh0
-    rho = lax.broadcasted_iota(jnp.int32, (D, 2 * 256), 0)
+    rho = lax.broadcasted_iota(jnp.int32, (D, bucket_ref.shape[1]), 0)
     bucket_of = jnp.where(rho % rows < rel_rows, (rho // rows) * rel_rows + rho % rows, -2)
-    r.hit[...] = (bucket_ref[...] == bucket_of).astype(f32).astype(bf16)
-    gather.run_to(PAIRS - 1, 4)
+    r.hit[...] = jnp.zeros_like(r.hit)
+    offset_count = bucket_ref.shape[1]
+    r.hit[:, 0:offset_count] = (bucket_ref[...] == bucket_of).astype(f32).astype(bf16)
+    gather.run_to(*FIRST_READY)
 
     small = r.small_t
     small[...] = jnp.transpose(first[:, 2 * FF : 2 * FF + 128].astype(f32))
@@ -1149,16 +1247,18 @@
     taps = [small[SMALL_DEPTH + k : SMALL_DEPTH + k + 1, :] for k in range(K)]
     CH = 512
 
-    def ffn_forward_fused(index, field, normed, weights, u_ref, s_ref):
+    def ffn_forward_fused(index, field, normed, up, down, u_ref, s_ref):
         low = (normed * gains[(0, 1, 2, 3)[index]]).astype(bf16)
         a[index] = low
         for c in range(0, FF, CH):
-            u = matmul(low, weights[:, c : c + CH])
+            u = matmul(low, up[:, c : c + CH])
             u_ref[:, c : c + CH] = u
             s_ref[:, c : c + CH] = (u * jax.nn.sigmoid(u)).astype(bf16)
-        return field + 0.5 * matmul_right_t(s_ref[...], weights[:, FF : 2 * FF])
-
-    section1 = ffn_forward_fused(0, x_ref[...], xh[0], first, r.u1, r.s1)
+        return field + 0.5 * matmul_right_t(s_ref[...], down[...])
+
+    down1, up1 = first.at[:, pl.ds(0, FF)], first.at[:, pl.ds(FF, FF)]
+    up2, down2 = second.at[:, pl.ds(0, FF)], second.at[:, pl.ds(FF, FF)]
+    section1 = ffn_forward_fused(0, x_ref[...], xh[0], up1, down1, r.u1, r.s1)
     r.sec1[...] = section1
     xh1, inv1 = normalize(section1)
     xh[1] = xh1
@@ -1169,7 +1269,7 @@
     )
     for h in range(H):
         r.bias[h] = skew(offsets[h : h + 1, :], tokens)[:, : 2 * tokens]
-    gather.run_to(2 * PAIRS - 1, 4)
+    gather.run_to(*MIDDLE_READY)
 
     q_ref, kv = r.q, r.kv
     kv[pl.ds(first_row, tokens), :] = matmul(a[1], middle[:, D : 3 * D]).astype(bf16)
@@ -1182,6 +1282,7 @@
     )
     kv_copy.start()
     q_ref[...] = matmul(a[1], middle[:, :D]).astype(bf16)
+    gather.run_to(4, 3)
     kv_copy.wait_recv()
     lane = lax.broadcasted_iota(jnp.int32, (1, 128), 1)
     lane_masks = [(lane // DH == e).astype(f32) for e in range(2)]
@@ -1200,9 +1301,9 @@
             out = matmul(prob.astype(bf16), v_pair) * lane_masks[e]
             merged = out if merged is None else merged + out
         r.att[:, columns] = merged
+    gather.run_to(*SECOND_READY)
     att_low = r.att[...].astype(bf16)
     r.att_low[...] = att_low
-    gather.run_to(3 * PAIRS - 1, 2)
     section2 = r.sec1[...] + matmul(att_low, middle[:, 3 * D : 4 * D])
     r.sec2[...] = section2
     xh2, inv2 = normalize(section2)
@@ -1238,7 +1339,6 @@
     row_to_tile(r.tile1, 4, part_square)
     stats = Collect(cube, r.tile1, r.slots1, r.c1_send, r.c1_recv)
     stats.start()
-    gather.run_to(3 * PAIRS - 1, 4)
     stats.arrive()
     sums = stats.total()
     mean4 = sums[0:4] * (1.0 / token_total)
@@ -1259,9 +1359,10 @@
     section3 = r.sec2[...] + matmul(sw, middle[:, 6 * D : 7 * D])
     xh3, inv3 = normalize(section3)
     xh[3] = xh3
-    section4 = ffn_forward_fused(3, section3, xh3, second, r.u2, r.s2)
+    section4 = ffn_forward_fused(3, section3, xh3, up2, down2, r.u2, r.s2)
     xh4, inv4 = normalize(section4)
     r.outputs[...] = xh4 * gains[4]
+    r.stores[0].start()
 
     sg = r.small_grad
     sg[...] = jnp.zeros_like(sg)
@@ -1272,12 +1373,10 @@
         sigma = jax.nn.sigmoid(value)
         return sigma * (1.0 + value * (1.0 - sigma))
 
-    def ffn_backward_fused(grad, weights, u_ref, du_ref):
-        low = (0.5 * grad).astype(bf16)
+    def slopes(low, down, u_ref, du_ref):
         for c in range(0, FF, CH):
-            act = matmul(low, weights[:, FF + c : FF + c + CH])
+            act = matmul(low, down[:, c : c + CH])
             du_ref[:, c : c + CH] = (act * slope(u_ref[:, c : c + CH])).astype(bf16)
-        return low, matmul_right_t(du_ref[...], weights[:, :FF])
 
     def weight_grad(left, right_ref, target, start, width):
         for c in range(0, width, CH):
@@ -1285,8 +1384,9 @@
                 left, right_ref[:, c : c + CH]
             ).astype(bf16)
 
-    e2, back = ffn_backward_fused(d4, second, r.u2, r.du)
-    r.e_low[...] = e2
+    r.e_low[...] = (0.5 * d4).astype(bf16)
+    slopes(r.e_low[...], down2, r.u2, r.du)
+    back = matmul_right_t(r.du[...], up2[...])
     part, sg[SMALL_VEC + 3 : SMALL_VEC + 4, :] = norm_grad(back, xh[3], inv3, gains[3])
     d3 = d4 + part
     r.d[...] = d3
@@ -1310,9 +1410,9 @@
     edge_copy.start()
 
     weight_grad(r.e_low[...], r.s2, d_second, FF, FF)
+    scatter.start(0, 0)
     weight_grad(a[3], r.du, d_second, 0, FF)
-    for n in range(PAIRS):
-        scatter.start(SECOND + n, 0)
+    scatter.start(1, 0)
     weight_grad(r.sw[...], r.e3, d_middle, 6 * D, D)
     edge_copy.wait()
     sums2.arrive()
@@ -1334,8 +1434,7 @@
     dglu, sig = dglu_ref[...], r.sig[...]
     r.dgates[:, :D] = (dglu * sig).astype(bf16)
     r.dgates[:, D:] = (dglu * r.gate[...] * sig * (1.0 - sig)).astype(bf16)
-    for n in range(PAIRS):
-        scatter.advance(SECOND + n, 0)
+    scatter.advance(0, 0)
     back = matmul_right_t(r.dgates[...], middle[:, 4 * D : 6 * D])
     part, sg[SMALL_VEC + 2 : SMALL_VEC + 3, :] = norm_grad(back, xh[2], inv2, gains[2])
     d2 = r.d[...] + part
@@ -1344,6 +1443,10 @@
     r.e_low[...] = e1
     dob = matmul_right_t(e1, middle[:, 3 * D : 4 * D]).astype(bf16)
     r.dob[...] = dob
+    weight_grad(r.att_low[...], r.e_low, d_middle, 3 * D, D)
+    weight_grad(a[2], r.dgates, d_middle, 4 * D, 2 * D)
+    scatter.advance(1, 0)
+    scatter.start(2, 0)
 
     off_rows = []
     give, keep, got = r.give, r.keep, r.got
@@ -1379,34 +1482,12 @@
         )
         copy.start()
         kv_grads.append(copy)
-        if p == 1:
-            scatter.advance(SECOND, 1)
+        if p == 2:
+            scatter.advance(0, 1)
     off = jnp.concatenate(off_rows, axis=0)
     off = jnp.where(early, pltpu.roll(off, 255, 1), pltpu.roll(off, 255 - tokens, 1))
     off_high, off_low = split(off)
     sg[0:8, :] = matmul_right_t(off_high, r.hit[...]) + matmul_right_t(off_low, r.hit[...])
-    weight_grad(r.att_low[...], r.e_low, d_middle, 3 * D, D)
-    weight_grad(a[2], r.dgates, d_middle, 4 * D, 2 * D)
-    for p in range(H // 2):
-        kv_grads[p].wait()
-        for n in range(2):
-            at = D * (n + 1) + 128 * p
-            r.dqkv[:, at : at + 128] = (keep[p, n] + got[p, n].astype(f32)).astype(bf16)
-    scatter.advance(SECOND + 1, 1)
-    scatter.advance(SECOND, 2)
-    weight_grad(a[1], r.dqkv, d_middle, 0, 3 * D)
-    for n in range(PAIRS):
-        scatter.start(MIDDLE + n, 0)
-    back = matmul_right_t(r.dqkv[...], middle[:, : 3 * D])
-    part, sg[SMALL_VEC + 1 : SMALL_VEC + 2, :] = norm_grad(back, xh[1], inv1, gains[1])
-    d1 = r.d[...] + part
-    scatter.advance(SECOND + 1, 2)
-    scatter.advance(SECOND, 3)
-    e0, back = ffn_backward_fused(d1, first, r.u1, r.du)
-    for n in range(PAIRS):
-        scatter.advance(MIDDLE + n, 0)
-    part, sg[SMALL_VEC : SMALL_VEC + 1, :] = norm_grad(back, xh[0], inv0, gains[0])
-    r.input_grad[...] = d1 + part
     for b in range(D // 128):
         cols = slice(128 * b, 128 * (b + 1))
         dconv = dwide[EDGE : EDGE + tokens, cols]
@@ -1414,38 +1495,38 @@
             sg[SMALL_DEPTH + k : SMALL_DEPTH + k + 1, cols] = jnp.sum(
                 dconv * wide[k + 1 : k + 1 + tokens, cols], axis=0, keepdims=True
             )
+    scatter.advance(2, 0)
+    for p in range(H // 2):
+        kv_grads[p].wait()
+        for n in range(2):
+            at = D * (n + 1) + 128 * p
+            r.dqkv[:, at : at + 128] = (keep[p, n] + got[p, n].astype(f32)).astype(bf16)
+    back = matmul_right_t(r.dqkv[...], middle[:, : 3 * D])
+    part, sg[SMALL_VEC + 1 : SMALL_VEC + 2, :] = norm_grad(back, xh[1], inv1, gains[1])
+    d1 = r.d[...] + part
+    e0 = (0.5 * d1).astype(bf16)
+    weight_grad(a[1], r.dqkv, d_middle, 0, 3 * D)
+    scatter.start(3, 0)
+    scatter.advance(1, 1)
+    weight_grad(e0, r.s1, d_first, 0, FF)
+    scatter.start(4, 0)
+    scatter.advance(0, 2)
+    slopes(e0, down1, r.u1, r.du)
+    back = matmul_right_t(r.du[...], up1[...])
+    part, sg[SMALL_VEC : SMALL_VEC + 1, :] = norm_grad(back, xh[0], inv0, gains[0])
+    r.input_grad[...] = d1 + part
+    r.stores[1].start()
+    scatter.advance(3, 0)
     d_first[:, 2 * FF : 2 * FF + 128] = jnp.transpose(sg[...]).astype(bf16)
-    weight_grad(e0, r.s1, d_first, FF, FF)
-    weight_grad(a[0], r.du, d_first, 0, FF)
-    for n in range(PAIRS):
-        scatter.start(FIRST + n, 0)
-    scatter.advance(SECOND + 1, 3)
-    scatter.advance(SECOND, 4)
-    for n in range(PAIRS):
-        scatter.advance(FIRST + n, 0)
-    scatter.advance(MIDDLE, 1)
-    scatter.advance(SECOND + 1, 4)
-    for j in (1, 3):
-        momenta.send(j)
-    scatter.advance(MIDDLE + 1, 1)
-    scatter.advance(MIDDLE, 2)
-    scatter.advance(FIRST, 1)
-    scatter.advance(MIDDLE + 1, 2)
-    scatter.advance(MIDDLE, 3)
-    scatter.advance(FIRST + 1, 1)
-    scatter.advance(MIDDLE, 4)
-    scatter.advance(MIDDLE + 1, 3)
-    scatter.advance(FIRST, 2)
-    scatter.advance(MIDDLE + 1, 4)
-    for j in (4, 5, 6, 7):
-        momenta.send(j)
-    scatter.advance(FIRST + 1, 2)
-    scatter.advance(FIRST, 3)
-    scatter.advance(FIRST + 1, 3)
-    scatter.advance(FIRST, 4)
-    scatter.advance(FIRST + 1, 4)
-    for j in (0, 2):
-        momenta.send(j)
+    weight_grad(a[0], r.du, d_first, FF, FF)
+    scatter.start(5, 0)
+    for n, stage in SCATTER_EVENTS:
+        scatter.advance(n, stage)
+        if stage == scatter.cube.digits - 1:
+            for j in SCATTER_MATRICES[n]:
+                momenta.send(j)
+            for store in SCATTER_STORES[n]:
+                r.stores[store].start()
     next_small = MOMENTUM * r.m_small[...] + r.share_first[:, 2 * FF :]
     r.tile3[...] = jnp.zeros_like(r.tile3)
     r.tile3[0:1, :] = jnp.sum(next_small * next_small, axis=0, keepdims=True)
@@ -1456,16 +1537,19 @@
     momenta.send_back()
     squares.arrive()
     r.squares[...] = squares.total()
+    r.stores[5].start()
     momenta.receive_back()
     momenta.finish()
     gather.finish()
     scatter.finish()
+    for store in r.stores:
+        store.wait()
     kv_copy.wait_send()
 
 
-def fused_step(cube, inputs, cotangent, weights, momenta, small, bucket, rel_rows, collective_id):
+def fused_step(cube, inputs, cotangent, weights, momenta, bucket, collective_id):
     bf16, f32 = jnp.bfloat16, jnp.float32
-    tokens, rows = inputs.shape[0], small.shape[0]
+    tokens, rows = inputs.shape[0], weights[0].shape[0]
     widths = (2 * FF + 128, 7 * D, 2 * FF)
     lead = (2,) * cube.digits
     named = dict(
@@ -1477,14 +1561,18 @@
         w_out=weights[3],
         w_glu=weights[4],
         w_point=weights[5],
+        vec=weights[6],
+        depth=weights[7],
+        rel=weights[8],
         m_up=momenta[0],
         m_down=momenta[1],
         m_qkv=momenta[2],
         m_out=momenta[3],
         m_glu=momenta[4],
         m_point=momenta[5],
-        m_small=momenta[6],
-        small=small,
+        m_vec=momenta[6],
+        m_depth=momenta[7],
+        m_rel=momenta[8],
         bucket=bucket,
     )
     outs = dict(
@@ -1504,17 +1592,17 @@
     pairs = pltpu.VMEM((H // 2, 2, tokens, 128), bf16)
     tile = pltpu.VMEM((8, 128), f32)
     slots = pltpu.VMEM((cube.total, 8, 128), f32)
-    stages = pltpu.SemaphoreType.DMA((3 * PAIRS, 2, cube.digits))
+    stages = pltpu.SemaphoreType.DMA((6, 2, cube.digits))
+    gather_stages = pltpu.SemaphoreType.DMA((8, 2, cube.digits))
     everyone = pltpu.SemaphoreType.DMA((cube.total,))
     single = pltpu.SemaphoreType.DMA
     bands = [pltpu.VMEM(lead + (rows, w), bf16) for w in widths]
     land = []
-    for w in (widths[2], widths[1], widths[0]):
-        for pair in chunk_pairs(w, PAIRS):
-            for _, part in pair:
-                for stage in range(cube.digits):
-                    shape = (2,) * (cube.digits - 1 - stage) + (rows, part)
-                    land.append(pltpu.VMEM(shape, bf16))
+    for _, pair in SCATTER_CHUNKS:
+        for _, part in pair:
+            for stage in range(cube.digits):
+                shape = (2,) * (cube.digits - 1 - stage) + (rows, part)
+                land.append(pltpu.VMEM(shape, bf16))
     scratch = dict(
         first=bands[0],
         middle=bands[1],
@@ -1560,6 +1648,9 @@
         give=pairs,
         got=pairs,
         keep=pltpu.VMEM((H // 2, 2, tokens, 128), f32),
+        small=pltpu.VMEM((rows, 128), f32),
+        m_small=pltpu.VMEM((rows, 128), f32),
+        turn=pltpu.VMEM((128, 128), f32),
         hit=pltpu.VMEM((D, 512), bf16),
         small_t=pltpu.VMEM((128, D), f32),
         small_grad=pltpu.VMEM((128, D), f32),
@@ -1585,8 +1676,8 @@
         n_recv=pltpu.SemaphoreType.DMA((3,)),
         c3_send=everyone,
         c3_recv=everyone,
-        g_send=stages,
-        g_recv=stages,
+        g_send=gather_stages,
+        g_recv=gather_stages,
         s_send=stages,
         s_recv=stages,
         c1_send=everyone,
@@ -1603,16 +1694,36 @@
         dkv_recv=pltpu.SemaphoreType.DMA((H // 2,)),
     )
 
+    kept = [n for n in outs if n != "returned"]
+    buffers = dict({n: pltpu.VMEM(v.shape, v.dtype) for n, v in named.items()})
+    buffers |= {n: pltpu.VMEM(outs[n].shape, outs[n].dtype) for n in kept}
+    scratch |= buffers
+    scratch |= dict(
+        load_sem=pltpu.SemaphoreType.DMA((len(named),)),
+        store_sem=pltpu.SemaphoreType.DMA((len(kept),)),
+        k_sem=single,
+    )
+
     def body(*refs):
         count = len(named) + len(outs)
-        r = dict(zip(list(named) + list(outs), refs[:count])) | dict(zip(scratch, refs[count:]))
-        step_kernel(cube, rel_rows, types.SimpleNamespace(**r))
+        far = dict(zip(list(named) + list(outs), refs[:count]))
+        near = dict(zip(scratch, refs[count:]))
+        near["returned"] = far["returned"]
+        near["loads"] = {
+            name: pltpu.make_async_copy(far[name], near[name], near["load_sem"].at[n])
+            for n, name in enumerate(named)
+        }
+        near["stores"] = [
+            pltpu.make_async_copy(near[name], far[name], near["store_sem"].at[n])
+            for n, name in enumerate(kept)
+        ]
+        step_kernel(cube, types.SimpleNamespace(**near))
 
     return pl.pallas_call(
         body,
         out_shape=list(outs.values()),
-        in_specs=[pl.BlockSpec(memory_space=pltpu.VMEM)] * len(named),
-        out_specs=[pl.BlockSpec(memory_space=pltpu.VMEM)] * len(outs),
+        in_specs=[pl.BlockSpec(memory_space=pl.ANY)] * len(named),
+        out_specs=[pl.BlockSpec(memory_space=pl.ANY)] * len(outs),
         scratch_shapes=list(scratch.values()),
         compiler_params=pltpu.CompilerParams(
             collective_id=collective_id, has_side_effects=True, vmem_limit_bytes=60 << 20
@@ -1621,69 +1732,96 @@
     )(*named.values())
 
 
-def finish_kernel(rel_rows, r):
+def finish_kernel(r):
     f32 = jnp.float32
+    for load in r.loads:
+        load.start()
+    for load in r.loads:
+        load.wait()
+    pack_small(r.small, r.turn, r.weight[8], r.weight[6], r.weight[7])
+    pack_small(r.m_small, r.turn, r.moment[8], r.moment[6], r.moment[7])
+    share_first, share_middle, share_second, returned, squares = r.results
     for j in range(8):
         width = WIDTHS[j]
         if j < 4:
             columns = slice(FF * (j % 2), FF * (j % 2 + 1))
-            share = (r.share_first, r.share_second)[j % 2]
-            grad = share[:, FF * (j // 2) : FF * (j // 2 + 1)]
+            grad = (share_first, share_second)[j % 2][:, share_columns(j)]
         else:
             columns = slice(0, width)
             start = STARTS[j] - STARTS[4]
-            grad = r.share_middle[:, start : start + width]
+            grad = share_middle[:, start : start + width]
         n = j // 2 if j < 4 else j - 2
         updated = MOMENTUM * r.moment[n][:, columns] + grad
         r.grad[n][:, columns] = grad
         r.next[n][:, columns] = updated
-        solved = [
-            r.returned[4 * j + q, :, 0 : width // 4].astype(f32) for q in range(4)
-        ]
+        solved = [returned[4 * j + q, :, 0 : width // 4].astype(f32) for q in range(4)]
         r.new[n][:, columns] = r.weight[n][:, columns] - RATE_MATRIX * jnp.concatenate(
             solved, axis=1
         )
-    grad = r.share_first[:, 2 * FF :]
+    grad = share_first[:, 2 * FF :]
     updated = MOMENTUM * r.m_small[...] + grad
     lane = lax.broadcasted_iota(jnp.int32, (1, 128), 1)
     count = jnp.where(lane < SMALL_VEC, float(NB), float(D))
-    scale = lax.rsqrt(r.squares[0:1, :] / count + EPS_SCALE)
+    scale = lax.rsqrt(squares[0:1, :] / count + EPS_SCALE)
     new = r.small[...] - RATE_VECTOR * updated * scale
+    rows, rel_rows = r.small.shape[0], r.weight[8].shape[0]
     for value, outs in ((grad, r.grad), (new, r.new), (updated, r.next)):
-        outs[6][...] = value[:, SMALL_VEC : SMALL_VEC + 7]
+        r.turn[...] = jnp.zeros_like(r.turn)
+        r.turn[0:rows, :] = value
+        turned = jnp.transpose(r.turn[...])
+        outs[6][...] = turned[SMALL_VEC : SMALL_VEC + 7, 0:rows]
         outs[7][...] = value[:, SMALL_DEPTH : SMALL_DEPTH + K]
-        outs[8][...] = value[0:rel_rows, 0:H]
-
-
-def finish_step(shares, returned, squares, weights, momenta, small, shapes, rel_rows):
-    operands = (*shares, returned, squares, *weights, small, *momenta)
+        outs[8][...] = value[0:rel_rows, SMALL_REL : SMALL_REL + H]
+    for store in r.stores:
+        store.start()
+    for store in r.stores:
+        store.wait()
+
+
+def finish_step(fields, shares, returned, squares, weights, momenta):
+    sources = (*shares, returned, squares, *weights, *momenta)
+    operands = sources + tuple(fields)
+    rows, count = weights[0].shape[0], len(sources)
+    shapes = [jax.ShapeDtypeStruct(v.shape, v.dtype) for v in weights] * 3
+    shapes += [jax.ShapeDtypeStruct(v.shape, v.dtype) for v in fields]
 
     def body(*refs):
-        outs = refs[len(operands) :]
+        ins, refs = refs[: len(operands)], refs[len(operands) :]
+        outs, refs = refs[: len(shapes)], refs[len(shapes) :]
+        near, refs = refs[: count + 2], refs[count + 2 :]
+        made, refs = refs[:27], refs[27:]
+        small, m_small, turn, sem = refs
+        pairs = list(zip(ins, near)) + list(zip(made + near[-2:], outs))
+        moves = [pltpu.make_async_copy(a, b, sem.at[n]) for n, (a, b) in enumerate(pairs)]
         finish_kernel(
-            rel_rows,
             types.SimpleNamespace(
-                share_first=refs[0],
-                share_middle=refs[1],
-                share_second=refs[2],
-                returned=refs[3],
-                squares=refs[4],
-                weight=refs[5:11],
-                small=refs[11],
-                moment=refs[12:18],
-                m_small=refs[18],
-                grad=outs[:9],
-                new=outs[9:18],
-                next=outs[18:],
+                loads=moves[: count + 2],
+                stores=moves[count + 2 :],
+                results=near[:5],
+                weight=near[5:14],
+                moment=near[14:23],
+                grad=made[:9],
+                new=made[9:18],
+                next=made[18:27],
+                small=small,
+                m_small=m_small,
+                turn=turn,
             ),
         )
 
     return pl.pallas_call(
         body,
-        out_shape=[jax.ShapeDtypeStruct(s, jnp.float32) for s in shapes * 3],
-        in_specs=[pl.BlockSpec(memory_space=pltpu.VMEM)] * len(operands),
-        out_specs=[pl.BlockSpec(memory_space=pltpu.VMEM)] * 27,
-        compiler_params=pltpu.CompilerParams(vmem_limit_bytes=32 << 20),
+        out_shape=shapes,
+        in_specs=[pl.BlockSpec(memory_space=pl.ANY)] * len(operands),
+        out_specs=[pl.BlockSpec(memory_space=pl.ANY)] * len(shapes),
+        scratch_shapes=[pltpu.VMEM(v.shape, v.dtype) for v in list(operands) + shapes[:27]]
+        + [
+            pltpu.VMEM((rows, 128), jnp.float32),
+            pltpu.VMEM((rows, 128), jnp.float32),
+            pltpu.VMEM((128, 128), jnp.float32),
+            pltpu.SemaphoreType.DMA((len(operands) + len(shapes),)),
+        ],
+        compiler_params=pltpu.CompilerParams(vmem_limit_bytes=60 << 20),
         name="finish_step",
     )(*operands)
 
@@ -1898,15 +2036,18 @@
     )
     small = pack(rel_bias, vectors, depth_kernel)
     weights = (w_up, w_down, w_qkv, w_out, w_glu, w_point)
-    if rows % 16 == 0 and cube.total % 32 == 0:
-        bucket = jnp.pad(bucket_table, (0, 1), constant_values=-1)[None]
-        momenta = (m_up, m_down, m_qkv, m_out, m_glu, m_point)
-        momenta += (pack(m_rel, m_vectors, m_depth),)
+    if rows % 16 == 0 and cube.total == 32:
+        bucket = bucket_table[None]
+        weights += (vectors.T, depth_kernel, rel_bias)
+        momenta = (m_up, m_down, m_qkv, m_out, m_glu, m_point, m_vectors.T, m_depth, m_rel)
         outputs, input_grad, *shares, returned, squares = fused_step(
-            cube, inputs[0], cotangent[0], weights, momenta, small, bucket, rel_rows, 0
+            cube, inputs[0], cotangent[0], weights, momenta, bucket, 0
         )
-        shapes = [v.shape for v in weights + (vectors, depth_kernel, rel_bias)]
-        rest = finish_step(shares, returned, squares, weights, momenta, small, shapes, rel_rows)
+        *rest, outputs, input_grad = finish_step(
+            (outputs, input_grad), shares, returned, squares, weights, momenta
+        )
+        for n in (6, 15, 24):
+            rest[n] = rest[n].T
         return (outputs[None], input_grad[None], *rest)
     outputs, input_grad, share_first, share_middle, share_second = unfused_step(
         cube, inputs, cotangent, *weights, small, bucket_table

time: 251 us -> 214 us (0.85)
  Pallas kernels: 236 us -> 213 us
  local copies, waits for them, and re-layouts: 12.9 us -> 0 us
    pallas_call x1, Pallas kernels: 235 us -> 209 us  [fused_step(): pl.pallas_call(body, out_shape=list(outs.values()), in_specs=[pl.BlockSpe...]
    unnamed x63 -> x0, local copies, waits for them, and re-layouts: 11.1 us -> none
    pallas_call x1, Pallas kernels: 1.41 us -> 4.28 us  [finish_step(): pl.pallas_call(body, out_shape=shapes, in_specs=[pl.BlockSpec(memory_spac...]
where the time goes in v4:
time: 214 us
  Pallas kernels  213 us (100%)
    pallas_call x1, Pallas kernels, fused_step(): pl.pallas_call(body, out_shape=list(outs.values()), in_specs=[pl.BlockSpe...  209 us
    pallas_call x1, Pallas kernels, finish_step(): pl.pallas_call(body, out_shape=shapes, in_specs=[pl.BlockSpec(memory_spac...  4.28 us

profile of v4, /device:TPU:31, one launch (start us, length us, event | category | flops | bytes accessed | tf_op | source)
XLA Modules:
  0.0 213.7 jit_solution(5258528551070955437)
XLA Ops:
  0.7 208.5 %block_step.1 = (f32[128,512]{1,0:T(8,128)}, f32[128,512]{1,0:T(8,128)}, f32[16,4224]{1,0:T(8,128)}, f32[16,3584]{1,0:T(8,128)}, f32[16,4096]{1,0:T(8,128)}, /*i...) custom-call(f32[128,512]{1,0:T(8,128)} %bitcast.10, f32[128,512]{1,0:T(8,128)} %bitcast.11, f32[16,4096]{1,0:T(8,128)} %refs_5_.3, ...), custom_call_target="tpu_custom_call" | custom-call | tf_op jit(solution)/shard_map/block_step/pallas_call | solution.py:1722
  209.2 4.3 %finish_step.1 = (f32[16,4096]{1,0:T(8,128)}, f32[16,4096]{1,0:T(8,128)}, f32[16,1536]{1,0:T(8,128)}, f32[16,512]{1,0:T(8,128)}, f32[16,1024]{1,0:T(8,128)}, /*i...) custom-call(f32[16,4224]{1,0:T(8,128)} %get-tuple-element.65.refs_0_, ...), custom_call_target="tpu_custom_call" | custom-call | tf_op jit(solution)/shard_map/finish_step/pallas_call | solution.py:1812

commit v5 on v4

--- a/solution.py
+++ b/solution.py
@@ -46,6 +46,8 @@
         self.gather_orders = (high + [low, seq, core], high + [seq, low, core])
         self.gather_late_orders = ([seq, low] + high + [core], [low, seq] + high + [core])
         self.scatter_orders = tuple(order[::-1] for order in self.gather_orders)
+        self.scatter_high_orders = tuple(order[::-1] for order in self.gather_late_orders)
+        self.scatter_low_orders = ([core, low, seq] + high[::-1],) * 2
 
     def mine(self):
         d = lax.axis_index("dp")
@@ -831,14 +833,16 @@
 class Scatter:
     def __init__(self, cube, mine, bands, landed, outs, send_sem, recv_sem):
         self.cube, self.mine, self.landed = cube, mine, landed
-        self.chunks = [(bands[g], outs[g], pair) for g, pair in SCATTER_CHUNKS]
+        kinds = (cube.scatter_orders, cube.scatter_high_orders, cube.scatter_low_orders)
+        self.chunks = [(bands[g], outs[g], pair) for g, pair, _ in SCATTER_CHUNKS]
+        self.orders = [kinds[kind] for _, _, kind in SCATTER_CHUNKS]
         self.send_sem, self.recv_sem = send_sem, recv_sem
         self.copies = {}
 
     def start(self, n, stage):
         band, _, pair = self.chunks[n]
         for half in range(2):
-            order = self.cube.scatter_orders[half]
+            order = self.orders[n][half]
             index = []
             for k in range(self.cube.digits):
                 at = order.index(k)
@@ -857,7 +861,7 @@
             self.copies[n, half, stage] = copy
 
     def add(self, n, half, stage):
-        order = self.cube.scatter_orders[half]
+        order = self.orders[n][half]
         band, out, pair = self.chunks[n]
         columns = pl.ds(*pair[half])
         free = [k for k in range(self.cube.digits) if order.index(k) > stage]
@@ -870,11 +874,10 @@
             }
             full = tuple(digit.get(k, self.mine[k]) for k in range(self.cube.digits)) + everything
             short = tuple(digit[k] for k in free) + (slice(None), slice(None))
-            total = band[full].astype(jnp.float32) + extra[short].astype(jnp.float32)
             if free:
-                band[full] = total.astype(band.dtype)
+                band[full] = band[full] + extra[short]
             else:
-                out[:, columns] = total
+                out[:, columns] = band[full].astype(jnp.float32) + extra[short].astype(jnp.float32)
 
         if free:
             pl.loop(0, 1 << len(free))(one)
@@ -1074,25 +1077,32 @@
     core, seq = lax.axis_index("shard"), lax.axis_index("seq")
     block = r.owned.reshape(D, BLOCK)
     lines = [slice(128 * i, 128 * (i + 1)) for i in range(4)]
-    for share in range(2):
-        for n, (i, j) in enumerate(GRAM_SHARES[share]):
+    peers = (cube.partner(cube.levels + 1), cube.partner(cube.levels))
+    count = len(GRAM_SHARES[0])
+
+    def piece(step, n):
+        source, target, peer = (
+            (r.packed.at[1 - core, n], r.packed_in.at[0, n], peers[0]),
+            (r.summed.at[n], r.packed_in.at[1, n], peers[1]),
+            (r.whole.at[core, n], r.whole.at[core, n], peers[0]),
+        )[step]
+        return remote(source, target, r.n_send.at[step, n], r.n_recv.at[step, n], peer)
+
+    for n in range(count):
+        for share in range(2):
+            i, j = GRAM_SHARES[share][n]
             r.packed[share, n] = matmul_right_t(block[lines[i], :], block[lines[j], :])
-    peers = (cube.partner(cube.levels + 1), cube.partner(cube.levels))
-    first = remote(
-        r.packed.at[1 - core], r.packed_in.at[0], r.n_send.at[0], r.n_recv.at[0], peers[0]
-    )
-    first.start()
-    first.wait()
-    r.summed[...] = r.packed[core] + r.packed_in[0]
-    second = remote(r.summed, r.packed_in.at[1], r.n_send.at[1], r.n_recv.at[1], peers[1])
-    second.start()
-    second.wait()
-    r.whole[core] = r.summed[...] + r.packed_in[1]
-    third = remote(
-        r.whole.at[core], r.whole.at[core], r.n_send.at[2], r.n_recv.at[2], peers[0]
-    )
-    third.start()
-    third.wait()
+        piece(0, n).start()
+    for n in range(count):
+        piece(0, n).wait()
+        r.summed[n] = r.packed[core, n] + r.packed_in[0, n]
+        piece(1, n).start()
+    for n in range(count):
+        piece(1, n).wait()
+        r.whole[core, n] = r.summed[n] + r.packed_in[1, n]
+        piece(2, n).start()
+    for n in range(count):
+        piece(2, n).wait()
     for share in range(2):
         for n, (i, j) in enumerate(GRAM_SHARES[share]):
             value = r.whole[share, n]
@@ -1137,14 +1147,14 @@
     + ((2, 4), (3, 3), (7, 2), (6, 3), (3, 4), (6, 4), (4, 3), (7, 3), (4, 4), (7, 4))
 )
 SCATTER_EVENTS = (
-    ((0, 3), (4, 0), (2, 1), (5, 0), (0, 4), (1, 2), (1, 3), (3, 1), (1, 4), (4, 1), (2, 2))
-    + ((2, 3), (5, 1), (2, 4), (3, 2), (4, 2), (3, 3), (5, 2), (4, 3), (3, 4), (5, 3))
-    + ((4, 4), (5, 4))
+    ((0, 1), (3, 0), (1, 1), (4, 0), (2, 1), (5, 0), (3, 1), (6, 1), (0, 2), (1, 2), (4, 1))
+    + ((2, 2), (5, 1), (6, 2), (3, 2), (1, 3), (2, 3), (0, 3), (4, 2), (3, 3), (1, 4), (2, 4))
+    + ((0, 4), (5, 2), (6, 3), (4, 3), (3, 4), (6, 4), (5, 3), (4, 4), (5, 4))
 )
-SCATTER_STORES = ((), (4,), (), (3,), (), (2,))
+SCATTER_STORES = ((4,), (), (), (), (), (2,), (3,))
 EARLY_LOADS = tuple("w_up w_down w_qkv w_out".split()) + tuple("w_glu w_point rel vec".split())
 EARLY_LOADS += tuple("depth m_rel m_vec m_depth".split())
-SCATTER_MATRICES = ((3,), (1,), (), (4, 5, 6, 7), (2,), (0,))
+SCATTER_MATRICES = ((3,), (1,), (5,), (4,), (2,), (0,), (6, 7))
 GATHER_HELD = ((5, 2), (6, 2), (7, 2))
 GATHER_AFTER = {
     (0, 0): [(1, 0)],
@@ -1159,12 +1169,13 @@
 }
 FIRST_READY, MIDDLE_READY, SECOND_READY = (1, 4), (3, 4), (7, 4)
 SCATTER_CHUNKS = (
-    (0, tile_ranges(16, 16, 2)),
-    (0, tile_ranges(0, 16, 2)),
-    (1, tile_ranges(12, 16, 2)),
-    (1, tile_ranges(0, 12, 2)),
-    (2, tile_ranges(0, 16, 2)),
-    (2, tile_ranges(16, 17, 2)),
+    (0, tile_ranges(16, 16, 2), 1),
+    (0, tile_ranges(0, 16, 2), 2),
+    (1, tile_ranges(12, 4, 2), 0),
+    (1, tile_ranges(0, 12, 2), 0),
+    (2, tile_ranges(0, 16, 2), 0),
+    (2, tile_ranges(16, 17, 2), 0),
+    (1, tile_ranges(16, 12, 2), 1),
 )
 
 
@@ -1445,8 +1456,8 @@
     r.dob[...] = dob
     weight_grad(r.att_low[...], r.e_low, d_middle, 3 * D, D)
     weight_grad(a[2], r.dgates, d_middle, 4 * D, 2 * D)
-    scatter.advance(1, 0)
     scatter.start(2, 0)
+    scatter.start(6, 0)
 
     off_rows = []
     give, keep, got = r.give, r.keep, r.got
@@ -1482,8 +1493,8 @@
         )
         copy.start()
         kv_grads.append(copy)
-        if p == 2:
-            scatter.advance(0, 1)
+        if p == 1:
+            scatter.advance(1, 0)
     off = jnp.concatenate(off_rows, axis=0)
     off = jnp.where(early, pltpu.roll(off, 255, 1), pltpu.roll(off, 255 - tokens, 1))
     off_high, off_low = split(off)
@@ -1495,28 +1506,26 @@
             sg[SMALL_DEPTH + k : SMALL_DEPTH + k + 1, cols] = jnp.sum(
                 dconv * wide[k + 1 : k + 1 + tokens, cols], axis=0, keepdims=True
             )
-    scatter.advance(2, 0)
     for p in range(H // 2):
         kv_grads[p].wait()
         for n in range(2):
             at = D * (n + 1) + 128 * p
             r.dqkv[:, at : at + 128] = (keep[p, n] + got[p, n].astype(f32)).astype(bf16)
+    scatter.advance(2, 0)
+    scatter.advance(6, 0)
     back = matmul_right_t(r.dqkv[...], middle[:, : 3 * D])
     part, sg[SMALL_VEC + 1 : SMALL_VEC + 2, :] = norm_grad(back, xh[1], inv1, gains[1])
     d1 = r.d[...] + part
     e0 = (0.5 * d1).astype(bf16)
     weight_grad(a[1], r.dqkv, d_middle, 0, 3 * D)
     scatter.start(3, 0)
-    scatter.advance(1, 1)
     weight_grad(e0, r.s1, d_first, 0, FF)
     scatter.start(4, 0)
-    scatter.advance(0, 2)
     slopes(e0, down1, r.u1, r.du)
     back = matmul_right_t(r.du[...], up1[...])
     part, sg[SMALL_VEC : SMALL_VEC + 1, :] = norm_grad(back, xh[0], inv0, gains[0])
     r.input_grad[...] = d1 + part
     r.stores[1].start()
-    scatter.advance(3, 0)
     d_first[:, 2 * FF : 2 * FF + 128] = jnp.transpose(sg[...]).astype(bf16)
     weight_grad(a[0], r.du, d_first, FF, FF)
     scatter.start(5, 0)
@@ -1592,13 +1601,13 @@
     pairs = pltpu.VMEM((H // 2, 2, tokens, 128), bf16)
     tile = pltpu.VMEM((8, 128), f32)
     slots = pltpu.VMEM((cube.total, 8, 128), f32)
-    stages = pltpu.SemaphoreType.DMA((6, 2, cube.digits))
+    stages = pltpu.SemaphoreType.DMA((7, 2, cube.digits))
     gather_stages = pltpu.SemaphoreType.DMA((8, 2, cube.digits))
     everyone = pltpu.SemaphoreType.DMA((cube.total,))
     single = pltpu.SemaphoreType.DMA
     bands = [pltpu.VMEM(lead + (rows, w), bf16) for w in widths]
     land = []
-    for _, pair in SCATTER_CHUNKS:
+    for _, pair, _ in SCATTER_CHUNKS:
         for _, part in pair:
             for stage in range(cube.digits):
                 shape = (2,) * (cube.digits - 1 - stage) + (rows, part)
@@ -1672,8 +1681,8 @@
         m_recv=everyone,
         b_send=everyone,
         b_recv=pltpu.SemaphoreType.DMA((32,)),
-        n_send=pltpu.SemaphoreType.DMA((3,)),
-        n_recv=pltpu.SemaphoreType.DMA((3,)),
+        n_send=pltpu.SemaphoreType.DMA((3, 5)),
+        n_recv=pltpu.SemaphoreType.DMA((3, 5)),
         c3_send=everyone,
         c3_recv=everyone,
         g_send=gather_stages,

time: 214 us -> 205 us (0.958)
  Pallas kernels: 213 us -> 204 us
    pallas_call x1, Pallas kernels: 209 us -> 200 us  [fused_step(): pl.pallas_call(body, out_shape=list(outs.values()), in_specs=[pl.BlockSpe...]
where the time goes in v5:
time: 205 us
  Pallas kernels  204 us (100%)
    pallas_call x1, Pallas kernels, fused_step(): pl.pallas_call(body, out_shape=list(outs.values()), in_specs=[pl.BlockSpe...  200 us
    pallas_call x1, Pallas kernels, finish_step(): pl.pallas_call(body, out_shape=shapes, in_specs=[pl.BlockSpec(memory_spac...  4.28 us

profile of v5, /device:TPU:31, one launch (start us, length us, event | category | flops | bytes accessed | tf_op | source)
XLA Modules:
  0.0 204.9 jit_solution(3059533053952132825)
XLA Ops:
  0.7 199.7 %block_step.1 = (f32[128,512]{1,0:T(8,128)}, f32[128,512]{1,0:T(8,128)}, f32[16,4224]{1,0:T(8,128)}, f32[16,3584]{1,0:T(8,128)}, f32[16,4096]{1,0:T(8,128)}, /*i...) custom-call(f32[128,512]{1,0:T(8,128)} %bitcast.10, f32[128,512]{1,0:T(8,128)} %bitcast.11, f32[16,4096]{1,0:T(8,128)} %refs_5_.3, ...), custom_call_target="tpu_custom_call" | custom-call | tf_op jit(solution)/shard_map/block_step/pallas_call | solution.py:1731
  200.4 4.3 %finish_step.1 = (f32[16,4096]{1,0:T(8,128)}, f32[16,4096]{1,0:T(8,128)}, f32[16,1536]{1,0:T(8,128)}, f32[16,512]{1,0:T(8,128)}, f32[16,1024]{1,0:T(8,128)}, /*i...) custom-call(f32[16,4224]{1,0:T(8,128)} %get-tuple-element.65.refs_0_, ...), custom_call_target="tpu_custom_call" | custom-call | tf_op jit(solution)/shard_map/finish_step/pallas_call | solution.py:1821

commit v6 on v5

--- a/solution.py
+++ b/solution.py
@@ -769,22 +769,10 @@
     return ranges
 
 
-def gather_chunks(widths):
-    chunks = []
-    for g in range(2):
-        ranges = tile_ranges(0, widths[g] // 128, 4)
-        chunks += [(g, ranges[0:2], 0), (g, ranges[2:4], 0)]
-    tiles = widths[2] // 128
-    cut = tiles * 2 // 5
-    chunks.append((2, tile_ranges(0, cut, 2), 0))
-    ranges = tile_ranges(cut, tiles - cut, 6)
-    return chunks + [(2, ranges[2 * n : 2 * n + 2], 1) for n in range(3)]
-
-
 class Gather:
     def __init__(self, cube, mine, bands, send_sem, recv_sem):
         self.cube, self.mine, self.bands = cube, mine, bands
-        self.chunks = gather_chunks([band.shape[-1] for band in bands])
+        self.chunks = GATHER_CHUNKS
         self.send_sem, self.recv_sem = send_sem, recv_sem
         self.copies = {}
         self.events = list(GATHER_EVENTS)
@@ -810,8 +798,8 @@
             self.copies[n, half, stage] = copy
 
     def begin(self):
-        self.start(0, 0)
-        self.start(5, 0)
+        for n, stage in GATHER_BEGIN:
+            self.start(n, stage)
 
     def advance(self, n, stage):
         for half in range(2):
@@ -1062,6 +1050,15 @@
     (lh, ll), (rh, rl) = left, right
     top = product((lh[:half], ll[:half]), right)
     corner = product((lh[half:], ll[half:]), (rh[:, half:], rl[:, half:]))
+    low = jnp.concatenate([jnp.transpose(top[:, half:]), corner], axis=1)
+    return jnp.concatenate([top, low], axis=0)
+
+
+def short_product(left, right):
+    half = D // 2
+    (lh, ll), rh = left, right[0]
+    top = matmul(lh[:half], rh) + matmul(ll[:half], rh)
+    corner = matmul(lh[half:], rh[:, half:]) + matmul(ll[half:], rh[:, half:])
     low = jnp.concatenate([jnp.transpose(top[:, half:]), corner], axis=1)
     return jnp.concatenate([top, low], axis=0)
 
@@ -1119,7 +1116,7 @@
     scale = 1.0 / (jnp.sqrt(square) + 1e-07)
     gram = gram * (scale * scale)
     value = None
-    for step in range(5):
+    for step in range(4):
         parts = split(gram)
         mixed = COEF_B * gram + COEF_C * symmetric_product(parts, parts)
         mixed = jnp.where(eye, mixed + COEF_A, mixed)
@@ -1127,24 +1124,35 @@
         if step == 0:
             start_high, start_low = split(mixed * scale)
             value = matmul(start_high, block[...]) + matmul(start_low, block[...])
-        elif step < 4:
+        elif step < 3:
             value = product((high, low), split(value))
         else:
             value = matmul(high, value.astype(jnp.bfloat16))
-        if step < 4:
-            inner = symmetric_product((high, low), parts)
-            gram = symmetric_product((high, low), split(inner))
+        times = symmetric_product if step < 3 else short_product
+        gram = times((high, low), split(times((high, low), parts)))
+    short = gram.astype(jnp.bfloat16)
+    mixed = COEF_B * gram + COEF_C * matmul(short, short)
+    mixed = jnp.where(eye, mixed + COEF_A, mixed).astype(jnp.bfloat16)
+    value = matmul(mixed, value.astype(jnp.bfloat16))
     r.solved.reshape(D, BLOCK)[...] = value.astype(jnp.bfloat16)
 
 
 SMALL_REL, SMALL_VEC, SMALL_DEPTH = 0, H, H + 7
 SMALL_END = H + 7 + K
 EDGE = 16
+GATHER_CHUNKS = (
+    (0, tile_ranges(0, 17, 2), 0),
+    (0, tile_ranges(17, 16, 2), 0),
+    (1, tile_ranges(0, 20, 2), 0),
+    (2, tile_ranges(0, 16, 2), 0),
+    (1, tile_ranges(20, 8, 2), 1),
+    (2, tile_ranges(16, 16, 2), 1),
+)
+GATHER_BEGIN = ((0, 0), (4, 0),)
 GATHER_EVENTS = (
-    ((5, 0), (5, 1), (0, 0), (6, 0), (6, 1), (7, 0), (0, 1), (1, 0), (7, 1), (0, 2))
-    + ((1, 1), (2, 0), (2, 1), (3, 0), (1, 2), (0, 3), (3, 1), (4, 0), (0, 4), (4, 1))
-    + ((2, 2), (5, 2), (3, 2), (1, 3), (1, 4), (6, 2), (5, 3), (4, 2), (2, 3), (5, 4))
-    + ((2, 4), (3, 3), (7, 2), (6, 3), (3, 4), (6, 4), (4, 3), (7, 3), (4, 4), (7, 4))
+    ((4, 0), (0, 0), (4, 1), (5, 0), (5, 1), (0, 1), (1, 0), (0, 2), (1, 1), (2, 0))
+    + ((2, 1), (3, 0), (1, 2), (0, 3), (0, 4), (4, 2), (3, 1), (2, 2), (1, 3), (1, 4))
+    + ((5, 2), (3, 2), (2, 3), (4, 3), (4, 4), (2, 4), (3, 3), (3, 4), (5, 3), (5, 4))
 )
 SCATTER_EVENTS = (
     ((0, 1), (3, 0), (1, 1), (4, 0), (2, 1), (5, 0), (3, 1), (6, 1), (0, 2), (1, 2), (4, 1))
@@ -1155,19 +1163,16 @@
 EARLY_LOADS = tuple("w_up w_down w_qkv w_out".split()) + tuple("w_glu w_point rel vec".split())
 EARLY_LOADS += tuple("depth m_rel m_vec m_depth".split())
 SCATTER_MATRICES = ((3,), (1,), (5,), (4,), (2,), (0,), (6, 7))
-GATHER_HELD = ((5, 2), (6, 2), (7, 2))
+GATHER_HELD = ((4, 2), (5, 2),)
 GATHER_AFTER = {
+    (4, 0): [(5, 0)],
     (0, 0): [(1, 0)],
     (1, 0): [(2, 0)],
     (2, 0): [(3, 0)],
-    (3, 0): [(4, 0)],
-    (5, 0): [(6, 0)],
-    (6, 0): [(7, 0)],
-    (4, 1): [(5, 2)],
-    (5, 2): [(6, 2)],
-    (6, 2): [(7, 2)],
+    (2, 1): [(4, 2)],
+    (4, 2): [(5, 2)],
 }
-FIRST_READY, MIDDLE_READY, SECOND_READY = (1, 4), (3, 4), (7, 4)
+FIRST_READY, MIDDLE_READY, SECOND_READY = (1, 4), (2, 4), (5, 4)
 SCATTER_CHUNKS = (
     (0, tile_ranges(16, 16, 2), 1),
     (0, tile_ranges(0, 16, 2), 2),
@@ -1293,8 +1298,9 @@
     )
     kv_copy.start()
     q_ref[...] = matmul(a[1], middle[:, :D]).astype(bf16)
-    gather.run_to(4, 3)
+    gather.run_to(*(2, 4))
     kv_copy.wait_recv()
+    gather.run_to(*(3, 3))
     lane = lax.broadcasted_iota(jnp.int32, (1, 128), 1)
     lane_masks = [(lane // DH == e).astype(f32) for e in range(2)]
     low_masks = [m.astype(bf16) for m in lane_masks]
@@ -1312,6 +1318,8 @@
             out = matmul(prob.astype(bf16), v_pair) * lane_masks[e]
             merged = out if merged is None else merged + out
         r.att[:, columns] = merged
+        if p == 1:
+            gather.run_to(*(3, 4))
     gather.run_to(*SECOND_READY)
     att_low = r.att[...].astype(bf16)
     r.att_low[...] = att_low
@@ -1602,7 +1610,7 @@
     tile = pltpu.VMEM((8, 128), f32)
     slots = pltpu.VMEM((cube.total, 8, 128), f32)
     stages = pltpu.SemaphoreType.DMA((7, 2, cube.digits))
-    gather_stages = pltpu.SemaphoreType.DMA((8, 2, cube.digits))
+    gather_stages = pltpu.SemaphoreType.DMA((6, 2, cube.digits))
     everyone = pltpu.SemaphoreType.DMA((cube.total,))
     single = pltpu.SemaphoreType.DMA
     bands = [pltpu.VMEM(lead + (rows, w), bf16) for w in widths]
@@ -1745,10 +1753,8 @@
     f32 = jnp.float32
     for load in r.loads:
         load.start()
-    for load in r.loads:
+    for load in r.loads[:5]:
         load.wait()
-    pack_small(r.small, r.turn, r.weight[8], r.weight[6], r.weight[7])
-    pack_small(r.m_small, r.turn, r.moment[8], r.moment[6], r.moment[7])
     share_first, share_middle, share_second, returned, squares = r.results
     for j in range(8):
         width = WIDTHS[j]
@@ -1760,6 +1766,9 @@
             start = STARTS[j] - STARTS[4]
             grad = share_middle[:, start : start + width]
         n = j // 2 if j < 4 else j - 2
+        if j not in (1, 3):
+            r.loads[5 + n].wait()
+            r.loads[14 + n].wait()
         updated = MOMENTUM * r.moment[n][:, columns] + grad
         r.grad[n][:, columns] = grad
         r.next[n][:, columns] = updated
@@ -1767,6 +1776,14 @@
         r.new[n][:, columns] = r.weight[n][:, columns] - RATE_MATRIX * jnp.concatenate(
             solved, axis=1
         )
+        if j not in (0, 2):
+            for store in (r.stores[n], r.stores[9 + n], r.stores[18 + n]):
+                store.start()
+    for n in (6, 7, 8):
+        r.loads[5 + n].wait()
+        r.loads[14 + n].wait()
+    pack_small(r.small, r.turn, r.weight[8], r.weight[6], r.weight[7])
+    pack_small(r.m_small, r.turn, r.moment[8], r.moment[6], r.moment[7])
     grad = share_first[:, 2 * FF :]
     updated = MOMENTUM * r.m_small[...] + grad
     lane = lax.broadcasted_iota(jnp.int32, (1, 128), 1)
@@ -1781,8 +1798,12 @@
         outs[6][...] = turned[SMALL_VEC : SMALL_VEC + 7, 0:rows]
         outs[7][...] = value[:, SMALL_DEPTH : SMALL_DEPTH + K]
         outs[8][...] = value[0:rel_rows, SMALL_REL : SMALL_REL + H]
-    for store in r.stores:
-        store.start()
+    for n in (6, 7, 8):
+        for store in (r.stores[n], r.stores[9 + n], r.stores[18 + n]):
+            store.start()
+    for n in range(2):
+        r.loads[23 + n].wait()
+        r.stores[27 + n].start()
     for store in r.stores:
         store.wait()
 

time: 205 us -> 201 us (0.980)
  Pallas kernels: 204 us -> 200 us
    pallas_call x1, Pallas kernels: 200 us -> 196 us  [fused_step(): pl.pallas_call(body, out_shape=list(outs.values()), in_specs=[pl.BlockSpe...]
where the time goes in v6:
time: 201 us
  Pallas kernels  200 us (100%)
    pallas_call x1, Pallas kernels, fused_step(): pl.pallas_call(body, out_shape=list(outs.values()), in_specs=[pl.BlockSpe...  196 us

profile of v6, /device:TPU:31, one launch (start us, length us, event | category | flops | bytes accessed | tf_op | source)
XLA Modules:
  0.0 201.1 jit_solution(1702558344766875566)
XLA Ops:
  0.7 196.5 %block_step.1 = (f32[128,512]{1,0:T(8,128)}, f32[128,512]{1,0:T(8,128)}, f32[16,4224]{1,0:T(8,128)}, f32[16,3584]{1,0:T(8,128)}, f32[16,4096]{1,0:T(8,128)}, /*i...) custom-call(f32[128,512]{1,0:T(8,128)} %bitcast.10, f32[128,512]{1,0:T(8,128)} %bitcast.11, f32[16,4096]{1,0:T(8,128)} %refs_5_.3, ...), custom_call_target="tpu_custom_call" | custom-call | tf_op jit(solution)/shard_map/block_step/pallas_call | solution.py:1739
  197.1 3.8 %finish_step.1 = (f32[16,4096]{1,0:T(8,128)}, f32[16,4096]{1,0:T(8,128)}, f32[16,1536]{1,0:T(8,128)}, f32[16,512]{1,0:T(8,128)}, f32[16,1024]{1,0:T(8,128)}, /*i...) custom-call(f32[16,4224]{1,0:T(8,128)} %get-tuple-element.65.refs_0_, ...), custom_call_target="tpu_custom_call" | custom-call | tf_op jit(solution)/shard_map/finish_step/pallas_call | solution.py:1842

commit v7 on v6

--- a/solution.py
+++ b/solution.py
@@ -48,6 +48,11 @@
         self.scatter_orders = tuple(order[::-1] for order in self.gather_orders)
         self.scatter_high_orders = tuple(order[::-1] for order in self.gather_late_orders)
         self.scatter_low_orders = ([core, low, seq] + high[::-1],) * 2
+        self.scatter_kinds = (
+            self.scatter_orders,
+            self.scatter_high_orders,
+            self.scatter_low_orders,
+        )
 
     def mine(self):
         d = lax.axis_index("dp")
@@ -769,6 +774,13 @@
     return ranges
 
 
+def joined(orders, pair, stage):
+    one, two = orders
+    if one[stage] == two[stage] and set(one[:stage]) == set(two[:stage]):
+        return [(pair[0][0], pair[0][1] + pair[1][1])]
+    return list(pair)
+
+
 class Gather:
     def __init__(self, cube, mine, bands, send_sem, recv_sem):
         self.cube, self.mine, self.bands = cube, mine, bands
@@ -780,13 +792,14 @@
 
     def start(self, n, stage):
         g, pair, kind = self.chunks[n]
-        for half in range(2):
-            order = (self.cube.gather_orders, self.cube.gather_late_orders)[kind][half]
+        orders = (self.cube.gather_orders, self.cube.gather_late_orders)[kind]
+        for half, columns in enumerate(joined(orders, pair, stage)):
+            order = orders[half]
             done = order[:stage]
             index = tuple(
                 slice(None) if k in done else self.mine[k] for k in range(self.cube.digits)
             )
-            place = self.bands[g].at[index + (slice(None), pl.ds(*pair[half]))]
+            place = self.bands[g].at[index + (slice(None), pl.ds(*columns))]
             copy = remote(
                 place,
                 place,
@@ -803,7 +816,8 @@
 
     def advance(self, n, stage):
         for half in range(2):
-            self.copies[n, half, stage].wait_recv()
+            if (n, half, stage) in self.copies:
+                self.copies[n, half, stage].wait_recv()
         if stage < self.last and (n, stage + 1) not in GATHER_HELD:
             self.start(n, stage + 1)
         for other in GATHER_AFTER.get((n, stage), ()):
@@ -821,15 +835,14 @@
 class Scatter:
     def __init__(self, cube, mine, bands, landed, outs, send_sem, recv_sem):
         self.cube, self.mine, self.landed = cube, mine, landed
-        kinds = (cube.scatter_orders, cube.scatter_high_orders, cube.scatter_low_orders)
         self.chunks = [(bands[g], outs[g], pair) for g, pair, _ in SCATTER_CHUNKS]
-        self.orders = [kinds[kind] for _, _, kind in SCATTER_CHUNKS]
+        self.orders = [cube.scatter_kinds[kind] for _, _, kind in SCATTER_CHUNKS]
         self.send_sem, self.recv_sem = send_sem, recv_sem
         self.copies = {}
 
     def start(self, n, stage):
         band, _, pair = self.chunks[n]
-        for half in range(2):
+        for half, columns in enumerate(joined(self.orders[n], pair, stage)):
             order = self.orders[n][half]
             index = []
             for k in range(self.cube.digits):
@@ -839,7 +852,7 @@
                 else:
                     index.append(1 - self.mine[k] if at == stage else self.mine[k])
             copy = remote(
-                band.at[tuple(index) + (slice(None), pl.ds(*pair[half]))],
+                band.at[tuple(index) + (slice(None), pl.ds(*columns))],
                 self.landed[(n * 2 + half) * self.cube.digits + stage],
                 self.send_sem.at[n, half, stage],
                 self.recv_sem.at[n, half, stage],
@@ -851,7 +864,7 @@
     def add(self, n, half, stage):
         order = self.orders[n][half]
         band, out, pair = self.chunks[n]
-        columns = pl.ds(*pair[half])
+        columns = pl.ds(*joined(self.orders[n], pair, stage)[half])
         free = [k for k in range(self.cube.digits) if order.index(k) > stage]
         extra = self.landed[(n * 2 + half) * self.cube.digits + stage]
         everything = (slice(None), columns)
@@ -874,8 +887,9 @@
 
     def advance(self, n, stage):
         for half in range(2):
-            self.copies[n, half, stage].wait_recv()
-            self.add(n, half, stage)
+            if (n, half, stage) in self.copies:
+                self.copies[n, half, stage].wait_recv()
+                self.add(n, half, stage)
         if stage + 1 < self.cube.digits:
             self.start(n, stage + 1)
 
@@ -1340,9 +1354,8 @@
     )
     halo_copy.start()
     zero_edge = jnp.zeros((EDGE, D), f32)
-    halo_copy.wait()
-    wide[0:EDGE, :] = jnp.where(early, zero_edge, r.halo[...])
-    wide[EDGE + tokens :, :] = jnp.where(early, r.halo[...], zero_edge)
+    wide[0:EDGE, :] = zero_edge
+    wide[EDGE + tokens :, :] = zero_edge
     conv_ref = r.conv
     for b in range(D // 128):
         cols = slice(128 * b, 128 * (b + 1))
@@ -1350,6 +1363,23 @@
         for k in range(K):
             total = total + wide[k + 1 : k + 1 + tokens, cols] * taps[k][:, cols]
         conv_ref[:, cols] = total
+    halo_copy.wait()
+    rim = r.rim
+    rim[...] = jnp.zeros_like(rim)
+    rim[0:EDGE, :] = jnp.where(early, zero_edge, r.halo[...])
+    rim[3 * EDGE :, :] = jnp.where(early, r.halo[...], zero_edge)
+    wide[0:EDGE, :] = rim[0:EDGE, :]
+    wide[EDGE + tokens :, :] = rim[3 * EDGE :, :]
+    for b in range(D // 128):
+        cols = slice(128 * b, 128 * (b + 1))
+        before = jnp.zeros((EDGE, 128), f32)
+        after = jnp.zeros((EDGE, 128), f32)
+        for k in range(K // 2):
+            before = before + rim[k + 1 : k + 1 + EDGE, cols] * taps[k][:, cols]
+        for k in range(K // 2 + 1, K):
+            after = after + rim[k + 17 : k + 17 + EDGE, cols] * taps[k][:, cols]
+        conv_ref[0:EDGE, cols] = conv_ref[0:EDGE, cols] + before
+        conv_ref[tokens - EDGE :, cols] = conv_ref[tokens - EDGE :, cols] + after
     conv = conv_ref[...]
     part_sum = jnp.sum(conv, axis=0, keepdims=True)
     part_off = conv - part_sum * (1.0 / tokens)
@@ -1615,10 +1645,13 @@
     single = pltpu.SemaphoreType.DMA
     bands = [pltpu.VMEM(lead + (rows, w), bf16) for w in widths]
     land = []
-    for _, pair, _ in SCATTER_CHUNKS:
-        for _, part in pair:
+    for _, pair, kind in SCATTER_CHUNKS:
+        for half in range(2):
             for stage in range(cube.digits):
-                shape = (2,) * (cube.digits - 1 - stage) + (rows, part)
+                columns = joined(cube.scatter_kinds[kind], pair, stage)
+                part = columns[half][1] if half < len(columns) else 0
+                lead_shape = (2,) * (cube.digits - 1 - stage) + (rows, part)
+                shape = lead_shape if part else (rows, 128)
                 land.append(pltpu.VMEM(shape, bf16))
     scratch = dict(
         first=bands[0],
@@ -1657,6 +1690,7 @@
         wide=wide_field,
         dwide=wide_field,
         halo=pltpu.VMEM((EDGE, D), f32),
+        rim=pltpu.VMEM((4 * EDGE, D), f32),
         edges=pltpu.VMEM((2 * EDGE, D), f32),
         edges_in=pltpu.VMEM((2 * EDGE, D), f32),
         dgates=pltpu.VMEM((tokens, 2 * D), bf16),

time: 201 us -> 199 us (0.990)
    pallas_call x1, Pallas kernels: 196 us -> 194 us  [fused_step(): pl.pallas_call(body, out_shape=list(outs.values()), in_specs=[pl.BlockSpe...]
where the time goes in v7:
time: 199 us
  Pallas kernels  198 us (99%)
    pallas_call x1, Pallas kernels, fused_step(): pl.pallas_call(body, out_shape=list(outs.values()), in_specs=[pl.BlockSpe...  194 us

profile of v7, /device:TPU:31, one launch (start us, length us, event | category | flops | bytes accessed | tf_op | source)
XLA Modules:
  0.0 198.7 jit_solution(15149290290139180312)
XLA Ops:
  0.7 194.0 %block_step.1 = (f32[128,512]{1,0:T(8,128)}, f32[128,512]{1,0:T(8,128)}, f32[16,4224]{1,0:T(8,128)}, f32[16,3584]{1,0:T(8,128)}, f32[16,4096]{1,0:T(8,128)}, /*i...) custom-call(f32[128,512]{1,0:T(8,128)} %bitcast.10, f32[128,512]{1,0:T(8,128)} %bitcast.11, f32[16,4096]{1,0:T(8,128)} %refs_5_.3, ...), custom_call_target="tpu_custom_call" | custom-call | tf_op jit(solution)/shard_map/block_step/pallas_call | solution.py:1773
  194.7 3.8 %finish_step.1 = (f32[16,4096]{1,0:T(8,128)}, f32[16,4096]{1,0:T(8,128)}, f32[16,1536]{1,0:T(8,128)}, f32[16,512]{1,0:T(8,128)}, f32[16,1024]{1,0:T(8,128)}, /*i...) custom-call(f32[16,4224]{1,0:T(8,128)} %get-tuple-element.65.refs_0_, ...), custom_call_target="tpu_custom_call" | custom-call | tf_op jit(solution)/shard_map/finish_step/pallas_call | solution.py:1876

commit v8 on v7

--- a/solution.py
+++ b/solution.py
@@ -1083,7 +1083,7 @@
 )
 
 
-def orthogonalize(cube, r):
+def orthogonalize(cube, r, squares):
     f32 = jnp.float32
     core, seq = lax.axis_index("shard"), lax.axis_index("seq")
     block = r.owned.reshape(D, BLOCK)
@@ -1104,6 +1104,7 @@
             i, j = GRAM_SHARES[share][n]
             r.packed[share, n] = matmul_right_t(block[lines[i], :], block[lines[j], :])
         piece(0, n).start()
+    squares.start()
     for n in range(count):
         piece(0, n).wait()
         r.summed[n] = r.packed[core, n] + r.packed_in[0, n]
@@ -1302,18 +1303,16 @@
     gather.run_to(*MIDDLE_READY)
 
     q_ref, kv = r.q, r.kv
-    kv[pl.ds(first_row, tokens), :] = matmul(a[1], middle[:, D : 3 * D]).astype(bf16)
-    kv_copy = remote(
-        kv.at[pl.ds(first_row, tokens)],
-        kv.at[pl.ds(first_row, tokens)],
-        r.kv_send,
-        r.kv_recv,
-        across,
-    )
-    kv_copy.start()
+    kv_copies = []
+    for n in range(2):
+        place = kv.at[pl.ds(first_row, tokens), pl.ds(D * n, D)]
+        place[...] = matmul(a[1], middle[:, D * (n + 1) : D * (n + 2)]).astype(bf16)
+        copy = remote(place, place, r.kv_send.at[n], r.kv_recv.at[n], across)
+        copy.start()
+        kv_copies.append(copy)
     q_ref[...] = matmul(a[1], middle[:, :D]).astype(bf16)
     gather.run_to(*(2, 4))
-    kv_copy.wait_recv()
+    kv_copies[0].wait_recv()
     gather.run_to(*(3, 3))
     lane = lax.broadcasted_iota(jnp.int32, (1, 128), 1)
     lane_masks = [(lane // DH == e).astype(f32) for e in range(2)]
@@ -1321,7 +1320,7 @@
     scale = DH ** (-0.5)
     for p in range(H // 2):
         columns = slice(128 * p, 128 * (p + 1))
-        k_pair, v_pair = kv[:, columns], kv[:, D + 128 * p : D + 128 * (p + 1)]
+        k_pair = kv[:, columns]
         merged = None
         for e in range(2):
             q_head = q_ref[:, columns] * low_masks[e]
@@ -1329,6 +1328,9 @@
             shifted = jnp.exp(scores - jnp.max(scores, axis=1, keepdims=True))
             prob = shifted / jnp.sum(shifted, axis=1, keepdims=True)
             r.prob[2 * p + e] = prob
+            if p + e == 0:
+                kv_copies[1].wait_recv()
+            v_pair = kv[:, D + 128 * p : D + 128 * (p + 1)]
             out = matmul(prob.astype(bf16), v_pair) * lane_masks[e]
             merged = out if merged is None else merged + out
         r.att[:, columns] = merged
@@ -1578,9 +1580,8 @@
     r.tile3[...] = jnp.zeros_like(r.tile3)
     r.tile3[0:1, :] = jnp.sum(next_small * next_small, axis=0, keepdims=True)
     squares = Collect(cube, r.tile3, r.slots3, r.c3_send, r.c3_recv)
-    squares.start()
     momenta.receive()
-    orthogonalize(cube, r)
+    orthogonalize(cube, r, squares)
     momenta.send_back()
     squares.arrive()
     r.squares[...] = squares.total()
@@ -1591,7 +1592,8 @@
     scatter.finish()
     for store in r.stores:
         store.wait()
-    kv_copy.wait_send()
+    for copy in kv_copies:
+        copy.wait_send()
 
 
 def fused_step(cube, inputs, cotangent, weights, momenta, bucket, collective_id):
@@ -1735,8 +1737,8 @@
         c1_recv=everyone,
         c2_send=everyone,
         c2_recv=everyone,
-        kv_send=single,
-        kv_recv=single,
+        kv_send=pltpu.SemaphoreType.DMA((2,)),
+        kv_recv=pltpu.SemaphoreType.DMA((2,)),
         halo_send=single,
         halo_recv=single,
         edge_send=single,

time: 199 us -> 197 us (0.990)
  Pallas kernels: 198 us -> 196 us
where the time goes in v8:
time: 197 us
  Pallas kernels  196 us (99%)
    pallas_call x1, Pallas kernels, fused_step(): pl.pallas_call(body, out_shape=list(outs.values()), in_specs=[pl.BlockSpe...  192 us

profile of v8, /device:TPU:31, one launch (start us, length us, event | category | flops | bytes accessed | tf_op | source)
XLA Modules:
  0.0 196.9 jit_solution(44034081509313650)
XLA Ops:
  0.7 192.3 %block_step.1 = (f32[128,512]{1,0:T(8,128)}, f32[128,512]{1,0:T(8,128)}, f32[16,4224]{1,0:T(8,128)}, f32[16,3584]{1,0:T(8,128)}, f32[16,4096]{1,0:T(8,128)}, /*i...) custom-call(f32[128,512]{1,0:T(8,128)} %bitcast.10, f32[128,512]{1,0:T(8,128)} %bitcast.11, f32[16,4096]{1,0:T(8,128)} %refs_5_.3, ...), custom_call_target="tpu_custom_call" | custom-call | tf_op jit(solution)/shard_map/block_step/pallas_call | solution.py:1775
  193.0 3.8 %finish_step.1 = (f32[16,4096]{1,0:T(8,128)}, f32[16,4096]{1,0:T(8,128)}, f32[16,1536]{1,0:T(8,128)}, f32[16,512]{1,0:T(8,128)}, f32[16,1024]{1,0:T(8,128)}, /*i...) custom-call(f32[16,4224]{1,0:T(8,128)} %get-tuple-element.65.refs_0_, ...), custom_call_target="tpu_custom_call" | custom-call | tf_op jit(solution)/shard_map/finish_step/pallas_call | solution.py:1878
